TPU v7x, 32 devices: a whole 2x2x4 slice. The times are simulated.
32 devices in a mesh: group: 2 (over x), expert: 16 (over z, y, core).
Axes of the slice: x: 2, y: 2, z: 4, core: 2. Of those that a mesh axis runs over, the one named last changes fastest.
Arguments:
- layer_input: bfloat16 [4096, 2048], P(('group', 'expert')), parts along dimension 0, may hold values from -6 to 6
- out_grad: bfloat16 [4096, 2048], P(('group', 'expert')), parts along dimension 0, may hold values from -6 to 6
- expert_ids: int32 [4096, 8], P(('group', 'expert')), parts along dimension 0, may hold values from 0 to 15, all different within a row; in each aligned block of 128 rows (0 to 127, 128 to 255, ...) at most 80 rows name the same one
- gates: float32 [4096, 8], P(('group', 'expert')), parts along dimension 0, may hold values from 0.05 to 1
- w_gate: bfloat16 [16, 2048, 512], P('expert'), may hold values from -0.125 to 0.125
- w_up: bfloat16 [16, 2048, 512], P('expert'), may hold values from -0.125 to 0.125
- w_down: bfloat16 [16, 512, 2048], P('expert'), may hold values from -0.25 to 0.25
Outputs:
- input_grad: float32 [4096, 2048], P(('group', 'expert')), parts along dimension 0
There are 2 independent parts, one for each index of `group`. A program takes and returns all parts, laid end to end along the dimension named above; an argument that names none is the same for every part. Nothing has to cross between parts.
Inputs may be any that keep to these rules, and one draw needn't show every extreme that they name: `expert_ids`: within the rows of one device (aligned blocks of 128 tokens) no expert is named more than 80 times, a bound that some block reaches; a row names 8 different experts.
All inputs are finite; a program needn't handle non-finite values.
Results may differ from a plain program's by a relative error of at most 0.0041.
Values may be sent and summed in bfloat16 or wider, within the bound.
No kernel may reach another device: no remote copies, remote signals or barrier semaphores. Data moves between devices by JAX's collectives and lax.ppermute only.
A program may use at most 128 MiB of HBM per device.

v0:
```python
import jax
import jax.numpy as jnp
from jax import lax
from jax.sharding import PartitionSpec as P


def expert_rows(rows_in, rows_grad, gate_w, up_w, down_w):
    pre_gate = jnp.dot(rows_in, gate_w, preferred_element_type=jnp.float32)
    pre_up = jnp.dot(rows_in, up_w, preferred_element_type=jnp.float32)
    back = lax.dot_general(
        rows_grad, down_w, (((1,), (1,)), ((), ())), preferred_element_type=jnp.float32
    )
    sig = jax.nn.sigmoid(pre_gate)
    d_gate = (back * pre_up * sig * (1.0 + pre_gate * (1.0 - sig))).astype(jnp.bfloat16)
    d_up = (back * pre_gate * sig).astype(jnp.bfloat16)
    term = lax.dot_general(
        d_gate, gate_w, (((1,), (1,)), ((), ())), preferred_element_type=jnp.float32
    )
    term = term + lax.dot_general(
        d_up, up_w, (((1,), (1,)), ((), ())), preferred_element_type=jnp.float32
    )
    return term


def on_device(layer_input, out_grad, expert_ids, gates, w_gate, w_up, w_down):
    owners = lax.axis_size("expert")
    tok_rows = layer_input.shape[0]
    width = layer_input.shape[1]
    choose = expert_ids.shape[1]
    capacity = 5 * tok_rows * choose // (4 * owners)
    flat_ids = expert_ids.reshape(-1)
    flat_gates = gates.reshape(-1)
    assigned = flat_ids.shape[0]
    onehot = (flat_ids[:, None] == jnp.arange(owners, dtype=jnp.int32)[None, :]).astype(jnp.int32)
    before = jnp.cumsum(onehot, axis=0) - onehot
    position = jnp.sum(before * onehot, axis=1)
    slot = flat_ids * capacity + position
    source = (
        jnp.full((owners * capacity,), -1, jnp.int32)
        .at[slot]
        .set(jnp.arange(assigned, dtype=jnp.int32))
    )
    valid = source >= 0
    safe = jnp.maximum(source, 0)
    token = safe // choose
    send_in = jnp.where(valid[:, None], layer_input[token], jnp.zeros((), jnp.bfloat16))
    gate_val = jnp.where(valid, flat_gates[safe], jnp.float32(0.0))
    send_grad = (gate_val[:, None] * out_grad[token].astype(jnp.float32)).astype(jnp.bfloat16)
    send_in = send_in.reshape(owners, capacity, width)
    send_grad = send_grad.reshape(owners, capacity, width)
    gate_w = w_gate[0]
    up_w = w_up[0]
    down_w = w_down[0]
    rows_in = lax.all_to_all(send_in, "expert", split_axis=0, concat_axis=0, tiled=True)
    rows_grad = lax.all_to_all(send_grad, "expert", split_axis=0, concat_axis=0, tiled=True)
    count = rows_in.shape[1]
    term = expert_rows(
        rows_in.reshape(-1, width), rows_grad.reshape(-1, width), gate_w, up_w, down_w
    )
    back = lax.all_to_all(
        term.reshape(owners, count, width), "expert", split_axis=0, concat_axis=0, tiled=True
    )
    back_rows = back.reshape(owners * capacity, width)
    picked = back_rows[slot].reshape(tok_rows, choose, width)
    return jnp.sum(picked, axis=1)


def solution(mesh):
    placed = (
        P(("group", "expert"), None),
        P(("group", "expert"), None),
        P(("group", "expert"), None),
        P(("group", "expert"), None),
        P("expert", None, None),
        P("expert", None, None),
        P("expert", None, None),
    )
    return jax.shard_map(
        on_device,
        mesh=mesh,
        in_specs=placed,
        out_specs=P(("group", "expert"), None),
        check_vma=False,
    )
```

profile of v0, /device:TPU:13, one launch (start us, length us, event | category | flops | bytes accessed | tf_op | source)
XLA Modules:
  0.0 551.1 jit_solution(12372693153753491376)
XLA Ops:
  0.0 0.8 broadcast_multiply_fusion
  0.8 0.8 copy.11
  1.8 0.1 copy.10
  2.0 4.5 reduce-window.6
  6.6 0.1 copy.13
  7.0 4.3 scatter_custom_fusion
  11.4 0.8 copy.15
  12.3 5.0 gather_fusion
  17.4 6.1 %gather_fusion.2 = bf16[1280,2048]{1,0:T(8,128)(2,1)} fusion(bf16[128,2048]{1,0:T(8,128)(2,1)S(1)} %copy-done.1, s32[2048]{0:T(1024)S(1)} %get-tuple-element.9), kind=kCustom, calls=%fused_computation.2 | custom fusion | bytes 10490880 | tf_op jit(solution)/shard_map/gather | solution.py:46
  23.5 5.3 broadcast_select_fusion
  28.7 6.7 %all-to-all-start.1 = ((bf16[16,80,2048]{2,1,0:T(8,128)(2,1)}), bf16[16,80,2048]{2,1,0:T(8,128)(2,1)}, u32[]{:S(2)}, u32[]{:S(2)}) async-start(bf16[16,80,2048]{2,1,0:T(8,128)(2,1)} %broadcast_select_fusion), calls=%async_computation.1 | async-start | bytes 10485760 | tf_op jit(solution)/shard_map/all_to_all | solution.py:54
  35.5 6.2 %gather_fusion.1 = bf16[1280,2048]{1,0:T(8,128)(2,1)} fusion(bf16[128,2048]{1,0:T(8,128)(2,1)S(1)} %copy-done.2, s32[2048]{0:T(1024)S(1)} %get-tuple-element.9), kind=kCustom, calls=%fused_computation.1 | custom fusion | bytes 10490880 | tf_op jit(solution)/shard_map/gather | solution.py:48
  41.7 5.8 %fusion = bf16[16,80,2048]{2,1,0:T(8,128)(2,1)} fusion(bf16[16,80,2048]{2,1,0:T(8,128)(2,1)} %bitcast.49, f32[16,80]{1,0:T(8,128)S(1)} %mul.52), kind=kLoop, calls=%fused_computation.6 | loop fusion | flops 7864320 | bytes 10490880 | tf_op jit(solution)/shard_map/convert_element_type | solution.py:48
  47.5 102.9 %all-to-all-done.1 = bf16[16,80,2048]{2,1,0:T(8,128)(2,1)} async-done(((bf16[16,80,2048]{2,1,0:T(8,128)(2,1)}), bf16[16,80,2048]{2,1,0:T(8,128)(2,1)}, u32[]{:S(2)}, u32[]{:S(2)}) %all-to-all-start.1) | async-done | bytes 5242912 | tf_op jit(solution)/shard_map/all_to_all | solution.py:54
  150.4 4.9 all-to-all-start
  155.3 7.6 %fusion.6 = f32[1280,512]{1,0:T(8,128)} fusion(bf16[1280,2048]{1,0:T(8,128)(2,1)} %bitcast.8, bf16[1,2048,512]{2,1,0:T(8,128)(2,1)} %param.11), kind=kOutput, calls=%fused_computation.18 | convolution fusion | flops 2684354560 | bytes 9961472 | tf_op jit(solution)/shard_map/dot_general | solution.py:8
  162.8 107.4 %all-to-all-done = bf16[16,80,2048]{2,1,0:T(8,128)(2,1)} async-done(((bf16[16,80,2048]{2,1,0:T(8,128)(2,1)}), bf16[16,80,2048]{2,1,0:T(8,128)(2,1)}, u32[]{:S(2)}, u32[]{:S(2)}) %all-to-all-start) | async-done | bytes 5242912 | tf_op jit(solution)/shard_map/all_to_all | solution.py:55
  270.2 7.6 %fusion.10 = f32[1280,512]{1,0:T(8,128)} fusion(bf16[1280,2048]{1,0:T(8,128)(2,1)} %bitcast.5, bf16[1,512,2048]{2,1,0:T(8,128)(2,1)} %param.13), kind=kOutput, calls=%fused_computation.22 | convolution fusion | flops 2684354560 | bytes 9961472 | tf_op jit(solution)/shard_map/dot_general | solution.py:10
  277.8 12.1 %fusion.4 = f32[1280,2048]{1,0:T(8,128)} fusion(bf16[1,2048,512]{2,1,0:T(8,128)(2,1)} %param.11, f32[1280,512]{1,0:T(8,128)} %fusion.10, bf16[1280,2048]{1,0:T(8,128)(2,1)} %bitcast.8, f32[1280,512]{1,0:T(8,128)} %fusion.6, bf16[1,2048,512]{2,1,0:T(8,128)(2,1)S(1)} %copy-done), kind=kOutput, calls=%fused_computation.16 | convolution fusion | flops 5375262720 | bytes 25165824 | tf_op jit(solution)/shard_map/dot_general | solution.py:16
  289.9 9.6 %convolution_add_fusion = f32[1280,2048]{1,0:T(8,128)} fusion(f32[1280,2048]{1,0:T(8,128)} %fusion.4, bf16[1,2048,512]{2,1,0:T(8,128)(2,1)S(1)} %copy-done, f32[1280,512]{1,0:T(8,128)} %fusion.10, f32[1280,512]{1,0:T(8,128)} %fusion.6), kind=kOutput, calls=%fused_computation.7 | convolution fusion | flops 2690908160 | bytes 28311552 | tf_op jit(solution)/shard_map/dot_general | solution.py:19
  299.5 4.9 all-to-all-start.2
  304.5 227.3 %all-to-all-done.2 = f32[16,80,2048]{2,1,0:T(8,128)} async-done(((f32[16,80,2048]{2,1,0:T(8,128)}), f32[16,80,2048]{2,1,0:T(8,128)}, u32[]{:S(2)}, u32[]{:S(2)}) %all-to-all-start.2) | async-done | bytes 10485792 | tf_op jit(solution)/shard_map/all_to_all | solution.py:60
  531.7 13.0 %gather_fusion.3 = f32[1024,2048]{1,0:T(8,128)} fusion(f32[1280,2048]{1,0:T(8,128)} %bitcast.12, s32[1024]{0:T(1024)S(1)} %broadcast_clamp_fusion), kind=kCustom, calls=%fused_computation.3 | custom fusion | bytes 16781312 | tf_op jit(solution)/shard_map/gather | solution.py:64
  544.8 6.3 %bitcast_reduce_fusion = f32[128,2048]{1,0:T(8,128)} fusion(f32[1024,2048]{1,0:T(8,128)} %gather_fusion.3), kind=kLoop, calls=%fused_computation.8 | loop fusion | flops 1835008 | bytes 9437184 | tf_op jit(solution)/shard_map/reduce_sum | solution.py:65
  (25 shorter events, 0.9 us)
Async XLA Ops:
  0.0 277.8 %copy-start = (bf16[1,2048,512]{2,1,0:T(8,128)(2,1)S(1)}, bf16[1,2048,512]{2,1,0:T(8,128)(2,1)}, u32[]{:S(2)}) copy-start(bf16[1,2048,512]{2,1,0:T(8,128)(2,1)} %param.12) | copy-start | bytes 6291460
  12.3 5.1 copy-start.1
  28.7 6.8 %copy-start.2 = (bf16[128,2048]{1,0:T(8,128)(2,1)S(1)}, bf16[128,2048]{1,0:T(8,128)(2,1)}, u32[]{:S(2)}) copy-start(bf16[128,2048]{1,0:T(8,128)(2,1)} %param.8) | copy-start | bytes 1572868
  28.7 121.6 %all-to-all-start.1 = ((bf16[16,80,2048]{2,1,0:T(8,128)(2,1)}), bf16[16,80,2048]{2,1,0:T(8,128)(2,1)}, u32[]{:S(2)}, u32[]{:S(2)}) async-start(bf16[16,80,2048]{2,1,0:T(8,128)(2,1)} %broadcast_select_fusion), calls=%async_computation.1 | async-start | bytes 10485760 | tf_op jit(solution)/shard_map/all_to_all | solution.py:54
  150.4 119.8 %all-to-all-start = ((bf16[16,80,2048]{2,1,0:T(8,128)(2,1)}), bf16[16,80,2048]{2,1,0:T(8,128)(2,1)}, u32[]{:S(2)}, u32[]{:S(2)}) async-start(bf16[16,80,2048]{2,1,0:T(8,128)(2,1)} %fusion), calls=%async_computation | async-start | bytes 10485760 | tf_op jit(solution)/shard_map/all_to_all | solution.py:55
  299.5 232.2 %all-to-all-start.2 = ((f32[16,80,2048]{2,1,0:T(8,128)}), f32[16,80,2048]{2,1,0:T(8,128)}, u32[]{:S(2)}, u32[]{:S(2)}) async-start(f32[16,80,2048]{2,1,0:T(8,128)} %bitcast.48), calls=%async_computation.2 | async-start | bytes 20971520 | tf_op jit(solution)/shard_map/all_to_all | solution.py:60
where the time goes:
time: 552 us; the launch traced here: 551 us
  waiting for transfers between devices  438 us (79%)
  local copies, waits for them, and re-layouts  37.1 us (7%)
  matrix products  36.9 us (7%)
  other arithmetic  22.9 us (4%)
  starting transfers between devices  16.5 us (3%)
    all_to_all x1, waiting for transfers between devices, on_device(): lax.all_to_all(term.reshape(owners, count, width), 'expert', split_axis=0...  227 us
    all_to_all x1, waiting for transfers between devices, on_device(): lax.all_to_all(send_grad, 'expert', split_axis=0, concat_axis=0, tiled=True)  107 us
    all_to_all x1, waiting for transfers between devices, on_device(): lax.all_to_all(send_in, 'expert', split_axis=0, concat_axis=0, tiled=True)  103 us
    gather x1, local copies, waits for them, and re-layouts, on_device(): picked = back_rows[slot].reshape(tok_rows, choose, width)  13 us
    dot_general x1, matrix products, expert_rows(): lax.dot_general(d_gate, gate_w, (((1,), (1,)), ((), ())), preferred_eleme...  12.1 us
  transfers between devices with their start and end apart: 3, of which 3 were waited for; matrix products, arithmetic and copies ran while one was open for 4% of the time, Pallas kernels for 0%

commit v1 on v0

v1 whole, which is shorter than its diff:
```python
from functools import partial

import jax
import jax.numpy as jnp
from jax import lax
from jax.experimental import pallas as pl
from jax.experimental.pallas import tpu as pltpu
from jax.sharding import PartitionSpec as P

F32 = jnp.float32
BF16 = jnp.bfloat16
LAST = (((1,), (1,)), ((), ()))


def pair_kernel(blocks, first, wide, order, *refs):
    xs, gs = refs[:blocks], refs[blocks : 2 * blocks]
    gates = refs[2 * blocks]
    weights = refs[2 * blocks + 1 : 2 * blocks + 7]
    outs = refs[2 * blocks + 7 : 3 * blocks + 7]
    x_buf, g_buf, w_in, w_out, d_buf, sems = refs[3 * blocks + 7 :]
    rows = xs[0].shape[0]
    width, hidden = weights[0].shape
    copies = {}

    def start(key, source, target):
        copies[key] = pltpu.make_async_copy(source, target, sems.at[len(copies)])
        copies[key].start()

    for i in range(blocks):
        start(("x", i), xs[i], x_buf.at[pl.ds(i * rows, rows)])
    start(("w", 0), weights[0], w_in.at[:, pl.ds(0, hidden)])
    start(("w", 1), weights[1], w_in.at[:, pl.ds(hidden, hidden)])
    for i in range(blocks):
        start(("g", i), gs[i], g_buf.at[pl.ds(i * rows, rows)])
    start(("w", 2), weights[2], w_out.at[pl.ds(0, hidden)])
    start(("w", 3), weights[3], w_in.at[:, pl.ds(2 * hidden, hidden)])
    start(("w", 4), weights[4], w_in.at[:, pl.ds(3 * hidden, hidden)])
    start(("w", 5), weights[5], w_out.at[pl.ds(hidden, hidden)])
    for i in range(blocks):
        copies["x", i].wait()
    for k in range(2):
        at = 2 * k * hidden
        copies["w", 3 * k].wait()
        pre_gate = jnp.dot(x_buf[...], w_in[:, at : at + hidden], preferred_element_type=F32)
        copies["w", 3 * k + 1].wait()
        pre_up = jnp.dot(x_buf[...], w_in[:, at + hidden : at + 2 * hidden], preferred_element_type=F32)
        if k == 0:
            for i in range(blocks):
                copies["g", i].wait()
        copies["w", 3 * k + 2].wait()
        back = lax.dot_general(
            g_buf[...], w_out[k * hidden : (k + 1) * hidden, :], LAST, preferred_element_type=F32
        )
        gate = [
            gates[pl.ds(pl.multiple_of(order[first + i] * rows, rows), rows), k : k + 1] for i in range(blocks)
        ]
        back = back * jnp.concatenate(gate, axis=0)
        sig = jax.nn.sigmoid(pre_gate)
        back_sig = back * sig
        d_buf[:, at : at + hidden] = (back_sig * pre_up * (1.0 + pre_gate * (1.0 - sig))).astype(BF16)
        d_buf[:, at + hidden : at + 2 * hidden] = (back_sig * pre_gate).astype(BF16)
    for c in range(0, width, wide):
        term = lax.dot_general(d_buf[...], w_in[c : c + wide, :], LAST, preferred_element_type=F32)
        for i, out in enumerate(outs):
            out[:, c : c + wide] = term[i * rows : (i + 1) * rows, :].astype(out.dtype)


def pair_rows(xs, gs, gates, order, first, weights, kinds):
    blocks = len(xs)
    rows, width = xs[0].shape
    hidden = weights[0].shape[1]
    there = pl.BlockSpec(memory_space=pl.ANY)
    near = pl.BlockSpec(memory_space=pltpu.VMEM)
    count = blocks * rows
    return pl.pallas_call(
        partial(pair_kernel, blocks, first, 512 if width % 512 == 0 else width),
        in_specs=[pl.BlockSpec(memory_space=pltpu.SMEM)] + [there] * (2 * blocks) + [near] + [there] * 6,
        out_specs=[near] * blocks,
        out_shape=[jax.ShapeDtypeStruct((rows, width), kind) for kind in kinds],
        scratch_shapes=[
            pltpu.VMEM((count, width), BF16),
            pltpu.VMEM((count, width), BF16),
            pltpu.VMEM((width, 4 * hidden), BF16),
            pltpu.VMEM((2 * hidden, width), BF16),
            pltpu.VMEM((count, 4 * hidden), BF16),
            pltpu.SemaphoreType.DMA((2 * blocks + 6,)),
        ],
        compiler_params=pltpu.CompilerParams(vmem_limit_bytes=40 * 2**20),
        cost_estimate=pl.CostEstimate(
            flops=20 * count * width * hidden,
            bytes_accessed=12 * width * hidden + 7 * count * width,
            transcendentals=2 * count * hidden,
        ),
        name="pair_rows",
    )(order, *xs, *gs, gates, *weights)


def gathered(layer_input, out_grad, expert_ids, gates, w_gate, w_up, w_down):
    owners = lax.axis_size("expert")
    ring = owners // 4
    rows = layer_input.shape[0]
    me = lax.axis_index("expert")
    core, chip = me % 2, me // 2
    y, z = chip % 2, chip // 2

    def turn(value, by):
        return lax.ppermute(value, "expert", [(i, (i + 4 * by) % owners) for i in range(owners)])

    def swap(value, bit):
        return lax.ppermute(value, "expert", [(i, i ^ bit) for i in range(owners)])

    own = (w_gate[0], w_up[0], w_down[0])
    weights = own + tuple(swap(w, 1) for w in own)

    named = expert_ids[:, :, None] == jnp.arange(owners, dtype=jnp.int32)[None, None, :]
    dense = jnp.sum(jnp.where(named, gates[:, :, None], 0.0), axis=1)
    every = lax.all_gather(dense, "expert", tiled=True)
    pair = [jnp.sum(jnp.where(jnp.arange(owners)[None, :] == e, every, 0.0), axis=1) for e in (me, me ^ 1)]
    gate_pair = jnp.stack(pair, axis=1)
    zs = (z - jnp.arange(ring)) % ring
    order = ((zs[:, None] * 2 + jnp.stack([y, 1 - y])[None, :]) * 2 + core).reshape(-1).astype(jnp.int32)

    x_own, g_own = layer_input, out_grad
    total = None
    for s in range(ring):
        if s:
            x_own, g_own = turn(x_own, 1), turn(g_own, 1)
        x_far, g_far = swap(x_own, 2), swap(g_own, 2)
        near, far = pair_rows((x_own, x_far), (g_own, g_far), gate_pair, order, 2 * s, weights, (F32, BF16))
        both = near + swap(far, 2).astype(F32)
        if s:
            both = turn(both.astype(BF16), -s).astype(F32)
        total = both if total is None else total + both
    return total


def expert_rows(rows_in, rows_grad, gate_w, up_w, down_w):
    pre_gate = jnp.dot(rows_in, gate_w, preferred_element_type=F32)
    pre_up = jnp.dot(rows_in, up_w, preferred_element_type=F32)
    back = lax.dot_general(rows_grad, down_w, LAST, preferred_element_type=F32)
    sig = jax.nn.sigmoid(pre_gate)
    d_gate = (back * pre_up * sig * (1.0 + pre_gate * (1.0 - sig))).astype(BF16)
    d_up = (back * pre_gate * sig).astype(BF16)
    term = lax.dot_general(d_gate, gate_w, LAST, preferred_element_type=F32)
    return term + lax.dot_general(d_up, up_w, LAST, preferred_element_type=F32)


def routed(layer_input, out_grad, expert_ids, gates, w_gate, w_up, w_down):
    owners = lax.axis_size("expert")
    rows, width = layer_input.shape
    choose = expert_ids.shape[1]
    capacity = 5 * rows * choose // (4 * owners)
    flat_ids = expert_ids.reshape(-1)
    flat_gates = gates.reshape(-1)
    assigned = flat_ids.shape[0]
    onehot = flat_ids[:, None] == jnp.arange(owners, dtype=jnp.int32)[None, :]
    earlier = jnp.tril(jnp.ones((assigned, assigned), BF16), -1)
    before = jnp.dot(earlier, onehot.astype(BF16), preferred_element_type=F32)
    position = jnp.sum(jnp.where(onehot, before, 0.0), axis=1).astype(jnp.int32)
    slot = flat_ids * capacity + position
    source = jnp.full((owners * capacity,), -1, jnp.int32).at[slot].set(jnp.arange(assigned, dtype=jnp.int32))
    valid = source >= 0
    safe = jnp.maximum(source, 0)
    token = safe // choose
    send_in = jnp.where(valid[:, None], layer_input[token], jnp.zeros((), BF16))
    gate_val = jnp.where(valid, flat_gates[safe], 0.0)
    send_grad = (gate_val[:, None] * out_grad[token].astype(F32)).astype(BF16)

    def exchange(value):
        value = value.reshape(owners, capacity, width)
        value = lax.all_to_all(value, "expert", split_axis=0, concat_axis=0, tiled=True)
        return value.reshape(owners * capacity, width)

    term = expert_rows(exchange(send_in), exchange(send_grad), w_gate[0], w_up[0], w_down[0])
    picked = exchange(term)[slot].reshape(rows, choose, width)
    return jnp.sum(picked, axis=1)


def on_device(layer_input, out_grad, expert_ids, gates, w_gate, w_up, w_down):
    owners = lax.axis_size("expert")
    dense = owners % 4 == 0 and expert_ids.shape[1] * 4 >= owners
    plan = gathered if dense else routed
    return plan(layer_input, out_grad, expert_ids, gates, w_gate, w_up, w_down)


def solution(mesh):
    rows = P(("group", "expert"), None)
    owned = P("expert", None, None)
    return jax.shard_map(
        on_device,
        mesh=mesh,
        in_specs=(rows, rows, rows, rows, owned, owned, owned),
        out_specs=rows,
        check_vma=False,
    )
```

time: 552 us -> 222 us (0.40)
  the two profiles are of different devices: /device:TPU:13 before, /device:TPU:0 now
where the time goes in v1:
time: 222 us
  waiting for transfers between devices  121 us (55%)
  Pallas kernels  34.2 us (15%)
  blocking collectives  31.9 us (14%)
  starting transfers between devices  19.2 us (9%)
  local copies, waits for them, and re-layouts  12.7 us (6%)
  other arithmetic  2.67 us (1%)
    ppermute x15, waiting for transfers between devices, swap(): return lax.ppermute(value, 'expert', [(i, i ^ bit) for i in range(owners)])  70.6 us
    ppermute x9, waiting for transfers between devices, turn(): lax.ppermute(value, 'expert', [(i, (i + 4 * by) % owners) for i in range(...  50.3 us
    pallas_call x4, Pallas kernels, pair_rows(): pl.pallas_call(partial(pair_kernel, blocks, first, 512 if width % 512 ==...  34.2 us
    all_gather x1, blocking collectives, gathered(): every = lax.all_gather(dense, 'expert', tiled=True)  31.9 us
    ppermute x15, starting transfers between devices, swap(): return lax.ppermute(value, 'expert', [(i, i ^ bit) for i in range(owners)])  14.4 us
    unnamed x38, local copies, waits for them, and re-layouts  12.3 us
    ppermute x9, starting transfers between devices, turn(): lax.ppermute(value, 'expert', [(i, (i + 4 * by) % owners) for i in range(...  4.8 us
  transfers between devices with their start and end apart: 24, of which 15 were waited for; matrix products, arithmetic and copies ran while one was open for 1% of the time, Pallas kernels for 15%

profile of v1, /device:TPU:0, one launch (start us, length us, event | category | flops | bytes accessed | tf_op | source)
XLA Modules:
  0.0 221.8 jit_solution(5038860582127459652)
XLA Ops:
  0.0 3.0 %collective-permute-start.6 = (bf16[128,2048]{1,0:T(8,128)(2,1)}, bf16[128,2048]{1,0:T(8,128)(2,1)S(1)}, u32[]{:S(2)}, u32[]{:S(2)}) collective-permute-start(bf16[128,2048]{1,0:T(8,128)(2,1)} %refs_0_.1), channel_id=1, source_target_pairs={{0,4},{1,5},{2,6},{3,7},{4,8},{5,9},{6,10},{7,11},{8,12},{9,13},{1... | collective-permute-start | bytes 1572872 | tf_op jit(solution)/shard_map/ppermute | solution.py:107
  3.0 1.6 collective-permute-start.8
  5.1 12.9 %collective-permute-done.6.refs_0_ = bf16[128,2048]{1,0:T(8,128)(2,1)S(1)} collective-permute-done((bf16[128,2048]{1,0:T(8,128)(2,1)}, bf16[128,2048]{1,0:T(8,128)(2,1)S(1)}, u32[]{:S(2)}, u32[]{:S(2)}) %collective-permute-start.6) | collective-permute-done | bytes 524320 | tf_op jit(solution)/shard_map/ppermute | solution.py:107
  18.0 1.8 collective-permute-start.7
  19.8 8.6 %collective-permute-done.8.refs_2_ = bf16[128,2048]{1,0:T(8,128)(2,1)S(1)} collective-permute-done((bf16[128,2048]{1,0:T(8,128)(2,1)}, bf16[128,2048]{1,0:T(8,128)(2,1)S(1)}, u32[]{:S(2)}, u32[]{:S(2)}) %collective-permute-start.8) | collective-permute-done | bytes 524320 | tf_op jit(solution)/shard_map/ppermute | solution.py:107
  28.4 1.5 collective-permute-start.9
  32.0 9.6 %collective-permute-done.9.refs_3_ = bf16[128,2048]{1,0:T(8,128)(2,1)S(1)} collective-permute-done((bf16[128,2048]{1,0:T(8,128)(2,1)S(1)}, bf16[128,2048]{1,0:T(8,128)(2,1)S(1)}, u32[]{:S(2)}, u32[]{:S(2)}) %collective-permute-start.9) | collective-permute-done | bytes 524320 | tf_op jit(solution)/shard_map/ppermute | solution.py:110
  45.3 13.8 %collective-permute-done.14.refs_2_ = bf16[128,2048]{1,0:T(8,128)(2,1)} collective-permute-done((bf16[128,2048]{1,0:T(8,128)(2,1)S(1)}, bf16[128,2048]{1,0:T(8,128)(2,1)}, u32[]{:S(2)}, u32[]{:S(2)}) %collective-permute-start.14) | collective-permute-done | bytes 524320 | tf_op jit(solution)/shard_map/ppermute | solution.py:107
  59.2 31.9 %all_gather.3 = f32[2048,16]{0,1:T(8,128)S(1)} all-gather(f32[128,16]{0,1:T(8,128)S(1)} %select_reduce_fusion.2), channel_id=1, replica_groups=mesh['group'=2,'expert'=16] {'expert'}, dimensions={0}, use_global_device_ids=true | all-gather | bytes 139264 | tf_op jit(solution)/shard_map/all_gather | solution.py:117
  97.0 1.6 copy-done
  98.6 1.6 copy-done.2
  100.2 1.6 copy-done.4
  106.0 8.5 %pair_rows.5 = (f32[128,2048]{1,0:T(8,128)S(1)}, bf16[128,2048]{1,0:T(8,128)(2,1)S(1)}) custom-call(s32[8]{0:T(128)S(1)} %add.73.order, bf16[128,2048]{1,0:T(8,128)(2,1)S(1)} %copy-done.8, bf16[128,2048]{1,0:T(8,128)(2,1)S(1)} %copy-done.12, bf16[128,2048]{1,0:T(8,128)(2,1)S(1)} %copy-done.10, bf16[128,2048]{1,0:T(8,128)(2,1)S(1)} %copy-done.14, ...), custom_call_target="tpu_custom_call" | custom-call | flops 5368709120 | bytes 16252928 | tf_op jit(solution)/shard_map/pair_rows/pallas_call | solution.py:75
  115.6 2.0 collective-permute-done.15.refs_3_
  118.7 8.4 %pair_rows.6 = (f32[128,2048]{1,0:T(8,128)S(1)}, bf16[128,2048]{1,0:T(8,128)(2,1)S(1)}) custom-call(s32[8]{0:T(128)S(1)} %add.73.order, bf16[128,2048]{1,0:T(8,128)(2,1)} %collective-permute-done.12.refs_0_, bf16[128,2048]{1,0:T(8,128)(2,1)} %collective-permute-done.13.refs_1_, bf16[128,2048]{1,0:T(8,128)(2,1)} %collective-permute-done.14.refs_2_, ...), custom_call_target="tpu_custom_call" | custom-call | flops 5368709120 | bytes 16252928 | tf_op jit(solution)/shard_map/pair_rows/pallas_call | solution.py:75
  127.2 12.8 %collective-permute-done.19.refs_1_ = bf16[128,2048]{1,0:T(8,128)(2,1)S(1)} collective-permute-done((bf16[128,2048]{1,0:T(8,128)(2,1)}, bf16[128,2048]{1,0:T(8,128)(2,1)S(1)}, u32[]{:S(2)}, u32[]{:S(2)}) %collective-permute-start.19) | collective-permute-done | bytes 524320 | tf_op jit(solution)/shard_map/ppermute | solution.py:110
  141.0 10.2 %collective-permute-done.21.refs_3_ = bf16[128,2048]{1,0:T(8,128)(2,1)S(1)} collective-permute-done((bf16[128,2048]{1,0:T(8,128)(2,1)}, bf16[128,2048]{1,0:T(8,128)(2,1)S(1)}, u32[]{:S(2)}, u32[]{:S(2)}) %collective-permute-start.21) | collective-permute-done | bytes 524320 | tf_op jit(solution)/shard_map/ppermute | solution.py:110
  151.2 8.7 %pair_rows.7 = (f32[128,2048]{1,0:T(8,128)S(1)}, bf16[128,2048]{1,0:T(8,128)(2,1)S(1)}) custom-call(s32[8]{0:T(128)S(1)} %add.73.order, bf16[128,2048]{1,0:T(8,128)(2,1)S(1)} %copy-done.16, bf16[128,2048]{1,0:T(8,128)(2,1)S(1)} %collective-permute-done.19.refs_1_, bf16[128,2048]{1,0:T(8,128)(2,1)S(1)} %copy-done.18, ...), custom_call_target="tpu_custom_call" | custom-call | flops 5368709120 | bytes 16252928 | tf_op jit(solution)/shard_map/pair_rows/pallas_call | solution.py:75
  162.4 8.5 %pair_rows.4 = (f32[128,2048]{1,0:T(8,128)S(1)}, bf16[128,2048]{1,0:T(8,128)(2,1)S(1)}) custom-call(s32[8]{0:T(128)S(1)} %add.73.order, bf16[128,2048]{1,0:T(8,128)(2,1)S(1)} %copy-done.5, bf16[128,2048]{1,0:T(8,128)(2,1)S(1)} %collective-permute-done.refs_1_, bf16[128,2048]{1,0:T(8,128)(2,1)S(1)} %copy-done.6, ...), custom_call_target="tpu_custom_call" | custom-call | flops 5368709120 | bytes 16252928 | tf_op jit(solution)/shard_map/pair_rows/pallas_call | solution.py:75
  172.1 1.6 collective-permute-done.10
  173.9 11.1 %collective-permute-done.16 = bf16[128,2048]{1,0:T(8,128)(2,1)S(1)} collective-permute-done((bf16[128,2048]{1,0:T(8,128)(2,1)S(1)}, bf16[128,2048]{1,0:T(8,128)(2,1)S(1)}, u32[]{:S(2)}, u32[]{:S(2)}) %collective-permute-start.16) | collective-permute-done | bytes 524320 | tf_op jit(solution)/shard_map/ppermute | solution.py:110
  185.1 11.0 %collective-permute-done.22 = bf16[128,2048]{1,0:T(8,128)(2,1)S(1)} collective-permute-done((bf16[128,2048]{1,0:T(8,128)(2,1)S(1)}, bf16[128,2048]{1,0:T(8,128)(2,1)S(1)}, u32[]{:S(2)}, u32[]{:S(2)}) %collective-permute-start.22) | collective-permute-done | bytes 524320 | tf_op jit(solution)/shard_map/ppermute | solution.py:110
  196.3 10.5 %collective-permute-done.5 = bf16[128,2048]{1,0:T(8,128)(2,1)S(1)} collective-permute-done((bf16[128,2048]{1,0:T(8,128)(2,1)S(1)}, bf16[128,2048]{1,0:T(8,128)(2,1)S(1)}, u32[]{:S(2)}, u32[]{:S(2)}) %collective-permute-start.5) | collective-permute-done | bytes 524320 | tf_op jit(solution)/shard_map/ppermute | solution.py:110
  206.8 13.6 %collective-permute-done.17 = bf16[128,2048]{1,0:T(8,128)(2,1)S(1)} collective-permute-done((bf16[128,2048]{1,0:T(8,128)(2,1)S(1)}, bf16[128,2048]{1,0:T(8,128)(2,1)S(1)}, u32[]{:S(2)}, u32[]{:S(2)}) %collective-permute-start.17) | collective-permute-done | bytes 524320 | tf_op jit(solution)/shard_map/ppermute | solution.py:107
  (80 shorter events, 25.1 us)
Async XLA Ops:
  0.0 18.0 %collective-permute-start.6 = (bf16[128,2048]{1,0:T(8,128)(2,1)}, bf16[128,2048]{1,0:T(8,128)(2,1)S(1)}, u32[]{:S(2)}, u32[]{:S(2)}) collective-permute-start(bf16[128,2048]{1,0:T(8,128)(2,1)} %refs_0_.1), channel_id=1, source_target_pairs={{0,4},{1,5},{2,6},{3,7},{4,8},{5,9},{6,10},{7,11},{8,12},{9,13},{1... | collective-permute-start | bytes 1572872 | tf_op jit(solution)/shard_map/ppermute | solution.py:107
  3.0 25.4 %collective-permute-start.8 = (bf16[128,2048]{1,0:T(8,128)(2,1)}, bf16[128,2048]{1,0:T(8,128)(2,1)S(1)}, u32[]{:S(2)}, u32[]{:S(2)}) collective-permute-start(bf16[128,2048]{1,0:T(8,128)(2,1)} %refs_2_.1), channel_id=1, source_target_pairs={{0,4},{1,5},{2,6},{3,7},{4,8},{5,9},{6,10},{7,11},{8,12},{9,13},{1... | collective-permute-start | bytes 1572872 | tf_op jit(solution)/shard_map/ppermute | solution.py:107
  4.6 89.3 %collective-permute-start.2 = (bf16[2048,512]{1,0:T(8,128)(2,1)}, bf16[2048,512]{1,0:T(8,128)(2,1)S(1)}, u32[]{:S(2)}, u32[]{:S(2)}) collective-permute-start(bf16[2048,512]{1,0:T(8,128)(2,1)} %bitcast.7), channel_id=1, source_target_pairs={{0,1},{1,0},{2,3},{3,2},{4,5},{5,4},{6,7},{7,6},{8,9},{9,8},{10,11... | collective-permute-start | bytes 6291464 | tf_op jit(solution)/shard_map/ppermute | solution.py:110
  4.6 90.4 %collective-permute-start.3 = (bf16[2048,512]{1,0:T(8,128)(2,1)}, bf16[2048,512]{1,0:T(8,128)(2,1)}, u32[]{:S(2)}, u32[]{:S(2)}) collective-permute-start(bf16[2048,512]{1,0:T(8,128)(2,1)} %bitcast.12), channel_id=1, source_target_pairs={{0,1},{1,0},{2,3},{3,2},{4,5},{5,4},{6,7},{7,6},{8,9},{9,8},{10,11... | collective-permute-start | bytes 6291464 | tf_op jit(solution)/shard_map/ppermute | solution.py:110
  5.1 90.9 %collective-permute-start.4 = (bf16[512,2048]{1,0:T(8,128)(2,1)}, bf16[512,2048]{1,0:T(8,128)(2,1)}, u32[]{:S(2)}, u32[]{:S(2)}) collective-permute-start(bf16[512,2048]{1,0:T(8,128)(2,1)} %bitcast.17), channel_id=1, source_target_pairs={{0,1},{1,0},{2,3},{3,2},{4,5},{5,4},{6,7},{7,6},{8,9},{9,8},{10,11... | collective-permute-start | bytes 6291464 | tf_op jit(solution)/shard_map/ppermute | solution.py:110
  18.0 12.3 %collective-permute-start.7 = (bf16[128,2048]{1,0:T(8,128)(2,1)S(1)}, bf16[128,2048]{1,0:T(8,128)(2,1)S(1)}, u32[]{:S(2)}, u32[]{:S(2)}) collective-permute-start(bf16[128,2048]{1,0:T(8,128)(2,1)S(1)} %collective-permute-done.6.refs_0_), channel_id=1, source_target_pairs={{0,2},{1,3},{2,0},{3,1},{4,6},{5,7},{6,4},{7,5},{8,10},{9,11},{10,... | collective-permute-start | bytes 1572872 | tf_op jit(solution)/shard_map/ppermute | solution.py:110
  28.4 13.1 %collective-permute-start.9 = (bf16[128,2048]{1,0:T(8,128)(2,1)S(1)}, bf16[128,2048]{1,0:T(8,128)(2,1)S(1)}, u32[]{:S(2)}, u32[]{:S(2)}) collective-permute-start(bf16[128,2048]{1,0:T(8,128)(2,1)S(1)} %collective-permute-done.8.refs_2_), channel_id=1, source_target_pairs={{0,2},{1,3},{2,0},{3,1},{4,6},{5,7},{6,4},{7,5},{8,10},{9,11},{10,... | collective-permute-start | bytes 1572872 | tf_op jit(solution)/shard_map/ppermute | solution.py:110
  31.1 14.1 %collective-permute-start.12 = (bf16[128,2048]{1,0:T(8,128)(2,1)S(1)}, bf16[128,2048]{1,0:T(8,128)(2,1)}, u32[]{:S(2)}, u32[]{:S(2)}) collective-permute-start(bf16[128,2048]{1,0:T(8,128)(2,1)S(1)} %collective-permute-done.6.refs_0_), channel_id=1, source_target_pairs={{0,4},{1,5},{2,6},{3,7},{4,8},{5,9},{6,10},{7,11},{8,12},{9,13},{1... | collective-permute-start | bytes 1572872 | tf_op jit(solution)/shard_map/ppermute | solution.py:107
  42.3 16.8 %collective-permute-start.14 = (bf16[128,2048]{1,0:T(8,128)(2,1)S(1)}, bf16[128,2048]{1,0:T(8,128)(2,1)}, u32[]{:S(2)}, u32[]{:S(2)}) collective-permute-start(bf16[128,2048]{1,0:T(8,128)(2,1)S(1)} %collective-permute-done.8.refs_2_), channel_id=1, source_target_pairs={{0,4},{1,5},{2,6},{3,7},{4,8},{5,9},{6,10},{7,11},{8,12},{9,13},{1... | collective-permute-start | bytes 1572872 | tf_op jit(solution)/shard_map/ppermute | solution.py:107
  45.3 46.0 %collective-permute-start.18 = (bf16[128,2048]{1,0:T(8,128)(2,1)}, bf16[128,2048]{1,0:T(8,128)(2,1)S(1)}, u32[]{:S(2)}, u32[]{:S(2)}) collective-permute-start(bf16[128,2048]{1,0:T(8,128)(2,1)} %collective-permute-done.12.refs_0_), channel_id=1, source_target_pairs={{0,4},{1,5},{2,6},{3,7},{4,8},{5,9},{6,10},{7,11},{8,12},{9,13},{1... | collective-permute-start | bytes 1572872 | tf_op jit(solution)/shard_map/ppermute | solution.py:107
  59.1 33.2 %collective-permute-start.20 = (bf16[128,2048]{1,0:T(8,128)(2,1)}, bf16[128,2048]{1,0:T(8,128)(2,1)S(1)}, u32[]{:S(2)}, u32[]{:S(2)}) collective-permute-start(bf16[128,2048]{1,0:T(8,128)(2,1)} %collective-permute-done.14.refs_2_), channel_id=1, source_target_pairs={{0,4},{1,5},{2,6},{3,7},{4,8},{5,9},{6,10},{7,11},{8,12},{9,13},{1... | collective-permute-start | bytes 1572872 | tf_op jit(solution)/shard_map/ppermute | solution.py:107
  91.2 23.2 %collective-permute-start.13 = (bf16[128,2048]{1,0:T(8,128)(2,1)}, bf16[128,2048]{1,0:T(8,128)(2,1)}, u32[]{:S(2)}, u32[]{:S(2)}) collective-permute-start(bf16[128,2048]{1,0:T(8,128)(2,1)} %collective-permute-done.12.refs_0_), channel_id=1, source_target_pairs={{0,2},{1,3},{2,0},{3,1},{4,6},{5,7},{6,4},{7,5},{8,10},{9,11},{10,... | collective-permute-start | bytes 1572872 | tf_op jit(solution)/shard_map/ppermute | solution.py:110
  92.3 25.3 %collective-permute-start.15 = (bf16[128,2048]{1,0:T(8,128)(2,1)}, bf16[128,2048]{1,0:T(8,128)(2,1)}, u32[]{:S(2)}, u32[]{:S(2)}) collective-permute-start(bf16[128,2048]{1,0:T(8,128)(2,1)} %collective-permute-done.14.refs_2_), channel_id=1, source_target_pairs={{0,2},{1,3},{2,0},{3,1},{4,6},{5,7},{6,4},{7,5},{8,10},{9,11},{10,... | collective-permute-start | bytes 1572872 | tf_op jit(solution)/shard_map/ppermute | solution.py:110
  93.9 67.1 %collective-permute-start = (bf16[128,2048]{1,0:T(8,128)(2,1)}, bf16[128,2048]{1,0:T(8,128)(2,1)S(1)}, u32[]{:S(2)}, u32[]{:S(2)}) collective-permute-start(bf16[128,2048]{1,0:T(8,128)(2,1)} %refs_0_.1), channel_id=1, source_target_pairs={{0,2},{1,3},{2,0},{3,1},{4,6},{5,7},{6,4},{7,5},{8,10},{9,11},{10,... | collective-permute-start | bytes 1572872 | tf_op jit(solution)/shard_map/ppermute | solution.py:110
  95.0 45.0 %collective-permute-start.19 = (bf16[128,2048]{1,0:T(8,128)(2,1)}, bf16[128,2048]{1,0:T(8,128)(2,1)S(1)}, u32[]{:S(2)}, u32[]{:S(2)}) collective-permute-start(bf16[128,2048]{1,0:T(8,128)(2,1)} %copy-done.15), channel_id=1, source_target_pairs={{0,2},{1,3},{2,0},{3,1},{4,6},{5,7},{6,4},{7,5},{8,10},{9,11},{10,... | collective-permute-start | bytes 1572872 | tf_op jit(solution)/shard_map/ppermute | solution.py:110
  96.0 55.2 %collective-permute-start.21 = (bf16[128,2048]{1,0:T(8,128)(2,1)}, bf16[128,2048]{1,0:T(8,128)(2,1)S(1)}, u32[]{:S(2)}, u32[]{:S(2)}) collective-permute-start(bf16[128,2048]{1,0:T(8,128)(2,1)} %copy-done.17), channel_id=1, source_target_pairs={{0,2},{1,3},{2,0},{3,1},{4,6},{5,7},{6,4},{7,5},{8,10},{9,11},{10,... | collective-permute-start | bytes 1572872 | tf_op jit(solution)/shard_map/ppermute | solution.py:110
  114.5 47.9 %collective-permute-start.1 = (bf16[128,2048]{1,0:T(8,128)(2,1)S(1)}, bf16[128,2048]{1,0:T(8,128)(2,1)S(1)}, u32[]{:S(2)}, u32[]{:S(2)}) collective-permute-start(bf16[128,2048]{1,0:T(8,128)(2,1)S(1)} %copy-done.6), channel_id=1, source_target_pairs={{0,2},{1,3},{2,0},{3,1},{4,6},{5,7},{6,4},{7,5},{8,10},{9,11},{10,... | collective-permute-start | bytes 1572872 | tf_op jit(solution)/shard_map/ppermute | solution.py:110
  117.6 56.1 %collective-permute-start.10 = (bf16[128,2048]{1,0:T(8,128)(2,1)S(1)}, bf16[128,2048]{1,0:T(8,128)(2,1)S(1)}, u32[]{:S(2)}, u32[]{:S(2)}) collective-permute-start(bf16[128,2048]{1,0:T(8,128)(2,1)S(1)} %get-tuple-element.16), channel_id=1, source_target_pairs={{0,2},{1,3},{2,0},{3,1},{4,6},{5,7},{6,4},{7,5},{8,10},{9,11},{10,... | collective-permute-start | bytes 1572872 | tf_op jit(solution)/shard_map/ppermute | solution.py:110
  140.0 44.9 %collective-permute-start.16 = (bf16[128,2048]{1,0:T(8,128)(2,1)S(1)}, bf16[128,2048]{1,0:T(8,128)(2,1)S(1)}, u32[]{:S(2)}, u32[]{:S(2)}) collective-permute-start(bf16[128,2048]{1,0:T(8,128)(2,1)S(1)} %get-tuple-element.18), channel_id=1, source_target_pairs={{0,2},{1,3},{2,0},{3,1},{4,6},{5,7},{6,4},{7,5},{8,10},{9,11},{10,... | collective-permute-start | bytes 1572872 | tf_op jit(solution)/shard_map/ppermute | solution.py:110
  159.9 36.2 %collective-permute-start.22 = (bf16[128,2048]{1,0:T(8,128)(2,1)S(1)}, bf16[128,2048]{1,0:T(8,128)(2,1)S(1)}, u32[]{:S(2)}, u32[]{:S(2)}) collective-permute-start(bf16[128,2048]{1,0:T(8,128)(2,1)S(1)} %get-tuple-element.20), channel_id=1, source_target_pairs={{0,2},{1,3},{2,0},{3,1},{4,6},{5,7},{6,4},{7,5},{8,10},{9,11},{10,... | collective-permute-start | bytes 1572872 | tf_op jit(solution)/shard_map/ppermute | solution.py:110
  171.0 35.8 %collective-permute-start.5 = (bf16[128,2048]{1,0:T(8,128)(2,1)S(1)}, bf16[128,2048]{1,0:T(8,128)(2,1)S(1)}, u32[]{:S(2)}, u32[]{:S(2)}) collective-permute-start(bf16[128,2048]{1,0:T(8,128)(2,1)S(1)} %get-tuple-element.14), channel_id=1, source_target_pairs={{0,2},{1,3},{2,0},{3,1},{4,6},{5,7},{6,4},{7,5},{8,10},{9,11},{10,... | collective-permute-start | bytes 1572872 | tf_op jit(solution)/shard_map/ppermute | solution.py:110
  173.8 33.0 %collective-permute-start.11 = (bf16[128,2048]{1,0:T(8,128)(2,1)S(1)}, bf16[128,2048]{1,0:T(8,128)(2,1)S(1)}, u32[]{:S(2)}, u32[]{:S(2)}) collective-permute-start(bf16[128,2048]{1,0:T(8,128)(2,1)S(1)} %add_convert_fusion.2), channel_id=1, source_target_pairs={{0,12},{1,13},{2,14},{3,15},{4,0},{5,1},{6,2},{7,3},{8,4},{9,5},{1... | collective-permute-start | bytes 1572872 | tf_op jit(solution)/shard_map/ppermute | solution.py:107
  185.0 35.4 %collective-permute-start.17 = (bf16[128,2048]{1,0:T(8,128)(2,1)S(1)}, bf16[128,2048]{1,0:T(8,128)(2,1)S(1)}, u32[]{:S(2)}, u32[]{:S(2)}) collective-permute-start(bf16[128,2048]{1,0:T(8,128)(2,1)S(1)} %add_convert_fusion.1), channel_id=1, source_target_pairs={{0,8},{1,9},{2,10},{3,11},{4,12},{5,13},{6,14},{7,15},{8,0},{9,1},... | collective-permute-start | bytes 1572872 | tf_op jit(solution)/shard_map/ppermute | solution.py:107
  196.3 24.2 %collective-permute-start.23 = (bf16[128,2048]{1,0:T(8,128)(2,1)S(1)}, bf16[128,2048]{1,0:T(8,128)(2,1)S(1)}, u32[]{:S(2)}, u32[]{:S(2)}) collective-permute-start(bf16[128,2048]{1,0:T(8,128)(2,1)S(1)} %add_convert_fusion), channel_id=1, source_target_pairs={{0,4},{1,5},{2,6},{3,7},{4,8},{5,9},{6,10},{7,11},{8,12},{9,13},{1... | collective-permute-start | bytes 1572872 | tf_op jit(solution)/shard_map/ppermute | solution.py:107
  (19 other events, 180.9 us)

commit v2 on v1

--- a/solution.py
+++ b/solution.py
@@ -12,13 +12,13 @@
 LAST = (((1,), (1,)), ((), ()))
 
 
-def pair_kernel(blocks, first, wide, order, *refs):
-    xs, gs = refs[:blocks], refs[blocks : 2 * blocks]
-    gates = refs[2 * blocks]
-    weights = refs[2 * blocks + 1 : 2 * blocks + 7]
-    outs = refs[2 * blocks + 7 : 3 * blocks + 7]
-    x_buf, g_buf, w_in, w_out, d_buf, sems = refs[3 * blocks + 7 :]
-    rows = xs[0].shape[0]
+def pair_kernel(blocks, wide, experts, *refs):
+    sides = refs[:blocks]
+    gates = refs[blocks]
+    weights = refs[blocks + 1 : blocks + 7]
+    outs = refs[blocks + 7 : 2 * blocks + 7]
+    x_buf, g_buf, w_in, w_out, d_buf, sems = refs[2 * blocks + 7 :]
+    rows = sides[0].shape[0]
     width, hidden = weights[0].shape
     copies = {}
 
@@ -27,15 +27,16 @@
         copies[key].start()
 
     for i in range(blocks):
-        start(("x", i), xs[i], x_buf.at[pl.ds(i * rows, rows)])
+        start(("x", i), sides[i].at[:, pl.ds(0, width)], x_buf.at[pl.ds(i * rows, rows)])
     start(("w", 0), weights[0], w_in.at[:, pl.ds(0, hidden)])
     start(("w", 1), weights[1], w_in.at[:, pl.ds(hidden, hidden)])
     for i in range(blocks):
-        start(("g", i), gs[i], g_buf.at[pl.ds(i * rows, rows)])
+        start(("g", i), sides[i].at[:, pl.ds(width, width)], g_buf.at[pl.ds(i * rows, rows)])
     start(("w", 2), weights[2], w_out.at[pl.ds(0, hidden)])
     start(("w", 3), weights[3], w_in.at[:, pl.ds(2 * hidden, hidden)])
     start(("w", 4), weights[4], w_in.at[:, pl.ds(3 * hidden, hidden)])
     start(("w", 5), weights[5], w_out.at[pl.ds(hidden, hidden)])
+    lanes = lax.broadcasted_iota(jnp.int32, gates.shape, 1)
     for i in range(blocks):
         copies["x", i].wait()
     for k in range(2):
@@ -51,10 +52,7 @@
         back = lax.dot_general(
             g_buf[...], w_out[k * hidden : (k + 1) * hidden, :], LAST, preferred_element_type=F32
         )
-        gate = [
-            gates[pl.ds(pl.multiple_of(order[first + i] * rows, rows), rows), k : k + 1] for i in range(blocks)
-        ]
-        back = back * jnp.concatenate(gate, axis=0)
+        back = back * jnp.sum(jnp.where(lanes == experts[k], gates[...], 0.0), axis=1, keepdims=True)
         sig = jax.nn.sigmoid(pre_gate)
         back_sig = back * sig
         d_buf[:, at : at + hidden] = (back_sig * pre_up * (1.0 + pre_gate * (1.0 - sig))).astype(BF16)
@@ -65,16 +63,16 @@
             out[:, c : c + wide] = term[i * rows : (i + 1) * rows, :].astype(out.dtype)
 
 
-def pair_rows(xs, gs, gates, order, first, weights, kinds):
-    blocks = len(xs)
-    rows, width = xs[0].shape
+def pair_rows(sides, gates, experts, weights, kinds):
+    blocks = len(sides)
+    rows, width = sides[0].shape[0], sides[0].shape[1] // 2
     hidden = weights[0].shape[1]
-    there = pl.BlockSpec(memory_space=pl.ANY)
+    there = pl.BlockSpec(memory_space=pltpu.HBM)
     near = pl.BlockSpec(memory_space=pltpu.VMEM)
     count = blocks * rows
     return pl.pallas_call(
-        partial(pair_kernel, blocks, first, 512 if width % 512 == 0 else width),
-        in_specs=[pl.BlockSpec(memory_space=pltpu.SMEM)] + [there] * (2 * blocks) + [near] + [there] * 6,
+        partial(pair_kernel, blocks, 512 if width % 512 == 0 else width),
+        in_specs=[pl.BlockSpec(memory_space=pltpu.SMEM)] + [there] * blocks + [near] + [there] * 6,
         out_specs=[near] * blocks,
         out_shape=[jax.ShapeDtypeStruct((rows, width), kind) for kind in kinds],
         scratch_shapes=[
@@ -85,23 +83,20 @@
             pltpu.VMEM((count, 4 * hidden), BF16),
             pltpu.SemaphoreType.DMA((2 * blocks + 6,)),
         ],
-        compiler_params=pltpu.CompilerParams(vmem_limit_bytes=40 * 2**20),
+        compiler_params=pltpu.CompilerParams(vmem_limit_bytes=60 * 2**20),
         cost_estimate=pl.CostEstimate(
             flops=20 * count * width * hidden,
             bytes_accessed=12 * width * hidden + 7 * count * width,
             transcendentals=2 * count * hidden,
         ),
         name="pair_rows",
-    )(order, *xs, *gs, gates, *weights)
+    )(experts, *sides, gates, *weights)
 
 
 def gathered(layer_input, out_grad, expert_ids, gates, w_gate, w_up, w_down):
     owners = lax.axis_size("expert")
     ring = owners // 4
-    rows = layer_input.shape[0]
     me = lax.axis_index("expert")
-    core, chip = me % 2, me // 2
-    y, z = chip % 2, chip // 2
 
     def turn(value, by):
         return lax.ppermute(value, "expert", [(i, (i + 4 * by) % owners) for i in range(owners)])
@@ -111,23 +106,36 @@
 
     own = (w_gate[0], w_up[0], w_down[0])
     weights = own + tuple(swap(w, 1) for w in own)
+    experts = jnp.stack([me, me ^ 1]).astype(jnp.int32)
 
     named = expert_ids[:, :, None] == jnp.arange(owners, dtype=jnp.int32)[None, None, :]
     dense = jnp.sum(jnp.where(named, gates[:, :, None], 0.0), axis=1)
-    every = lax.all_gather(dense, "expert", tiled=True)
-    pair = [jnp.sum(jnp.where(jnp.arange(owners)[None, :] == e, every, 0.0), axis=1) for e in (me, me ^ 1)]
-    gate_pair = jnp.stack(pair, axis=1)
-    zs = (z - jnp.arange(ring)) % ring
-    order = ((zs[:, None] * 2 + jnp.stack([y, 1 - y])[None, :]) * 2 + core).reshape(-1).astype(jnp.int32)
-
-    x_own, g_own = layer_input, out_grad
+    pair_gates = jnp.concatenate([dense, swap(dense, 2)], axis=0)
+
+    near_side = jnp.concatenate([layer_input, out_grad], axis=1)
+    step_gates = [pair_gates]
+    held, parts = [], []
+    for s in range(ring):
+        far_side = swap(near_side, 2)
+        next_side = turn(near_side, 1) if s + 1 < ring else None
+        if s == 0:
+            far_side, next_side, weights, step_gates = lax.optimization_barrier(
+                (far_side, next_side, weights, step_gates)
+            )
+        else:
+            if s == 1:
+                step_gates = step_gates + [turn(step_gates[0], by) for by in range(1, ring)]
+            near, far = pair_rows(held, step_gates[s - 1], experts, weights, (F32, BF16))
+            far = swap(far, 2)
+            far_side, next_side, step_gates, near = lax.optimization_barrier((far_side, next_side, step_gates, near))
+            parts.append((near, far))
+        held = [near_side, far_side]
+        near_side = next_side
+    near, far = pair_rows(held, step_gates[ring - 1], experts, weights, (F32, BF16))
+    parts.append((near, swap(far, 2)))
     total = None
-    for s in range(ring):
-        if s:
-            x_own, g_own = turn(x_own, 1), turn(g_own, 1)
-        x_far, g_far = swap(x_own, 2), swap(g_own, 2)
-        near, far = pair_rows((x_own, x_far), (g_own, g_far), gate_pair, order, 2 * s, weights, (F32, BF16))
-        both = near + swap(far, 2).astype(F32)
+    for s, (near, far) in enumerate(parts):
+        both = near + far.astype(F32)
         if s:
             both = turn(both.astype(BF16), -s).astype(F32)
         total = both if total is None else total + both

time: 222 us -> 194 us (0.87)
  blocking collectives: 31.9 us -> 0 us
  local copies, waits for them, and re-layouts: 12.7 us -> 2.3 us
  Pallas kernels: 34.2 us -> 43.8 us
  waiting for transfers between devices: 121 us -> 126 us
    all_gather x1 -> x0, blocking collectives: 31.9 us -> none  [gathered(): every = lax.all_gather(dense, 'expert', tiled=True)]
    unnamed x38 -> x27, local copies, waits for them, and re-layouts: 12.3 us -> 1.13 us
    pallas_call x4, Pallas kernels: 34.2 us -> 43.8 us  [pair_rows(): pl.pallas_call(partial(pair_kernel, blocks, 512 if width % 512 == 0 else...]
    ppermute x15 -> x12, waiting for transfers between devices: 70.6 us -> 77.5 us  [swap(): return lax.ppermute(value, 'expert', [(i, i ^ bit) for i in range(owners)])]
    ppermute x15 -> x12, starting transfers between devices: 14.4 us -> 11.5 us  [swap(): return lax.ppermute(value, 'expert', [(i, i ^ bit) for i in range(owners)])]
  transfers between devices with their start and end apart: 24 -> 21, of which waited for: 15 -> 12; matrix products, arithmetic and copies ran while one was open for 1% -> 2% of each run, Pallas kernels for 15% -> 23%
where the time goes in v2:
time: 194 us; the launch traced here: 193 us
  waiting for transfers between devices  126 us (65%)
  Pallas kernels  43.8 us (23%)
  starting transfers between devices  18.3 us (9%)
  other arithmetic  3.02 us (2%)
  local copies, waits for them, and re-layouts  2.3 us (1%)
    ppermute x12, waiting for transfers between devices, swap(): return lax.ppermute(value, 'expert', [(i, i ^ bit) for i in range(owners)])  77.5 us
    ppermute x9, waiting for transfers between devices, turn(): lax.ppermute(value, 'expert', [(i, (i + 4 * by) % owners) for i in range(...  48.2 us
    pallas_call x4, Pallas kernels, pair_rows(): pl.pallas_call(partial(pair_kernel, blocks, 512 if width % 512 == 0 else...  43.8 us
    ppermute x12, starting transfers between devices, swap(): return lax.ppermute(value, 'expert', [(i, i ^ bit) for i in range(owners)])  11.5 us
    ppermute x9, starting transfers between devices, turn(): lax.ppermute(value, 'expert', [(i, (i + 4 * by) % owners) for i in range(...  6.76 us
  transfers between devices with their start and end apart: 21, of which 12 were waited for; matrix products, arithmetic and copies ran while one was open for 2% of the time, Pallas kernels for 23%

profile of v2, /device:TPU:0, one launch (start us, length us, event | category | flops | bytes accessed | tf_op | source)
XLA Modules:
  0.0 193.3 jit_solution(3659501103489597860)
XLA Ops:
  1.7 2.6 %collective-permute-start.5 = (f32[128,16]{0,1:T(8,128)S(1)}, f32[128,16]{0,1:T(8,128)S(1)}, u32[]{:S(2)}, u32[]{:S(2)}) collective-permute-start(f32[128,16]{0,1:T(8,128)S(1)} %select_reduce_fusion), channel_id=1, source_target_pairs={{0,2},{1,3},{2,0},{3,1},{4,6},{5,7},{6,4},{7,5},{8,10},{9,11},{10,... | collective-permute-start | bytes 24584 | tf_op jit(solution)/shard_map/ppermute | solution.py:105
  6.5 2.1 %collective-permute-start.1 = (bf16[128,4096]{1,0:T(8,128)(2,1)S(1)}, bf16[128,4096]{1,0:T(8,128)(2,1)}, u32[]{:S(2)}, u32[]{:S(2)}) collective-permute-start(bf16[128,4096]{1,0:T(8,128)(2,1)S(1)} %constant_dynamic-update-slice_fusion.refs_0_), channel_id=1, source_target_pairs={{0,4},{1,5},{2,6},{3,7},{4,8},{5,9},{6,10},{7,11},{8,12},{9,13},{1... | collective-permute-start | bytes 3145736 | tf_op jit(solution)/shard_map/ppermute | solution.py:102
  8.6 23.2 %collective-permute-done.refs_1_ = bf16[128,4096]{1,0:T(8,128)(2,1)S(1)} collective-permute-done((bf16[128,4096]{1,0:T(8,128)(2,1)S(1)}, bf16[128,4096]{1,0:T(8,128)(2,1)S(1)}, u32[]{:S(2)}, u32[]{:S(2)}) %collective-permute-start) | collective-permute-done | bytes 1048608 | tf_op jit(solution)/shard_map/ppermute | solution.py:105
  31.8 2.2 %collective-permute-done.1.refs_0_ = bf16[128,4096]{1,0:T(8,128)(2,1)} collective-permute-done((bf16[128,4096]{1,0:T(8,128)(2,1)S(1)}, bf16[128,4096]{1,0:T(8,128)(2,1)}, u32[]{:S(2)}, u32[]{:S(2)}) %collective-permute-start.1) | collective-permute-done | bytes 1048608 | tf_op jit(solution)/shard_map/ppermute | solution.py:102
  34.0 1.6 collective-permute-start.6
  36.4 3.9 %collective-permute-start.10 = (f32[256,16]{1,0:T(8,128)S(1)}, f32[256,16]{1,0:T(8,128)S(1)}, u32[]{:S(2)}, u32[]{:S(2)}) collective-permute-start(f32[256,16]{1,0:T(8,128)S(1)} %copy.16.refs_2_), channel_id=1, source_target_pairs={{0,12},{1,13},{2,14},{3,15},{4,0},{5,1},{6,2},{7,3},{8,4},{9,5},{1... | collective-permute-start | bytes 49160 | tf_op jit(solution)/shard_map/ppermute | solution.py:102
  40.9 10.9 %pair_rows.4 = (f32[128,2048]{1,0:T(8,128)}, bf16[128,2048]{1,0:T(8,128)(2,1)}) custom-call(s32[2]{0:T(128)} %pad_add_fusion.experts, bf16[128,4096]{1,0:T(8,128)(2,1)} %copy-done.4, bf16[128,4096]{1,0:T(8,128)(2,1)} %copy-done.7, f32[256,16]{1,0:T(8,128)} %copy-done.5, bf16[2048,512]{1,0:T(8,128)(2,1)} %bitcast.6, bf16[2048,512]{1,0:T(8,128)(2,1)} %bitcast.11, ...), custom_call_target="tpu_custom_call" | custom-call | flops 5368709120 | bytes 16252928 | tf_op jit(solution)/shard_map/pair_rows/pallas_call | solution.py:73
  51.7 13.3 %collective-permute-done.10.refs_2_ = f32[256,16]{1,0:T(8,128)S(1)} collective-permute-done((f32[256,16]{1,0:T(8,128)S(1)}, f32[256,16]{1,0:T(8,128)S(1)}, u32[]{:S(2)}, u32[]{:S(2)}) %collective-permute-start.10) | collective-permute-done | bytes 16416 | tf_op jit(solution)/shard_map/ppermute | solution.py:102
  65.0 3.6 %collective-permute-done.8.refs_2_ = f32[256,16]{1,0:T(8,128)S(1)} collective-permute-done((f32[256,16]{1,0:T(8,128)S(1)}, f32[256,16]{1,0:T(8,128)S(1)}, u32[]{:S(2)}, u32[]{:S(2)}) %collective-permute-start.8) | collective-permute-done | bytes 16416 | tf_op jit(solution)/shard_map/ppermute | solution.py:102
  68.6 3.4 %collective-permute-done.9.refs_2_ = f32[256,16]{1,0:T(8,128)S(1)} collective-permute-done((f32[256,16]{1,0:T(8,128)S(1)}, f32[256,16]{1,0:T(8,128)S(1)}, u32[]{:S(2)}, u32[]{:S(2)}) %collective-permute-start.9) | collective-permute-done | bytes 16416 | tf_op jit(solution)/shard_map/ppermute | solution.py:102
  72.0 1.6 collective-permute-start.12
  73.6 10.8 %pair_rows.5 = (f32[128,2048]{1,0:T(8,128)}, bf16[128,2048]{1,0:T(8,128)(2,1)}) custom-call(s32[2]{0:T(128)} %pad_add_fusion.experts, bf16[128,4096]{1,0:T(8,128)(2,1)} %collective-permute-done.1.refs_0_, bf16[128,4096]{1,0:T(8,128)(2,1)} %collective-permute-done.6.refs_1_, f32[256,16]{1,0:T(8,128)} %copy-done.12, bf16[2048,512]{1,0:T(8,128)(2,1)} %bitcast.7, ...), custom_call_target="tpu_custom_call" | custom-call | flops 5368709120 | bytes 16252928 | tf_op jit(solution)/shard_map/pair_rows/pallas_call | solution.py:73
  84.5 12.7 %collective-permute-done.12.refs_1_ = bf16[128,4096]{1,0:T(8,128)(2,1)S(1)} collective-permute-done((bf16[128,4096]{1,0:T(8,128)(2,1)}, bf16[128,4096]{1,0:T(8,128)(2,1)S(1)}, u32[]{:S(2)}, u32[]{:S(2)}) %collective-permute-start.12) | collective-permute-done | bytes 1048608 | tf_op jit(solution)/shard_map/ppermute | solution.py:105
  97.2 3.3 %collective-permute-done.13.refs_0_ = bf16[128,4096]{1,0:T(8,128)(2,1)S(1)} collective-permute-done((bf16[128,4096]{1,0:T(8,128)(2,1)}, bf16[128,4096]{1,0:T(8,128)(2,1)S(1)}, u32[]{:S(2)}, u32[]{:S(2)}) %collective-permute-start.13) | collective-permute-done | bytes 1048608 | tf_op jit(solution)/shard_map/ppermute | solution.py:102
  100.9 1.5 collective-permute-start.11
  103.0 10.9 %pair_rows.6 = (f32[128,2048]{1,0:T(8,128)}, bf16[128,2048]{1,0:T(8,128)(2,1)}) custom-call(s32[2]{0:T(128)} %pad_add_fusion.experts, bf16[128,4096]{1,0:T(8,128)(2,1)} %collective-permute-done.7.refs_0_, bf16[128,4096]{1,0:T(8,128)(2,1)} %copy-done.9, f32[256,16]{1,0:T(8,128)} %copy-done.11, bf16[2048,512]{1,0:T(8,128)(2,1)} %bitcast.8, ...), custom_call_target="tpu_custom_call" | custom-call | flops 5368709120 | bytes 16252928 | tf_op jit(solution)/shard_map/pair_rows/pallas_call | solution.py:73
  113.9 1.6 collective-permute-start.17
  115.4 11.2 %collective-permute-done.16.refs_1_ = bf16[128,4096]{1,0:T(8,128)(2,1)} collective-permute-done((bf16[128,4096]{1,0:T(8,128)(2,1)S(1)}, bf16[128,4096]{1,0:T(8,128)(2,1)}, u32[]{:S(2)}, u32[]{:S(2)}) %collective-permute-start.16) | collective-permute-done | bytes 1048608 | tf_op jit(solution)/shard_map/ppermute | solution.py:105
  126.6 11.2 %pair_rows.7 = (f32[128,2048]{1,0:T(8,128)}, bf16[128,2048]{1,0:T(8,128)(2,1)}) custom-call(s32[2]{0:T(128)} %pad_add_fusion.experts, bf16[128,4096]{1,0:T(8,128)(2,1)} %copy-done.8, bf16[128,4096]{1,0:T(8,128)(2,1)} %collective-permute-done.16.refs_1_, f32[256,16]{1,0:T(8,128)} %copy-done.10, bf16[2048,512]{1,0:T(8,128)(2,1)} %bitcast.9, ...), custom_call_target="tpu_custom_call" | custom-call | flops 5368709120 | bytes 16252928 | tf_op jit(solution)/shard_map/pair_rows/pallas_call | solution.py:73
  138.5 10.5 %collective-permute-done.14 = bf16[128,2048]{1,0:T(8,128)(2,1)S(1)} collective-permute-done((bf16[128,2048]{1,0:T(8,128)(2,1)}, bf16[128,2048]{1,0:T(8,128)(2,1)S(1)}, u32[]{:S(2)}, u32[]{:S(2)}) %collective-permute-start.14) | collective-permute-done | bytes 524320 | tf_op jit(solution)/shard_map/ppermute | solution.py:105
  149.2 11.0 %collective-permute-done.17 = bf16[128,2048]{1,0:T(8,128)(2,1)S(1)} collective-permute-done((bf16[128,2048]{1,0:T(8,128)(2,1)}, bf16[128,2048]{1,0:T(8,128)(2,1)S(1)}, u32[]{:S(2)}, u32[]{:S(2)}) %collective-permute-start.17) | collective-permute-done | bytes 524320 | tf_op jit(solution)/shard_map/ppermute | solution.py:105
  160.4 8.8 %collective-permute-done.19 = bf16[128,2048]{1,0:T(8,128)(2,1)S(1)} collective-permute-done((bf16[128,2048]{1,0:T(8,128)(2,1)}, bf16[128,2048]{1,0:T(8,128)(2,1)S(1)}, u32[]{:S(2)}, u32[]{:S(2)}) %collective-permute-start.19) | collective-permute-done | bytes 524320 | tf_op jit(solution)/shard_map/ppermute | solution.py:105
  169.5 22.4 %collective-permute-done.18 = bf16[128,2048]{1,0:T(8,128)(2,1)S(1)} collective-permute-done((bf16[128,2048]{1,0:T(8,128)(2,1)S(1)}, bf16[128,2048]{1,0:T(8,128)(2,1)S(1)}, u32[]{:S(2)}, u32[]{:S(2)}) %collective-permute-start.18) | collective-permute-done | bytes 524320 | tf_op jit(solution)/shard_map/ppermute | solution.py:102
  191.9 1.4 convert_add_fusion
  (58 shorter events, 7.5 us)
Async XLA Ops:
  0.0 34.0 %collective-permute-start.2 = (bf16[2048,512]{1,0:T(8,128)(2,1)}, bf16[2048,512]{1,0:T(8,128)(2,1)S(1)}, u32[]{:S(2)}, u32[]{:S(2)}) collective-permute-start(bf16[2048,512]{1,0:T(8,128)(2,1)} %bitcast.5), channel_id=1, source_target_pairs={{0,1},{1,0},{2,3},{3,2},{4,5},{5,4},{6,7},{7,6},{8,9},{9,8},{10,11... | collective-permute-start | bytes 6291464 | tf_op jit(solution)/shard_map/ppermute | solution.py:105
  0.5 33.5 %collective-permute-start.3 = (bf16[2048,512]{1,0:T(8,128)(2,1)}, bf16[2048,512]{1,0:T(8,128)(2,1)}, u32[]{:S(2)}, u32[]{:S(2)}) collective-permute-start(bf16[2048,512]{1,0:T(8,128)(2,1)} %bitcast.10), channel_id=1, source_target_pairs={{0,1},{1,0},{2,3},{3,2},{4,5},{5,4},{6,7},{7,6},{8,9},{9,8},{10,11... | collective-permute-start | bytes 6291464 | tf_op jit(solution)/shard_map/ppermute | solution.py:105
  0.5 33.5 %collective-permute-start.4 = (bf16[512,2048]{1,0:T(8,128)(2,1)}, bf16[512,2048]{1,0:T(8,128)(2,1)}, u32[]{:S(2)}, u32[]{:S(2)}) collective-permute-start(bf16[512,2048]{1,0:T(8,128)(2,1)} %bitcast.15), channel_id=1, source_target_pairs={{0,1},{1,0},{2,3},{3,2},{4,5},{5,4},{6,7},{7,6},{8,9},{9,8},{10,11... | collective-permute-start | bytes 6291464 | tf_op jit(solution)/shard_map/ppermute | solution.py:105
  1.7 4.8 %collective-permute-start.5 = (f32[128,16]{0,1:T(8,128)S(1)}, f32[128,16]{0,1:T(8,128)S(1)}, u32[]{:S(2)}, u32[]{:S(2)}) collective-permute-start(f32[128,16]{0,1:T(8,128)S(1)} %select_reduce_fusion), channel_id=1, source_target_pairs={{0,2},{1,3},{2,0},{3,1},{4,6},{5,7},{6,4},{7,5},{8,10},{9,11},{10,... | collective-permute-start | bytes 24584 | tf_op jit(solution)/shard_map/ppermute | solution.py:105
  6.4 34.4 %copy-start.4 = (bf16[128,4096]{1,0:T(8,128)(2,1)}, bf16[128,4096]{1,0:T(8,128)(2,1)S(1)}, u32[]{:S(2)}) copy-start(bf16[128,4096]{1,0:T(8,128)(2,1)S(1)} %constant_dynamic-update-slice_fusion.refs_0_) | copy-start | bytes 3145732
  6.4 25.4 %collective-permute-start = (bf16[128,4096]{1,0:T(8,128)(2,1)S(1)}, bf16[128,4096]{1,0:T(8,128)(2,1)S(1)}, u32[]{:S(2)}, u32[]{:S(2)}) collective-permute-start(bf16[128,4096]{1,0:T(8,128)(2,1)S(1)} %constant_dynamic-update-slice_fusion.refs_0_), channel_id=1, source_target_pairs={{0,2},{1,3},{2,0},{3,1},{4,6},{5,7},{6,4},{7,5},{8,10},{9,11},{10,... | collective-permute-start | bytes 3145736 | tf_op jit(solution)/shard_map/ppermute | solution.py:105
  6.5 27.5 %collective-permute-start.1 = (bf16[128,4096]{1,0:T(8,128)(2,1)S(1)}, bf16[128,4096]{1,0:T(8,128)(2,1)}, u32[]{:S(2)}, u32[]{:S(2)}) collective-permute-start(bf16[128,4096]{1,0:T(8,128)(2,1)S(1)} %constant_dynamic-update-slice_fusion.refs_0_), channel_id=1, source_target_pairs={{0,4},{1,5},{2,6},{3,7},{4,8},{5,9},{6,10},{7,11},{8,12},{9,13},{1... | collective-permute-start | bytes 3145736 | tf_op jit(solution)/shard_map/ppermute | solution.py:102
  34.0 38.0 %collective-permute-start.6 = (bf16[128,4096]{1,0:T(8,128)(2,1)}, bf16[128,4096]{1,0:T(8,128)(2,1)}, u32[]{:S(2)}, u32[]{:S(2)}) collective-permute-start(bf16[128,4096]{1,0:T(8,128)(2,1)} %collective-permute-done.1.refs_0_), channel_id=1, source_target_pairs={{0,2},{1,3},{2,0},{3,1},{4,6},{5,7},{6,4},{7,5},{8,10},{9,11},{10,... | collective-permute-start | bytes 3145736 | tf_op jit(solution)/shard_map/ppermute | solution.py:105
  35.6 36.4 %collective-permute-start.7 = (bf16[128,4096]{1,0:T(8,128)(2,1)}, bf16[128,4096]{1,0:T(8,128)(2,1)}, u32[]{:S(2)}, u32[]{:S(2)}) collective-permute-start(bf16[128,4096]{1,0:T(8,128)(2,1)} %collective-permute-done.1.refs_0_), channel_id=1, source_target_pairs={{0,4},{1,5},{2,6},{3,7},{4,8},{5,9},{6,10},{7,11},{8,12},{9,13},{1... | collective-permute-start | bytes 3145736 | tf_op jit(solution)/shard_map/ppermute | solution.py:102
  36.4 28.6 %collective-permute-start.10 = (f32[256,16]{1,0:T(8,128)S(1)}, f32[256,16]{1,0:T(8,128)S(1)}, u32[]{:S(2)}, u32[]{:S(2)}) collective-permute-start(f32[256,16]{1,0:T(8,128)S(1)} %copy.16.refs_2_), channel_id=1, source_target_pairs={{0,12},{1,13},{2,14},{3,15},{4,0},{5,1},{6,2},{7,3},{8,4},{9,5},{1... | collective-permute-start | bytes 49160 | tf_op jit(solution)/shard_map/ppermute | solution.py:102
  40.2 28.4 %collective-permute-start.8 = (f32[256,16]{1,0:T(8,128)S(1)}, f32[256,16]{1,0:T(8,128)S(1)}, u32[]{:S(2)}, u32[]{:S(2)}) collective-permute-start(f32[256,16]{1,0:T(8,128)S(1)} %copy.16.refs_2_), channel_id=1, source_target_pairs={{0,4},{1,5},{2,6},{3,7},{4,8},{5,9},{6,10},{7,11},{8,12},{9,13},{1... | collective-permute-start | bytes 49160 | tf_op jit(solution)/shard_map/ppermute | solution.py:102
  40.2 31.8 %collective-permute-start.9 = (f32[256,16]{1,0:T(8,128)S(1)}, f32[256,16]{1,0:T(8,128)S(1)}, u32[]{:S(2)}, u32[]{:S(2)}) collective-permute-start(f32[256,16]{1,0:T(8,128)S(1)} %copy.16.refs_2_), channel_id=1, source_target_pairs={{0,8},{1,9},{2,10},{3,11},{4,12},{5,13},{6,14},{7,15},{8,0},{9,1},... | collective-permute-start | bytes 49160 | tf_op jit(solution)/shard_map/ppermute | solution.py:102
  72.0 25.1 %collective-permute-start.12 = (bf16[128,4096]{1,0:T(8,128)(2,1)}, bf16[128,4096]{1,0:T(8,128)(2,1)S(1)}, u32[]{:S(2)}, u32[]{:S(2)}) collective-permute-start(bf16[128,4096]{1,0:T(8,128)(2,1)} %collective-permute-done.7.refs_0_), channel_id=1, source_target_pairs={{0,2},{1,3},{2,0},{3,1},{4,6},{5,7},{6,4},{7,5},{8,10},{9,11},{10,... | collective-permute-start | bytes 3145736 | tf_op jit(solution)/shard_map/ppermute | solution.py:105
  73.6 26.8 %collective-permute-start.13 = (bf16[128,4096]{1,0:T(8,128)(2,1)}, bf16[128,4096]{1,0:T(8,128)(2,1)S(1)}, u32[]{:S(2)}, u32[]{:S(2)}) collective-permute-start(bf16[128,4096]{1,0:T(8,128)(2,1)} %collective-permute-done.7.refs_0_), channel_id=1, source_target_pairs={{0,4},{1,5},{2,6},{3,7},{4,8},{5,9},{6,10},{7,11},{8,12},{9,13},{1... | collective-permute-start | bytes 3145736 | tf_op jit(solution)/shard_map/ppermute | solution.py:102
  100.4 26.2 %collective-permute-start.16 = (bf16[128,4096]{1,0:T(8,128)(2,1)S(1)}, bf16[128,4096]{1,0:T(8,128)(2,1)}, u32[]{:S(2)}, u32[]{:S(2)}) collective-permute-start(bf16[128,4096]{1,0:T(8,128)(2,1)S(1)} %collective-permute-done.13.refs_0_), channel_id=1, source_target_pairs={{0,2},{1,3},{2,0},{3,1},{4,6},{5,7},{6,4},{7,5},{8,10},{9,11},{10,... | collective-permute-start | bytes 3145736 | tf_op jit(solution)/shard_map/ppermute | solution.py:105
  100.9 68.5 %collective-permute-start.11 = (bf16[128,2048]{1,0:T(8,128)(2,1)}, bf16[128,2048]{1,0:T(8,128)(2,1)S(1)}, u32[]{:S(2)}, u32[]{:S(2)}) collective-permute-start(bf16[128,2048]{1,0:T(8,128)(2,1)} %get-tuple-element.47), channel_id=1, source_target_pairs={{0,2},{1,3},{2,0},{3,1},{4,6},{5,7},{6,4},{7,5},{8,10},{9,11},{10,... | collective-permute-start | bytes 1572872 | tf_op jit(solution)/shard_map/ppermute | solution.py:105
  102.4 46.5 %collective-permute-start.14 = (bf16[128,2048]{1,0:T(8,128)(2,1)}, bf16[128,2048]{1,0:T(8,128)(2,1)S(1)}, u32[]{:S(2)}, u32[]{:S(2)}) collective-permute-start(bf16[128,2048]{1,0:T(8,128)(2,1)} %get-tuple-element.55), channel_id=1, source_target_pairs={{0,2},{1,3},{2,0},{3,1},{4,6},{5,7},{6,4},{7,5},{8,10},{9,11},{10,... | collective-permute-start | bytes 1572872 | tf_op jit(solution)/shard_map/ppermute | solution.py:105
  113.9 46.4 %collective-permute-start.17 = (bf16[128,2048]{1,0:T(8,128)(2,1)}, bf16[128,2048]{1,0:T(8,128)(2,1)S(1)}, u32[]{:S(2)}, u32[]{:S(2)}) collective-permute-start(bf16[128,2048]{1,0:T(8,128)(2,1)} %get-tuple-element.62), channel_id=1, source_target_pairs={{0,2},{1,3},{2,0},{3,1},{4,6},{5,7},{6,4},{7,5},{8,10},{9,11},{10,... | collective-permute-start | bytes 1572872 | tf_op jit(solution)/shard_map/ppermute | solution.py:105
  137.9 31.4 %copy-start.2 = (f32[128,2048]{1,0:T(8,128)S(1)}, f32[128,2048]{1,0:T(8,128)}, u32[]{:S(2)}) copy-start(f32[128,2048]{1,0:T(8,128)} %get-tuple-element.65) | copy-start | bytes 3145732
  137.9 31.4 %collective-permute-start.19 = (bf16[128,2048]{1,0:T(8,128)(2,1)}, bf16[128,2048]{1,0:T(8,128)(2,1)S(1)}, u32[]{:S(2)}, u32[]{:S(2)}) collective-permute-start(bf16[128,2048]{1,0:T(8,128)(2,1)} %get-tuple-element.66), channel_id=1, source_target_pairs={{0,2},{1,3},{2,0},{3,1},{4,6},{5,7},{6,4},{7,5},{8,10},{9,11},{10,... | collective-permute-start | bytes 1572872 | tf_op jit(solution)/shard_map/ppermute | solution.py:105
  149.1 42.8 %copy-start.3 = (f32[128,2048]{1,0:T(8,128)S(1)}, f32[128,2048]{1,0:T(8,128)}, u32[]{:S(2)}) copy-start(f32[128,2048]{1,0:T(8,128)} %get-tuple-element.46) | copy-start | bytes 3145732
  149.1 20.3 %collective-permute-start.15 = (bf16[128,2048]{1,0:T(8,128)(2,1)S(1)}, bf16[128,2048]{1,0:T(8,128)(2,1)S(1)}, u32[]{:S(2)}, u32[]{:S(2)}) collective-permute-start(bf16[128,2048]{1,0:T(8,128)(2,1)S(1)} %add_convert_fusion.2), channel_id=1, source_target_pairs={{0,12},{1,13},{2,14},{3,15},{4,0},{5,1},{6,2},{7,3},{8,4},{9,5},{1... | collective-permute-start | bytes 1572872 | tf_op jit(solution)/shard_map/ppermute | solution.py:102
  160.3 31.6 %collective-permute-start.18 = (bf16[128,2048]{1,0:T(8,128)(2,1)S(1)}, bf16[128,2048]{1,0:T(8,128)(2,1)S(1)}, u32[]{:S(2)}, u32[]{:S(2)}) collective-permute-start(bf16[128,2048]{1,0:T(8,128)(2,1)S(1)} %add_convert_fusion.1), channel_id=1, source_target_pairs={{0,8},{1,9},{2,10},{3,11},{4,12},{5,13},{6,14},{7,15},{8,0},{9,1},... | collective-permute-start | bytes 1572872 | tf_op jit(solution)/shard_map/ppermute | solution.py:102
  169.4 22.5 %collective-permute-start.20 = (bf16[128,2048]{1,0:T(8,128)(2,1)S(1)}, bf16[128,2048]{1,0:T(8,128)(2,1)S(1)}, u32[]{:S(2)}, u32[]{:S(2)}) collective-permute-start(bf16[128,2048]{1,0:T(8,128)(2,1)S(1)} %add_convert_fusion), channel_id=1, source_target_pairs={{0,4},{1,5},{2,6},{3,7},{4,8},{5,9},{6,10},{7,11},{8,12},{9,13},{1... | collective-permute-start | bytes 1572872 | tf_op jit(solution)/shard_map/ppermute | solution.py:102
  (10 other events, 112.9 us)

commit v3 on v1

--- a/solution.py
+++ b/solution.py
@@ -12,12 +12,11 @@
 LAST = (((1,), (1,)), ((), ()))
 
 
-def pair_kernel(blocks, first, wide, order, *refs):
+def pair_kernel(blocks, owners, wide, experts, *refs):
     xs, gs = refs[:blocks], refs[blocks : 2 * blocks]
-    gates = refs[2 * blocks]
-    weights = refs[2 * blocks + 1 : 2 * blocks + 7]
-    outs = refs[2 * blocks + 7 : 3 * blocks + 7]
-    x_buf, g_buf, w_in, w_out, d_buf, sems = refs[3 * blocks + 7 :]
+    weights = refs[2 * blocks : 2 * blocks + 6]
+    outs = refs[2 * blocks + 6 : 3 * blocks + 6]
+    x_buf, g_buf, w_in, w_out, d_buf, sems = refs[3 * blocks + 6 :]
     rows = xs[0].shape[0]
     width, hidden = weights[0].shape
     copies = {}
@@ -47,14 +46,15 @@
         if k == 0:
             for i in range(blocks):
                 copies["g", i].wait()
+            pieces = g_buf[:, width:].astype(F32)
+            lane = lax.broadcasted_iota(jnp.int32, pieces.shape, 1)
+        chosen = (lane == experts[k]) | (lane == experts[k] + owners) | (lane == experts[k] + 2 * owners)
+        gate = jnp.sum(jnp.where(chosen, pieces, 0.0), axis=1, keepdims=True)
+        scaled = (gate * g_buf[:, :width].astype(F32)).astype(BF16)
         copies["w", 3 * k + 2].wait()
         back = lax.dot_general(
-            g_buf[...], w_out[k * hidden : (k + 1) * hidden, :], LAST, preferred_element_type=F32
+            scaled, w_out[k * hidden : (k + 1) * hidden, :], LAST, preferred_element_type=F32
         )
-        gate = [
-            gates[pl.ds(pl.multiple_of(order[first + i] * rows, rows), rows), k : k + 1] for i in range(blocks)
-        ]
-        back = back * jnp.concatenate(gate, axis=0)
         sig = jax.nn.sigmoid(pre_gate)
         back_sig = back * sig
         d_buf[:, at : at + hidden] = (back_sig * pre_up * (1.0 + pre_gate * (1.0 - sig))).astype(BF16)
@@ -65,34 +65,34 @@
             out[:, c : c + wide] = term[i * rows : (i + 1) * rows, :].astype(out.dtype)
 
 
-def pair_rows(xs, gs, gates, order, first, weights, kinds):
+def pair_rows(xs, gs, owners, experts, weights, kinds):
     blocks = len(xs)
     rows, width = xs[0].shape
     hidden = weights[0].shape[1]
-    there = pl.BlockSpec(memory_space=pl.ANY)
+    there = pl.BlockSpec(memory_space=pltpu.HBM)
     near = pl.BlockSpec(memory_space=pltpu.VMEM)
     count = blocks * rows
     return pl.pallas_call(
-        partial(pair_kernel, blocks, first, 512 if width % 512 == 0 else width),
-        in_specs=[pl.BlockSpec(memory_space=pltpu.SMEM)] + [there] * (2 * blocks) + [near] + [there] * 6,
+        partial(pair_kernel, blocks, owners, 512 if width % 512 == 0 else width),
+        in_specs=[pl.BlockSpec(memory_space=pltpu.SMEM)] + [there] * (2 * blocks + 6),
         out_specs=[near] * blocks,
         out_shape=[jax.ShapeDtypeStruct((rows, width), kind) for kind in kinds],
         scratch_shapes=[
             pltpu.VMEM((count, width), BF16),
-            pltpu.VMEM((count, width), BF16),
+            pltpu.VMEM((count, gs[0].shape[1]), BF16),
             pltpu.VMEM((width, 4 * hidden), BF16),
             pltpu.VMEM((2 * hidden, width), BF16),
             pltpu.VMEM((count, 4 * hidden), BF16),
             pltpu.SemaphoreType.DMA((2 * blocks + 6,)),
         ],
-        compiler_params=pltpu.CompilerParams(vmem_limit_bytes=40 * 2**20),
+        compiler_params=pltpu.CompilerParams(vmem_limit_bytes=60 * 2**20),
         cost_estimate=pl.CostEstimate(
             flops=20 * count * width * hidden,
             bytes_accessed=12 * width * hidden + 7 * count * width,
             transcendentals=2 * count * hidden,
         ),
         name="pair_rows",
-    )(order, *xs, *gs, gates, *weights)
+    )(experts, *xs, *gs, *weights)
 
 
 def gathered(layer_input, out_grad, expert_ids, gates, w_gate, w_up, w_down):
@@ -100,8 +100,7 @@
     ring = owners // 4
     rows = layer_input.shape[0]
     me = lax.axis_index("expert")
-    core, chip = me % 2, me // 2
-    y, z = chip % 2, chip // 2
+    experts = jnp.stack([me, me ^ 1]).astype(jnp.int32)
 
     def turn(value, by):
         return lax.ppermute(value, "expert", [(i, (i + 4 * by) % owners) for i in range(owners)])
@@ -109,29 +108,71 @@
     def swap(value, bit):
         return lax.ppermute(value, "expert", [(i, i ^ bit) for i in range(owners)])
 
+    named = expert_ids[:, :, None] == jnp.arange(owners, dtype=jnp.int32)[None, None, :]
+    rest = jnp.sum(jnp.where(named, gates[:, :, None], 0.0), axis=1)
+    parts = []
+    for _ in range(3):
+        part = lax.reduce_precision(rest, 8, 7)
+        rest = rest - part
+        parts.append(part.astype(BF16))
+    spare = jnp.zeros((rows, -3 * owners % 128), BF16)
+
     own = (w_gate[0], w_up[0], w_down[0])
     weights = own + tuple(swap(w, 1) for w in own)
 
-    named = expert_ids[:, :, None] == jnp.arange(owners, dtype=jnp.int32)[None, None, :]
-    dense = jnp.sum(jnp.where(named, gates[:, :, None], 0.0), axis=1)
-    every = lax.all_gather(dense, "expert", tiled=True)
-    pair = [jnp.sum(jnp.where(jnp.arange(owners)[None, :] == e, every, 0.0), axis=1) for e in (me, me ^ 1)]
-    gate_pair = jnp.stack(pair, axis=1)
-    zs = (z - jnp.arange(ring)) % ring
-    order = ((zs[:, None] * 2 + jnp.stack([y, 1 - y])[None, :]) * 2 + core).reshape(-1).astype(jnp.int32)
-
-    x_own, g_own = layer_input, out_grad
-    total = None
-    for s in range(ring):
-        if s:
-            x_own, g_own = turn(x_own, 1), turn(g_own, 1)
-        x_far, g_far = swap(x_own, 2), swap(g_own, 2)
-        near, far = pair_rows((x_own, x_far), (g_own, g_far), gate_pair, order, 2 * s, weights, (F32, BF16))
-        both = near + swap(far, 2).astype(F32)
-        if s:
-            both = turn(both.astype(BF16), -s).astype(F32)
-        total = both if total is None else total + both
-    return total
+    def rows_of(xs, gs, kinds=(F32, BF16)):
+        return pair_rows(xs, gs, owners, experts, weights, kinds)
+
+    xs, gs = [layer_input], [jnp.concatenate([out_grad, *parts, spare], axis=1)]
+    far_xs, far_gs, nears, fars = [], [], [], []
+    tie = lax.optimization_barrier
+
+    def compute(s):
+        near, far = rows_of((xs[s], far_xs[s]), (gs[s], far_gs[s]))
+        nears.append(near)
+        fars.append(swap(far, 2))
+
+    for s in range(ring - 1):
+        far_x, next_x = tie((swap(xs[s], 2), turn(xs[s], 1)))
+        far_g, next_g = swap(gs[s], 2), turn(gs[s], 1)
+        last_x = turn(far_xs[0], -1) if s and s == max(1, ring - 3) else None
+        last_g = turn(far_gs[0], -1) if s and s == ring - 2 else None
+        if s == 0:
+            far_g, next_g, weights = tie((far_g, next_g, weights))
+        else:
+            compute(s - 1)
+            if s < ring - 2:
+                far_g, next_g, nears[s - 1], last_x = tie((far_g, next_g, nears[s - 1], last_x))
+            else:
+                far_g, nears[s - 1], fars[: s - 1] = tie((far_g, nears[s - 1], fars[: s - 1]))
+        far_xs.append(far_x)
+        far_gs.append(far_g)
+        if s and s == ring - 2:
+            compute(s)
+            next_x, next_g, last_x, last_g, nears[s], fars[s - 1] = tie(
+                (next_x, next_g, last_x if last_x is not None else kept_x, last_g, nears[s], fars[s - 1])
+            )
+        xs.append(next_x)
+        gs.append(next_g)
+        kept_x = last_x
+    if ring == 1:
+        last_x, last_g = swap(xs[0], 2), swap(gs[0], 2)
+    elif ring == 2:
+        last_x, last_g = turn(far_xs[0], -1), turn(far_gs[0], -1)
+        compute(0)
+    far_xs.append(last_x)
+    far_gs.append(last_g)
+    compute(ring - 1)
+    sums = [near + far.astype(F32) for near, far in zip(nears, fars)]
+
+    total = sums[0]
+    carried = None
+    for s in range(ring - 2, 0, -1):
+        carried = sums[s] if carried is None else sums[s] + carried
+        carried = turn(carried.astype(BF16), -1).astype(F32)
+    if ring > 1:
+        total = total + turn(sums[ring - 1].astype(BF16), 1).astype(F32)
+    return total if carried is None else total + carried
 
 
 def expert_rows(rows_in, rows_grad, gate_w, up_w, down_w):

time: 222 us -> 159 us (0.72)
  waiting for transfers between devices: 121 us -> 85.7 us
  blocking collectives: 31.9 us -> 0 us
  local copies, waits for them, and re-layouts: 12.7 us -> 3.38 us
  Pallas kernels: 34.2 us -> 43.5 us
  starting transfers between devices: 19.2 us -> 22.9 us
    all_gather x1 -> x0, blocking collectives: 31.9 us -> none  [gathered(): every = lax.all_gather(dense, 'expert', tiled=True)]
    ppermute x15 -> x13, waiting for transfers between devices: 70.6 us -> 41.5 us  [swap(): return lax.ppermute(value, 'expert', [(i, i ^ bit) for i in range(owners)])]
    unnamed x38 -> x24, local copies, waits for them, and re-layouts: 12.3 us -> 1.87 us
    pallas_call x4, Pallas kernels: 34.2 us -> 43.5 us  [pair_rows(): pl.pallas_call(partial(pair_kernel, blocks, owners, 512 if width % 512 ==...]
    ppermute x9 -> x11, waiting for transfers between devices: 50.3 us -> 44.3 us  [turn(): lax.ppermute(value, 'expert', [(i, (i + 4 * by) % owners) for i in range(...]
    ppermute x9 -> x11, starting transfers between devices: 4.8 us -> 9.45 us  [turn(): lax.ppermute(value, 'expert', [(i, (i + 4 * by) % owners) for i in range(...]
    ppermute x15 -> x13, starting transfers between devices: 14.4 us -> 13.5 us  [swap(): return lax.ppermute(value, 'expert', [(i, i ^ bit) for i in range(owners)])]
  transfers between devices with their start and end apart: 24 -> 24, of which waited for: 15 -> 13; matrix products, arithmetic and copies ran while one was open for 1% -> 2% of each run, Pallas kernels for 15% -> 27%
where the time goes in v3:
time: 159 us
  waiting for transfers between devices  85.7 us (54%)
  Pallas kernels  43.5 us (27%)
  starting transfers between devices  22.9 us (14%)
  local copies, waits for them, and re-layouts  3.38 us (2%)
  other arithmetic  3.06 us (2%)
    ppermute x11, waiting for transfers between devices, turn(): lax.ppermute(value, 'expert', [(i, (i + 4 * by) % owners) for i in range(...  44.3 us
    pallas_call x4, Pallas kernels, pair_rows(): pl.pallas_call(partial(pair_kernel, blocks, owners, 512 if width % 512 ==...  43.5 us
    ppermute x13, waiting for transfers between devices, swap(): return lax.ppermute(value, 'expert', [(i, i ^ bit) for i in range(owners)])  41.5 us
    ppermute x13, starting transfers between devices, swap(): return lax.ppermute(value, 'expert', [(i, i ^ bit) for i in range(owners)])  13.5 us
    ppermute x11, starting transfers between devices, turn(): lax.ppermute(value, 'expert', [(i, (i + 4 * by) % owners) for i in range(...  9.45 us
  transfers between devices with their start and end apart: 24, of which 13 were waited for; matrix products, arithmetic and copies ran while one was open for 2% of the time, Pallas kernels for 27%

profile of v3, /device:TPU:0, one launch (start us, length us, event | category | flops | bytes accessed | tf_op | source)
XLA Modules:
  0.0 158.8 jit_solution(10607007350572960187)
XLA Ops:
  1.0 2.5 %collective-permute-start.7 = (bf16[128,2048]{1,0:T(8,128)(2,1)}, bf16[128,2048]{1,0:T(8,128)(2,1)}, u32[]{:S(2)}, u32[]{:S(2)}) collective-permute-start(bf16[128,2048]{1,0:T(8,128)(2,1)} %refs_0_.1), channel_id=1, source_target_pairs={{0,2},{1,3},{2,0},{3,1},{4,6},{5,7},{6,4},{7,5},{8,10},{9,11},{10,... | collective-permute-start | bytes 1572872 | tf_op jit(solution)/shard_map/ppermute | solution.py:109
  3.5 1.6 collective-permute-start.8
  6.2 1.2 concatenate.3.refs_2_
  7.3 9.0 %collective-permute-done.7.refs_1_ = bf16[128,2048]{1,0:T(8,128)(2,1)} collective-permute-done((bf16[128,2048]{1,0:T(8,128)(2,1)}, bf16[128,2048]{1,0:T(8,128)(2,1)}, u32[]{:S(2)}, u32[]{:S(2)}) %collective-permute-start.7) | collective-permute-done | bytes 524320 | tf_op jit(solution)/shard_map/ppermute | solution.py:109
  16.4 1.7 %collective-permute-start = (bf16[128,2176]{1,0:T(8,128)(2,1)S(1)}, bf16[128,2176]{1,0:T(8,128)(2,1)S(1)}, u32[]{:S(2)}, u32[]{:S(2)}) collective-permute-start(bf16[128,2176]{1,0:T(8,128)(2,1)S(1)} %concatenate.3.refs_2_), channel_id=1, source_target_pairs={{0,2},{1,3},{2,0},{3,1},{4,6},{5,7},{6,4},{7,5},{8,10},{9,11},{10,... | collective-permute-start | bytes 1671176 | tf_op jit(solution)/shard_map/ppermute | solution.py:109
  18.1 1.6 %collective-permute-done.8.refs_0_ = bf16[128,2048]{1,0:T(8,128)(2,1)} collective-permute-done((bf16[128,2048]{1,0:T(8,128)(2,1)}, bf16[128,2048]{1,0:T(8,128)(2,1)}, u32[]{:S(2)}, u32[]{:S(2)}) %collective-permute-start.8) | collective-permute-done | bytes 524320 | tf_op jit(solution)/shard_map/ppermute | solution.py:106
  19.7 11.1 %collective-permute-done.refs_3_ = bf16[128,2176]{1,0:T(8,128)(2,1)S(1)} collective-permute-done((bf16[128,2176]{1,0:T(8,128)(2,1)S(1)}, bf16[128,2176]{1,0:T(8,128)(2,1)S(1)}, u32[]{:S(2)}, u32[]{:S(2)}) %collective-permute-start) | collective-permute-done | bytes 557088 | tf_op jit(solution)/shard_map/ppermute | solution.py:109
  30.9 1.5 collective-permute-start.11
  32.4 3.3 %collective-permute-done.1.refs_2_ = bf16[128,2176]{1,0:T(8,128)(2,1)} collective-permute-done((bf16[128,2176]{1,0:T(8,128)(2,1)S(1)}, bf16[128,2176]{1,0:T(8,128)(2,1)}, u32[]{:S(2)}, u32[]{:S(2)}) %collective-permute-start.1) | collective-permute-done | bytes 557088 | tf_op jit(solution)/shard_map/ppermute | solution.py:106
  35.7 3.8 %collective-permute-start.9 = (bf16[128,2048]{1,0:T(8,128)(2,1)}, bf16[128,2048]{1,0:T(8,128)(2,1)}, u32[]{:S(2)}, u32[]{:S(2)}) collective-permute-start(bf16[128,2048]{1,0:T(8,128)(2,1)} %collective-permute-done.7.refs_1_), channel_id=1, source_target_pairs={{0,12},{1,13},{2,14},{3,15},{4,0},{5,1},{6,2},{7,3},{8,4},{9,5},{1... | collective-permute-start | bytes 1572872 | tf_op jit(solution)/shard_map/ppermute | solution.py:106
  40.9 5.1 %collective-permute-done.11.refs_1_ = bf16[128,2048]{1,0:T(8,128)(2,1)} collective-permute-done((bf16[128,2048]{1,0:T(8,128)(2,1)}, bf16[128,2048]{1,0:T(8,128)(2,1)}, u32[]{:S(2)}, u32[]{:S(2)}) %collective-permute-start.11) | collective-permute-done | bytes 524320 | tf_op jit(solution)/shard_map/ppermute | solution.py:109
  46.0 6.6 %collective-permute-done.12.refs_0_ = bf16[128,2048]{1,0:T(8,128)(2,1)} collective-permute-done((bf16[128,2048]{1,0:T(8,128)(2,1)}, bf16[128,2048]{1,0:T(8,128)(2,1)}, u32[]{:S(2)}, u32[]{:S(2)}) %collective-permute-start.12) | collective-permute-done | bytes 524320 | tf_op jit(solution)/shard_map/ppermute | solution.py:106
  53.4 10.8 %pair_rows.4 = (f32[128,2048]{1,0:T(8,128)}, bf16[128,2048]{1,0:T(8,128)(2,1)}) custom-call(s32[2]{0:T(128)} %pad_add_fusion.experts, bf16[128,2048]{1,0:T(8,128)(2,1)} %refs_0_.1, bf16[128,2048]{1,0:T(8,128)(2,1)} %collective-permute-done.7.refs_1_, bf16[128,2176]{1,0:T(8,128)(2,1)} %copy-done.4, bf16[128,2176]{1,0:T(8,128)(2,1)} %copy-done.6, ...), custom_call_target="tpu_custom_call" | custom-call | flops 5368709120 | bytes 16252928 | tf_op jit(solution)/shard_map/pair_rows/pallas_call | solution.py:75
  64.2 9.3 %collective-permute-done.6.refs_2_ = bf16[128,2176]{1,0:T(8,128)(2,1)} collective-permute-done((bf16[128,2176]{1,0:T(8,128)(2,1)}, bf16[128,2176]{1,0:T(8,128)(2,1)}, u32[]{:S(2)}, u32[]{:S(2)}) %collective-permute-start.6) | collective-permute-done | bytes 557088 | tf_op jit(solution)/shard_map/ppermute | solution.py:106
  75.5 3.8 %collective-permute-start.17 = (bf16[128,2176]{1,0:T(8,128)(2,1)S(1)}, bf16[128,2176]{1,0:T(8,128)(2,1)S(1)}, u32[]{:S(2)}, u32[]{:S(2)}) collective-permute-start(bf16[128,2176]{1,0:T(8,128)(2,1)S(1)} %copy-done.7), channel_id=1, source_target_pairs={{0,12},{1,13},{2,14},{3,15},{4,0},{5,1},{6,2},{7,3},{8,4},{9,5},{1... | collective-permute-start | bytes 1671176 | tf_op jit(solution)/shard_map/ppermute | solution.py:106
  79.3 10.8 %pair_rows.5 = (f32[128,2048]{1,0:T(8,128)}, bf16[128,2048]{1,0:T(8,128)(2,1)}) custom-call(s32[2]{0:T(128)} %pad_add_fusion.experts, bf16[128,2048]{1,0:T(8,128)(2,1)} %collective-permute-done.8.refs_0_, bf16[128,2048]{1,0:T(8,128)(2,1)} %collective-permute-done.11.refs_1_, bf16[128,2176]{1,0:T(8,128)(2,1)} %collective-permute-done.1.refs_2_, ...), custom_call_target="tpu_custom_call" | custom-call | flops 5368709120 | bytes 16252928 | tf_op jit(solution)/shard_map/pair_rows/pallas_call | solution.py:75
  93.2 7.3 %collective-permute-done.13 = bf16[128,2048]{1,0:T(8,128)(2,1)S(1)} collective-permute-done((bf16[128,2048]{1,0:T(8,128)(2,1)}, bf16[128,2048]{1,0:T(8,128)(2,1)S(1)}, u32[]{:S(2)}, u32[]{:S(2)}) %collective-permute-start.13) | collective-permute-done | bytes 524320 | tf_op jit(solution)/shard_map/ppermute | solution.py:109
  100.5 10.8 %pair_rows.6 = (f32[128,2048]{1,0:T(8,128)}, bf16[128,2048]{1,0:T(8,128)(2,1)}) custom-call(s32[2]{0:T(128)} %pad_add_fusion.experts, bf16[128,2048]{1,0:T(8,128)(2,1)} %collective-permute-done.12.refs_0_, bf16[128,2048]{1,0:T(8,128)(2,1)} %collective-permute-done.14.refs_1_, bf16[128,2176]{1,0:T(8,128)(2,1)} %collective-permute-done.6.refs_2_, ...), custom_call_target="tpu_custom_call" | custom-call | flops 5368709120 | bytes 16252928 | tf_op jit(solution)/shard_map/pair_rows/pallas_call | solution.py:75
  113.3 11.1 %pair_rows.7 = (f32[128,2048]{1,0:T(8,128)}, bf16[128,2048]{1,0:T(8,128)(2,1)}) custom-call(s32[2]{0:T(128)} %pad_add_fusion.experts, bf16[128,2048]{1,0:T(8,128)(2,1)} %copy-done.11, bf16[128,2048]{1,0:T(8,128)(2,1)} %collective-permute-done.9.refs_1_, bf16[128,2176]{1,0:T(8,128)(2,1)} %copy-done.10, bf16[128,2176]{1,0:T(8,128)(2,1)} %copy-done.9, ...), custom_call_target="tpu_custom_call" | custom-call | flops 5368709120 | bytes 16252928 | tf_op jit(solution)/shard_map/pair_rows/pallas_call | solution.py:75
  125.9 8.9 %collective-permute-done.19 = bf16[128,2048]{1,0:T(8,128)(2,1)S(1)} collective-permute-done((bf16[128,2048]{1,0:T(8,128)(2,1)}, bf16[128,2048]{1,0:T(8,128)(2,1)S(1)}, u32[]{:S(2)}, u32[]{:S(2)}) %collective-permute-start.19) | collective-permute-done | bytes 524320 | tf_op jit(solution)/shard_map/ppermute | solution.py:109
  135.0 9.8 %collective-permute-done.22 = bf16[128,2048]{1,0:T(8,128)(2,1)S(1)} collective-permute-done((bf16[128,2048]{1,0:T(8,128)(2,1)S(1)}, bf16[128,2048]{1,0:T(8,128)(2,1)S(1)}, u32[]{:S(2)}, u32[]{:S(2)}) %collective-permute-start.22) | collective-permute-done | bytes 524320 | tf_op jit(solution)/shard_map/ppermute | solution.py:106
  145.0 6.4 %collective-permute-done.20 = bf16[128,2048]{1,0:T(8,128)(2,1)S(1)} collective-permute-done((bf16[128,2048]{1,0:T(8,128)(2,1)S(1)}, bf16[128,2048]{1,0:T(8,128)(2,1)S(1)}, u32[]{:S(2)}, u32[]{:S(2)}) %collective-permute-start.20) | collective-permute-done | bytes 524320 | tf_op jit(solution)/shard_map/ppermute | solution.py:106
  151.5 6.0 %collective-permute-done.23 = bf16[128,2048]{1,0:T(8,128)(2,1)S(1)} collective-permute-done((bf16[128,2048]{1,0:T(8,128)(2,1)S(1)}, bf16[128,2048]{1,0:T(8,128)(2,1)S(1)}, u32[]{:S(2)}, u32[]{:S(2)}) %collective-permute-start.23) | collective-permute-done | bytes 524320 | tf_op jit(solution)/shard_map/ppermute | solution.py:106
  157.5 1.3 convert_add_fusion
  (65 shorter events, 13.1 us)
Async XLA Ops:
  0.0 35.7 %collective-permute-start.2 = (bf16[2048,512]{1,0:T(8,128)(2,1)}, bf16[2048,512]{1,0:T(8,128)(2,1)S(1)}, u32[]{:S(2)}, u32[]{:S(2)}) collective-permute-start(bf16[2048,512]{1,0:T(8,128)(2,1)} %bitcast.5), channel_id=1, source_target_pairs={{0,1},{1,0},{2,3},{3,2},{4,5},{5,4},{6,7},{7,6},{8,9},{9,8},{10,11... | collective-permute-start | bytes 6291464 | tf_op jit(solution)/shard_map/ppermute | solution.py:109
  0.5 39.1 %collective-permute-start.3 = (bf16[2048,512]{1,0:T(8,128)(2,1)}, bf16[2048,512]{1,0:T(8,128)(2,1)}, u32[]{:S(2)}, u32[]{:S(2)}) collective-permute-start(bf16[2048,512]{1,0:T(8,128)(2,1)} %bitcast.10), channel_id=1, source_target_pairs={{0,1},{1,0},{2,3},{3,2},{4,5},{5,4},{6,7},{7,6},{8,9},{9,8},{10,11... | collective-permute-start | bytes 6291464 | tf_op jit(solution)/shard_map/ppermute | solution.py:109
  0.5 39.0 %collective-permute-start.4 = (bf16[512,2048]{1,0:T(8,128)(2,1)}, bf16[512,2048]{1,0:T(8,128)(2,1)}, u32[]{:S(2)}, u32[]{:S(2)}) collective-permute-start(bf16[512,2048]{1,0:T(8,128)(2,1)} %bitcast.15), channel_id=1, source_target_pairs={{0,1},{1,0},{2,3},{3,2},{4,5},{5,4},{6,7},{7,6},{8,9},{9,8},{10,11... | collective-permute-start | bytes 6291464 | tf_op jit(solution)/shard_map/ppermute | solution.py:109
  1.0 15.4 %collective-permute-start.7 = (bf16[128,2048]{1,0:T(8,128)(2,1)}, bf16[128,2048]{1,0:T(8,128)(2,1)}, u32[]{:S(2)}, u32[]{:S(2)}) collective-permute-start(bf16[128,2048]{1,0:T(8,128)(2,1)} %refs_0_.1), channel_id=1, source_target_pairs={{0,2},{1,3},{2,0},{3,1},{4,6},{5,7},{6,4},{7,5},{8,10},{9,11},{10,... | collective-permute-start | bytes 1572872 | tf_op jit(solution)/shard_map/ppermute | solution.py:109
  3.5 16.3 %collective-permute-start.8 = (bf16[128,2048]{1,0:T(8,128)(2,1)}, bf16[128,2048]{1,0:T(8,128)(2,1)}, u32[]{:S(2)}, u32[]{:S(2)}) collective-permute-start(bf16[128,2048]{1,0:T(8,128)(2,1)} %refs_0_.1), channel_id=1, source_target_pairs={{0,4},{1,5},{2,6},{3,7},{4,8},{5,9},{6,10},{7,11},{8,12},{9,13},{1... | collective-permute-start | bytes 1572872 | tf_op jit(solution)/shard_map/ppermute | solution.py:106
  16.4 14.5 %collective-permute-start = (bf16[128,2176]{1,0:T(8,128)(2,1)S(1)}, bf16[128,2176]{1,0:T(8,128)(2,1)S(1)}, u32[]{:S(2)}, u32[]{:S(2)}) collective-permute-start(bf16[128,2176]{1,0:T(8,128)(2,1)S(1)} %concatenate.3.refs_2_), channel_id=1, source_target_pairs={{0,2},{1,3},{2,0},{3,1},{4,6},{5,7},{6,4},{7,5},{8,10},{9,11},{10,... | collective-permute-start | bytes 1671176 | tf_op jit(solution)/shard_map/ppermute | solution.py:109
  19.7 15.9 %collective-permute-start.1 = (bf16[128,2176]{1,0:T(8,128)(2,1)S(1)}, bf16[128,2176]{1,0:T(8,128)(2,1)}, u32[]{:S(2)}, u32[]{:S(2)}) collective-permute-start(bf16[128,2176]{1,0:T(8,128)(2,1)S(1)} %concatenate.3.refs_2_), channel_id=1, source_target_pairs={{0,4},{1,5},{2,6},{3,7},{4,8},{5,9},{6,10},{7,11},{8,12},{9,13},{1... | collective-permute-start | bytes 1671176 | tf_op jit(solution)/shard_map/ppermute | solution.py:106
  30.9 15.2 %collective-permute-start.11 = (bf16[128,2048]{1,0:T(8,128)(2,1)}, bf16[128,2048]{1,0:T(8,128)(2,1)}, u32[]{:S(2)}, u32[]{:S(2)}) collective-permute-start(bf16[128,2048]{1,0:T(8,128)(2,1)} %collective-permute-done.8.refs_0_), channel_id=1, source_target_pairs={{0,2},{1,3},{2,0},{3,1},{4,6},{5,7},{6,4},{7,5},{8,10},{9,11},{10,... | collective-permute-start | bytes 1572872 | tf_op jit(solution)/shard_map/ppermute | solution.py:109
  35.7 17.0 %collective-permute-start.12 = (bf16[128,2048]{1,0:T(8,128)(2,1)}, bf16[128,2048]{1,0:T(8,128)(2,1)}, u32[]{:S(2)}, u32[]{:S(2)}) collective-permute-start(bf16[128,2048]{1,0:T(8,128)(2,1)} %collective-permute-done.8.refs_0_), channel_id=1, source_target_pairs={{0,4},{1,5},{2,6},{3,7},{4,8},{5,9},{6,10},{7,11},{8,12},{9,13},{1... | collective-permute-start | bytes 1572872 | tf_op jit(solution)/shard_map/ppermute | solution.py:106
  35.7 28.5 %collective-permute-start.9 = (bf16[128,2048]{1,0:T(8,128)(2,1)}, bf16[128,2048]{1,0:T(8,128)(2,1)}, u32[]{:S(2)}, u32[]{:S(2)}) collective-permute-start(bf16[128,2048]{1,0:T(8,128)(2,1)} %collective-permute-done.7.refs_1_), channel_id=1, source_target_pairs={{0,12},{1,13},{2,14},{3,15},{4,0},{5,1},{6,2},{7,3},{8,4},{9,5},{1... | collective-permute-start | bytes 1572872 | tf_op jit(solution)/shard_map/ppermute | solution.py:106
  39.5 24.7 %collective-permute-start.5 = (bf16[128,2176]{1,0:T(8,128)(2,1)}, bf16[128,2176]{1,0:T(8,128)(2,1)S(1)}, u32[]{:S(2)}, u32[]{:S(2)}) collective-permute-start(bf16[128,2176]{1,0:T(8,128)(2,1)} %collective-permute-done.1.refs_2_), channel_id=1, source_target_pairs={{0,2},{1,3},{2,0},{3,1},{4,6},{5,7},{6,4},{7,5},{8,10},{9,11},{10,... | collective-permute-start | bytes 1671176 | tf_op jit(solution)/shard_map/ppermute | solution.py:109
  40.3 33.2 %collective-permute-start.6 = (bf16[128,2176]{1,0:T(8,128)(2,1)}, bf16[128,2176]{1,0:T(8,128)(2,1)}, u32[]{:S(2)}, u32[]{:S(2)}) collective-permute-start(bf16[128,2176]{1,0:T(8,128)(2,1)} %collective-permute-done.1.refs_2_), channel_id=1, source_target_pairs={{0,4},{1,5},{2,6},{3,7},{4,8},{5,9},{6,10},{7,11},{8,12},{9,13},{1... | collective-permute-start | bytes 1671176 | tf_op jit(solution)/shard_map/ppermute | solution.py:106
  52.7 26.6 %collective-permute-start.14 = (bf16[128,2048]{1,0:T(8,128)(2,1)}, bf16[128,2048]{1,0:T(8,128)(2,1)}, u32[]{:S(2)}, u32[]{:S(2)}) collective-permute-start(bf16[128,2048]{1,0:T(8,128)(2,1)} %collective-permute-done.12.refs_0_), channel_id=1, source_target_pairs={{0,2},{1,3},{2,0},{3,1},{4,6},{5,7},{6,4},{7,5},{8,10},{9,11},{10,... | collective-permute-start | bytes 1572872 | tf_op jit(solution)/shard_map/ppermute | solution.py:109
  73.5 27.0 %collective-permute-start.10 = (bf16[128,2176]{1,0:T(8,128)(2,1)}, bf16[128,2176]{1,0:T(8,128)(2,1)}, u32[]{:S(2)}, u32[]{:S(2)}) collective-permute-start(bf16[128,2176]{1,0:T(8,128)(2,1)} %collective-permute-done.6.refs_2_), channel_id=1, source_target_pairs={{0,2},{1,3},{2,0},{3,1},{4,6},{5,7},{6,4},{7,5},{8,10},{9,11},{10,... | collective-permute-start | bytes 1671176 | tf_op jit(solution)/shard_map/ppermute | solution.py:109
  74.4 16.9 %collective-permute-start.15 = (bf16[128,2048]{1,0:T(8,128)(2,1)}, bf16[128,2048]{1,0:T(8,128)(2,1)S(1)}, u32[]{:S(2)}, u32[]{:S(2)}) collective-permute-start(bf16[128,2048]{1,0:T(8,128)(2,1)} %collective-permute-done.12.refs_0_), channel_id=1, source_target_pairs={{0,4},{1,5},{2,6},{3,7},{4,8},{5,9},{6,10},{7,11},{8,12},{9,13},{1... | collective-permute-start | bytes 1572872 | tf_op jit(solution)/shard_map/ppermute | solution.py:106
  74.4 26.0 %collective-permute-start.13 = (bf16[128,2048]{1,0:T(8,128)(2,1)}, bf16[128,2048]{1,0:T(8,128)(2,1)S(1)}, u32[]{:S(2)}, u32[]{:S(2)}) collective-permute-start(bf16[128,2048]{1,0:T(8,128)(2,1)} %get-tuple-element.56), channel_id=1, source_target_pairs={{0,2},{1,3},{2,0},{3,1},{4,6},{5,7},{6,4},{7,5},{8,10},{9,11},{10,... | collective-permute-start | bytes 1572872 | tf_op jit(solution)/shard_map/ppermute | solution.py:109
  75.5 36.8 %collective-permute-start.17 = (bf16[128,2176]{1,0:T(8,128)(2,1)S(1)}, bf16[128,2176]{1,0:T(8,128)(2,1)S(1)}, u32[]{:S(2)}, u32[]{:S(2)}) collective-permute-start(bf16[128,2176]{1,0:T(8,128)(2,1)S(1)} %copy-done.7), channel_id=1, source_target_pairs={{0,12},{1,13},{2,14},{3,15},{4,0},{5,1},{6,2},{7,3},{8,4},{9,5},{1... | collective-permute-start | bytes 1671176 | tf_op jit(solution)/shard_map/ppermute | solution.py:106
  79.3 33.0 %collective-permute-start.16 = (bf16[128,2176]{1,0:T(8,128)(2,1)}, bf16[128,2176]{1,0:T(8,128)(2,1)S(1)}, u32[]{:S(2)}, u32[]{:S(2)}) collective-permute-start(bf16[128,2176]{1,0:T(8,128)(2,1)} %collective-permute-done.6.refs_2_), channel_id=1, source_target_pairs={{0,4},{1,5},{2,6},{3,7},{4,8},{5,9},{6,10},{7,11},{8,12},{9,13},{1... | collective-permute-start | bytes 1671176 | tf_op jit(solution)/shard_map/ppermute | solution.py:106
  92.1 20.2 %collective-permute-start.18 = (bf16[128,2048]{1,0:T(8,128)(2,1)}, bf16[128,2048]{1,0:T(8,128)(2,1)S(1)}, u32[]{:S(2)}, u32[]{:S(2)}) collective-permute-start(bf16[128,2048]{1,0:T(8,128)(2,1)} %get-tuple-element.64), channel_id=1, source_target_pairs={{0,2},{1,3},{2,0},{3,1},{4,6},{5,7},{6,4},{7,5},{8,10},{9,11},{10,... | collective-permute-start | bytes 1572872 | tf_op jit(solution)/shard_map/ppermute | solution.py:109
  111.3 14.4 %collective-permute-start.21 = (bf16[128,2048]{1,0:T(8,128)(2,1)}, bf16[128,2048]{1,0:T(8,128)(2,1)S(1)}, u32[]{:S(2)}, u32[]{:S(2)}) collective-permute-start(bf16[128,2048]{1,0:T(8,128)(2,1)} %get-tuple-element.74), channel_id=1, source_target_pairs={{0,2},{1,3},{2,0},{3,1},{4,6},{5,7},{6,4},{7,5},{8,10},{9,11},{10,... | collective-permute-start | bytes 1572872 | tf_op jit(solution)/shard_map/ppermute | solution.py:109
  124.5 10.3 %collective-permute-start.19 = (bf16[128,2048]{1,0:T(8,128)(2,1)}, bf16[128,2048]{1,0:T(8,128)(2,1)S(1)}, u32[]{:S(2)}, u32[]{:S(2)}) collective-permute-start(bf16[128,2048]{1,0:T(8,128)(2,1)} %get-tuple-element.70), channel_id=1, source_target_pairs={{0,2},{1,3},{2,0},{3,1},{4,6},{5,7},{6,4},{7,5},{8,10},{9,11},{10,... | collective-permute-start | bytes 1572872 | tf_op jit(solution)/shard_map/ppermute | solution.py:109
  125.8 19.0 %collective-permute-start.22 = (bf16[128,2048]{1,0:T(8,128)(2,1)S(1)}, bf16[128,2048]{1,0:T(8,128)(2,1)S(1)}, u32[]{:S(2)}, u32[]{:S(2)}) collective-permute-start(bf16[128,2048]{1,0:T(8,128)(2,1)S(1)} %add_convert_fusion.1), channel_id=1, source_target_pairs={{0,12},{1,13},{2,14},{3,15},{4,0},{5,1},{6,2},{7,3},{8,4},{9,5},{1... | collective-permute-start | bytes 1572872 | tf_op jit(solution)/shard_map/ppermute | solution.py:106
  134.9 16.6 %collective-permute-start.20 = (bf16[128,2048]{1,0:T(8,128)(2,1)S(1)}, bf16[128,2048]{1,0:T(8,128)(2,1)S(1)}, u32[]{:S(2)}, u32[]{:S(2)}) collective-permute-start(bf16[128,2048]{1,0:T(8,128)(2,1)S(1)} %add_convert_fusion.2), channel_id=1, source_target_pairs={{0,4},{1,5},{2,6},{3,7},{4,8},{5,9},{6,10},{7,11},{8,12},{9,13},{1... | collective-permute-start | bytes 1572872 | tf_op jit(solution)/shard_map/ppermute | solution.py:106
  145.0 12.5 %collective-permute-start.23 = (bf16[128,2048]{1,0:T(8,128)(2,1)S(1)}, bf16[128,2048]{1,0:T(8,128)(2,1)S(1)}, u32[]{:S(2)}, u32[]{:S(2)}) collective-permute-start(bf16[128,2048]{1,0:T(8,128)(2,1)S(1)} %add_convert_fusion), channel_id=1, source_target_pairs={{0,12},{1,13},{2,14},{3,15},{4,0},{5,1},{6,2},{7,3},{8,4},{9,5},{1... | collective-permute-start | bytes 1572872 | tf_op jit(solution)/shard_map/ppermute | solution.py:106
  (12 other events, 181.8 us)

commit v4 on v3

--- a/solution.py
+++ b/solution.py
@@ -74,7 +74,7 @@
     count = blocks * rows
     return pl.pallas_call(
         partial(pair_kernel, blocks, owners, 512 if width % 512 == 0 else width),
-        in_specs=[pl.BlockSpec(memory_space=pltpu.SMEM)] + [there] * (2 * blocks + 6),
+        in_specs=[pl.BlockSpec(memory_space=pltpu.SMEM)] + [there] * (2 * blocks) + [pl.BlockSpec(memory_space=pl.ANY)] * 6,
         out_specs=[near] * blocks,
         out_shape=[jax.ShapeDtypeStruct((rows, width), kind) for kind in kinds],
         scratch_shapes=[
@@ -85,7 +85,7 @@
             pltpu.VMEM((count, 4 * hidden), BF16),
             pltpu.SemaphoreType.DMA((2 * blocks + 6,)),
         ],
-        compiler_params=pltpu.CompilerParams(vmem_limit_bytes=60 * 2**20),
+        compiler_params=pltpu.CompilerParams(vmem_limit_bytes=36 * 2**20),
         cost_estimate=pl.CostEstimate(
             flops=20 * count * width * hidden,
             bytes_accessed=12 * width * hidden + 7 * count * width,
@@ -107,6 +107,8 @@
 
     def swap(value, bit):
         return lax.ppermute(value, "expert", [(i, i ^ bit) for i in range(owners)])
+
+    tie = lax.optimization_barrier
 
     named = expert_ids[:, :, None] == jnp.arange(owners, dtype=jnp.int32)[None, None, :]
     rest = jnp.sum(jnp.where(named, gates[:, :, None], 0.0), axis=1)
@@ -118,61 +120,56 @@
     spare = jnp.zeros((rows, -3 * owners % 128), BF16)
 
     own = (w_gate[0], w_up[0], w_down[0])
-    weights = own + tuple(swap(w, 1) for w in own)
-
-    def rows_of(xs, gs, kinds=(F32, BF16)):
-        return pair_rows(xs, gs, owners, experts, weights, kinds)
-
-    xs, gs = [layer_input], [jnp.concatenate([out_grad, *parts, spare], axis=1)]
+
+    x, g = tie((layer_input, jnp.concatenate([out_grad, *parts, spare], axis=1)))
+    xs, gs = [x], [g]
     far_xs, far_gs, nears, fars = [], [], [], []
-    tie = lax.optimization_barrier
 
     def compute(s):
-        near, far = rows_of((xs[s], far_xs[s]), (gs[s], far_gs[s]))
-        nears.append(near)
-        fars.append(swap(far, 2))
-
-    for s in range(ring - 1):
-        far_x, next_x = tie((swap(xs[s], 2), turn(xs[s], 1)))
-        far_g, next_g = swap(gs[s], 2), turn(gs[s], 1)
-        last_x = turn(far_xs[0], -1) if s and s == max(1, ring - 3) else None
-        last_g = turn(far_gs[0], -1) if s and s == ring - 2 else None
+        return pair_rows(
+            (xs[s], far_xs[s]), (gs[s], far_gs[s]), owners, experts, weights, (F32, BF16)
+        )
+
+    for s in range(ring - 2):
+        far_x, x, far_g, g = swap(xs[s], 2), turn(xs[s], 1), swap(gs[s], 2), turn(gs[s], 1)
         if s == 0:
-            far_g, next_g, weights = tie((far_g, next_g, weights))
+            theirs = [swap(own[0], 1)]
+            sent, far_x, x, theirs = tie((own[1:], far_x, x, theirs))
+            far_g, g, theirs = tie((far_g, g, theirs + [swap(w, 1) for w in sent]))
+            weights = (*own, *theirs)
         else:
-            compute(s - 1)
-            if s < ring - 2:
-                far_g, next_g, nears[s - 1], last_x = tie((far_g, next_g, nears[s - 1], last_x))
-            else:
-                far_g, nears[s - 1], fars[: s - 1] = tie((far_g, nears[s - 1], fars[: s - 1]))
-        far_xs.append(far_x)
-        far_gs.append(far_g)
-        if s and s == ring - 2:
-            compute(s)
-            next_x, next_g, last_x, last_g, nears[s], fars[s - 1] = tie(
-                (next_x, next_g, last_x if last_x is not None else kept_x, last_g, nears[s], fars[s - 1])
-            )
-        xs.append(next_x)
-        gs.append(next_g)
-        kept_x = last_x
-    if ring == 1:
-        last_x, last_g = swap(xs[0], 2), swap(gs[0], 2)
-    elif ring == 2:
-        last_x, last_g = turn(far_xs[0], -1), turn(far_gs[0], -1)
-        compute(0)
-    far_xs.append(last_x)
-    far_gs.append(last_g)
-    compute(ring - 1)
-    sums = [near + far.astype(F32) for near, far in zip(nears, fars)]
-
-    total = sums[0]
-    carried = None
-    for s in range(ring - 2, 0, -1):
-        carried = sums[s] if carried is None else sums[s] + carried
-        carried = turn(carried.astype(BF16), -1).astype(F32)
-    if ring > 1:
-        total = total + turn(sums[ring - 1].astype(BF16), 1).astype(F32)
-    return total if carried is None else total + carried
+            near, far = compute(s - 1)
+            far_x, x = tie((far_x, x))
+            far_g, g, near = tie((far_g, g, near))
+            nears.append(near)
+            fars.append(far)
+        xs, gs, far_xs, far_gs = xs + [x], gs + [g], far_xs + [far_x], far_gs + [far_g]
+
+    beyond_x, beyond_g = turn(far_xs[0], -1), turn(far_gs[0], -1)
+    x, beyond_x = tie((xs[-1], beyond_x))
+    x = turn(x, 1)
+    g, beyond_g = tie((gs[-1], beyond_g))
+    g = turn(g, 1)
+    near, far = compute(ring - 3)
+    far_x, far_g, near, beyond_x, beyond_g = tie((swap(xs[-1], 2), swap(gs[-1], 2), near, beyond_x, beyond_g))
+    far_xs, far_gs, nears, fars = far_xs + [far_x], far_gs + [far_g], nears + [near], fars + [far]
+    backs = [swap(far, 2) for far in fars[1:]]
+    near, far = compute(ring - 2)
+    near, far, beyond_x, x, backs = tie((near, far, beyond_x, x, backs))
+    (beyond,) = pair_rows((beyond_x,), (beyond_g,), owners, experts, weights, (BF16,))
+    sums = [None, *(near + back.astype(F32) for near, back in zip(nears[1:] + [near], backs + [swap(far, 2)]))]
+    one, carried = turn(sums[1].astype(BF16), -1), sums[2].astype(BF16)
+    x, g, first, carried, beyond = tie((x, g, fars[0], carried, beyond))
+    (last,) = pair_rows((x,), (g,), owners, experts, weights, (F32,))
+    last, one = tie((last, one))
+
+    for s in range(3, ring):
+        carried = turn(carried, 1).astype(F32)
+        if s < ring - 1:
+            carried = (sums[s] + carried).astype(BF16)
+    last = (last + swap(beyond, 2).astype(F32) + carried).astype(BF16)
+    total = nears[0] + swap(first, 2).astype(F32)
+    return total + turn(last, 1).astype(F32) + one.astype(F32)
 
 
 def expert_rows(rows_in, rows_grad, gate_w, up_w, down_w):
@@ -219,7 +216,7 @@
 
 def on_device(layer_input, out_grad, expert_ids, gates, w_gate, w_up, w_down):
     owners = lax.axis_size("expert")
-    dense = owners % 4 == 0 and expert_ids.shape[1] * 4 >= owners
+    dense = owners % 4 == 0 and owners >= 16 and expert_ids.shape[1] * 4 >= owners
     plan = gathered if dense else routed
     return plan(layer_input, out_grad, expert_ids, gates, w_gate, w_up, w_down)
 

time: 159 us -> 150 us (0.943)
  waiting for transfers between devices: 85.7 us -> 73 us
  local copies, waits for them, and re-layouts: 3.38 us -> 8.66 us
    ppermute x13, waiting for transfers between devices: 41.5 us -> 32.2 us  [swap(): return lax.ppermute(value, 'expert', [(i, i ^ bit) for i in range(owners)])]
    unnamed x24 -> x20, local copies, waits for them, and re-layouts: 1.87 us -> 7.15 us
    ppermute x11, waiting for transfers between devices: 44.3 us -> 40.8 us  [turn(): lax.ppermute(value, 'expert', [(i, (i + 4 * by) % owners) for i in range(...]
    ppermute x11, starting transfers between devices: 9.45 us -> 12.2 us  [turn(): lax.ppermute(value, 'expert', [(i, (i + 4 * by) % owners) for i in range(...]
    ppermute x13, starting transfers between devices: 13.5 us -> 10.7 us  [swap(): return lax.ppermute(value, 'expert', [(i, i ^ bit) for i in range(owners)])]
    pallas_call x4 -> x5, Pallas kernels: 43.5 us -> 42.6 us  [pair_rows(): pl.pallas_call(partial(pair_kernel, blocks, owners, 512 if width % 512 ==...]
  transfers between devices with their start and end apart: 24 -> 24, of which waited for: 13 -> 13; matrix products, arithmetic and copies ran while one was open for 2% -> 2% of each run, Pallas kernels for 27% -> 28%
where the time goes in v4:
time: 150 us
  waiting for transfers between devices  73 us (49%)
  Pallas kernels  42.6 us (28%)
  starting transfers between devices  23 us (15%)
  local copies, waits for them, and re-layouts  8.66 us (6%)
  other arithmetic  2.46 us (2%)
    pallas_call x5, Pallas kernels, pair_rows(): pl.pallas_call(partial(pair_kernel, blocks, owners, 512 if width % 512 ==...  42.6 us
    ppermute x11, waiting for transfers between devices, turn(): lax.ppermute(value, 'expert', [(i, (i + 4 * by) % owners) for i in range(...  40.8 us
    ppermute x13, waiting for transfers between devices, swap(): return lax.ppermute(value, 'expert', [(i, i ^ bit) for i in range(owners)])  32.2 us
    ppermute x11, starting transfers between devices, turn(): lax.ppermute(value, 'expert', [(i, (i + 4 * by) % owners) for i in range(...  12.2 us
    ppermute x13, starting transfers between devices, swap(): return lax.ppermute(value, 'expert', [(i, i ^ bit) for i in range(owners)])  10.7 us
    unnamed x20, local copies, waits for them, and re-layouts  7.15 us
  transfers between devices with their start and end apart: 24, of which 13 were waited for; matrix products, arithmetic and copies ran while one was open for 2% of the time, Pallas kernels for 28%

profile of v4, /device:TPU:0, one launch (start us, length us, event | category | flops | bytes accessed | tf_op | source)
XLA Modules:
  0.0 149.8 jit_solution(6519709768362838808)
XLA Ops:
  2.7 2.6 %collective-permute-start.2 = (bf16[128,2048]{1,0:T(8,128)(2,1)}, bf16[128,2048]{1,0:T(8,128)(2,1)S(1)}, u32[]{:S(2)}, u32[]{:S(2)}) collective-permute-start(bf16[128,2048]{1,0:T(8,128)(2,1)} %refs_0_), channel_id=1, source_target_pairs={{0,2},{1,3},{2,0},{3,1},{4,6},{5,7},{6,4},{7,5},{8,10},{9,11},{10,... | collective-permute-start | bytes 1572872 | tf_op jit(solution)/shard_map/ppermute | solution.py:109
  6.9 11.2 %collective-permute-done.2.refs_1_ = bf16[128,2048]{1,0:T(8,128)(2,1)S(1)} collective-permute-done((bf16[128,2048]{1,0:T(8,128)(2,1)}, bf16[128,2048]{1,0:T(8,128)(2,1)S(1)}, u32[]{:S(2)}, u32[]{:S(2)}) %collective-permute-start.2) | collective-permute-done | bytes 524320 | tf_op jit(solution)/shard_map/ppermute | solution.py:109
  18.1 3.3 %collective-permute-done.3.refs_0_ = bf16[128,2048]{1,0:T(8,128)(2,1)S(1)} collective-permute-done((bf16[128,2048]{1,0:T(8,128)(2,1)}, bf16[128,2048]{1,0:T(8,128)(2,1)S(1)}, u32[]{:S(2)}, u32[]{:S(2)}) %collective-permute-start.3) | collective-permute-done | bytes 524320 | tf_op jit(solution)/shard_map/ppermute | solution.py:106
  22.8 13.8 %collective-permute-done.refs_3_ = bf16[128,2176]{1,0:T(8,128)(2,1)S(1)} collective-permute-done((bf16[128,2176]{1,0:T(8,128)(2,1)S(1)}, bf16[128,2176]{1,0:T(8,128)(2,1)S(1)}, u32[]{:S(2)}, u32[]{:S(2)}) %collective-permute-start) | collective-permute-done | bytes 557088 | tf_op jit(solution)/shard_map/ppermute | solution.py:109
  36.6 2.1 %collective-permute-done.1.refs_2_ = bf16[128,2176]{1,0:T(8,128)(2,1)} collective-permute-done((bf16[128,2176]{1,0:T(8,128)(2,1)S(1)}, bf16[128,2176]{1,0:T(8,128)(2,1)}, u32[]{:S(2)}, u32[]{:S(2)}) %collective-permute-start.1) | collective-permute-done | bytes 557088 | tf_op jit(solution)/shard_map/ppermute | solution.py:106
  40.9 3.8 %collective-permute-start.13 = (bf16[128,2048]{1,0:T(8,128)(2,1)}, bf16[128,2048]{1,0:T(8,128)(2,1)S(1)}, u32[]{:S(2)}, u32[]{:S(2)}) collective-permute-start(bf16[128,2048]{1,0:T(8,128)(2,1)} %copy-done.8), channel_id=1, source_target_pairs={{0,12},{1,13},{2,14},{3,15},{4,0},{5,1},{6,2},{7,3},{8,4},{9,5},{1... | collective-permute-start | bytes 1572872 | tf_op jit(solution)/shard_map/ppermute | solution.py:106
  44.7 1.6 %copy-done = bf16[1,2048,512]{2,1,0:T(8,128)(2,1)S(1)} copy-done((bf16[1,2048,512]{2,1,0:T(8,128)(2,1)S(1)}, bf16[1,2048,512]{2,1,0:T(8,128)(2,1)}, u32[]{:S(2)}) %copy-start) | copy-done | bytes 2097176
  46.3 1.6 %copy-done.2 = bf16[1,2048,512]{2,1,0:T(8,128)(2,1)S(1)} copy-done((bf16[1,2048,512]{2,1,0:T(8,128)(2,1)S(1)}, bf16[1,2048,512]{2,1,0:T(8,128)(2,1)}, u32[]{:S(2)}) %copy-start.2) | copy-done | bytes 2097176
  51.6 8.9 %pair_rows.5 = (f32[128,2048]{1,0:T(8,128)S(1)}, bf16[128,2048]{1,0:T(8,128)(2,1)S(1)}) custom-call(s32[2]{0:T(128)S(1)} %pad_add_fusion.experts, bf16[128,2048]{1,0:T(8,128)(2,1)S(1)} %copy-done.5, bf16[128,2048]{1,0:T(8,128)(2,1)S(1)} %copy-done.9, bf16[128,2176]{1,0:T(8,128)(2,1)S(1)} %concatenate.3.refs_2_, ...), custom_call_target="tpu_custom_call" | custom-call | flops 5368709120 | bytes 16252928 | tf_op jit(solution)/shard_map/pair_rows/pallas_call | solution.py:75
  60.5 2.0 %collective-permute-start.14 = (bf16[128,2176]{1,0:T(8,128)(2,1)S(1)}, bf16[128,2176]{1,0:T(8,128)(2,1)S(1)}, u32[]{:S(2)}, u32[]{:S(2)}) collective-permute-start(bf16[128,2176]{1,0:T(8,128)(2,1)S(1)} %collective-permute-done.refs_3_), channel_id=1, source_target_pairs={{0,12},{1,13},{2,14},{3,15},{4,0},{5,1},{6,2},{7,3},{8,4},{9,5},{1... | collective-permute-start | bytes 1671176 | tf_op jit(solution)/shard_map/ppermute | solution.py:106
  64.0 5.1 %collective-permute-done.10.refs_0_ = bf16[128,2048]{1,0:T(8,128)(2,1)S(1)} collective-permute-done((bf16[128,2048]{1,0:T(8,128)(2,1)}, bf16[128,2048]{1,0:T(8,128)(2,1)S(1)}, u32[]{:S(2)}, u32[]{:S(2)}) %collective-permute-start.10) | collective-permute-done | bytes 524320 | tf_op jit(solution)/shard_map/ppermute | solution.py:106
  69.7 8.1 %collective-permute-done.13.refs_0_ = bf16[128,2048]{1,0:T(8,128)(2,1)S(1)} collective-permute-done((bf16[128,2048]{1,0:T(8,128)(2,1)}, bf16[128,2048]{1,0:T(8,128)(2,1)S(1)}, u32[]{:S(2)}, u32[]{:S(2)}) %collective-permute-start.13) | collective-permute-done | bytes 524320 | tf_op jit(solution)/shard_map/ppermute | solution.py:106
  78.2 8.8 %pair_rows.6 = (f32[128,2048]{1,0:T(8,128)S(1)}, bf16[128,2048]{1,0:T(8,128)(2,1)S(1)}) custom-call(s32[2]{0:T(128)S(1)} %pad_add_fusion.experts, bf16[128,2048]{1,0:T(8,128)(2,1)S(1)} %copy-done.7, bf16[128,2048]{1,0:T(8,128)(2,1)S(1)} %collective-permute-done.9.refs_1_, bf16[128,2176]{1,0:T(8,128)(2,1)} %collective-permute-done.1.refs_2_, ...), custom_call_target="tpu_custom_call" | custom-call | flops 5368709120 | bytes 16252928 | tf_op jit(solution)/shard_map/pair_rows/pallas_call | solution.py:75
  87.7 1.6 %collective-permute-done.14.refs_1_ = bf16[128,2176]{1,0:T(8,128)(2,1)S(1)} collective-permute-done((bf16[128,2176]{1,0:T(8,128)(2,1)S(1)}, bf16[128,2176]{1,0:T(8,128)(2,1)S(1)}, u32[]{:S(2)}, u32[]{:S(2)}) %collective-permute-start.14) | collective-permute-done | bytes 557088 | tf_op jit(solution)/shard_map/ppermute | solution.py:106
  89.3 3.4 %collective-permute-start.17 = (bf16[128,2176]{1,0:T(8,128)(2,1)S(1)}, bf16[128,2176]{1,0:T(8,128)(2,1)S(1)}, u32[]{:S(2)}, u32[]{:S(2)}) collective-permute-start(bf16[128,2176]{1,0:T(8,128)(2,1)S(1)} %collective-permute-done.8.refs_2_), channel_id=1, source_target_pairs={{0,4},{1,5},{2,6},{3,7},{4,8},{5,9},{6,10},{7,11},{8,12},{9,13},{1... | collective-permute-start | bytes 1671176 | tf_op jit(solution)/shard_map/ppermute | solution.py:106
  92.7 8.9 %pair_rows.7 = (f32[128,2048]{1,0:T(8,128)S(1)}, bf16[128,2048]{1,0:T(8,128)(2,1)S(1)}) custom-call(s32[2]{0:T(128)S(1)} %pad_add_fusion.experts, bf16[128,2048]{1,0:T(8,128)(2,1)S(1)} %collective-permute-done.10.refs_0_, bf16[128,2048]{1,0:T(8,128)(2,1)S(1)} %collective-permute-done.11.refs_1_, bf16[128,2176]{1,0:T(8,128)(2,1)S(1)} %collective-permute-done.8.refs_2_, ...), custom_call_target="tpu_custom_call" | custom-call | flops 5368709120 | bytes 16252928 | tf_op jit(solution)/shard_map/pair_rows/pallas_call | solution.py:75
  101.6 1.9 %collective-permute-done.15.refs_0_ = bf16[128,2048]{1,0:T(8,128)(2,1)S(1)} collective-permute-done((bf16[128,2048]{1,0:T(8,128)(2,1)S(1)}, bf16[128,2048]{1,0:T(8,128)(2,1)S(1)}, u32[]{:S(2)}, u32[]{:S(2)}) %collective-permute-start.15) | collective-permute-done | bytes 524320 | tf_op jit(solution)/shard_map/ppermute | solution.py:106
  105.0 8.1 %pair_rows.8 = bf16[128,2048]{1,0:T(8,128)(2,1)S(1)} custom-call(s32[2]{0:T(128)S(1)} %pad_add_fusion.experts, bf16[128,2048]{1,0:T(8,128)(2,1)S(1)} %collective-permute-done.13.refs_0_, bf16[128,2176]{1,0:T(8,128)(2,1)S(1)} %collective-permute-done.14.refs_1_, bf16[2048,512]{1,0:T(8,128)(2,1)S(1)} %bitcast.9, bf16[2048,512]{1,0:T(8,128)(2,1)S(1)} %bitcast.15, ...), custom_call_target="tpu_custom_call" | custom-call | flops 2684354560 | bytes 14417920 | tf_op jit(solution)/shard_map/pair_rows/pallas_call | solution.py:75
  113.1 2.3 %collective-permute-done.18 = bf16[128,2048]{1,0:T(8,128)(2,1)S(1)} collective-permute-done((bf16[128,2048]{1,0:T(8,128)(2,1)S(1)}, bf16[128,2048]{1,0:T(8,128)(2,1)S(1)}, u32[]{:S(2)}, u32[]{:S(2)}) %collective-permute-start.18) | collective-permute-done | bytes 524320 | tf_op jit(solution)/shard_map/ppermute | solution.py:109
  116.2 8.1 %pair_rows.9 = f32[128,2048]{1,0:T(8,128)S(1)} custom-call(s32[2]{0:T(128)S(1)} %pad_add_fusion.experts, bf16[128,2048]{1,0:T(8,128)(2,1)S(1)} %collective-permute-done.15.refs_0_, bf16[128,2176]{1,0:T(8,128)(2,1)S(1)} %collective-permute-done.17.refs_1_, bf16[2048,512]{1,0:T(8,128)(2,1)S(1)} %bitcast.10, bf16[2048,512]{1,0:T(8,128)(2,1)S(1)} %bitcast.16, ...), custom_call_target="tpu_custom_call" | custom-call | flops 2684354560 | bytes 14417920 | tf_op jit(solution)/shard_map/pair_rows/pallas_call | solution.py:75
  124.3 2.4 %collective-permute-done.20 = bf16[128,2048]{1,0:T(8,128)(2,1)S(1)} collective-permute-done((bf16[128,2048]{1,0:T(8,128)(2,1)S(1)}, bf16[128,2048]{1,0:T(8,128)(2,1)S(1)}, u32[]{:S(2)}, u32[]{:S(2)}) %collective-permute-start.20) | collective-permute-done | bytes 524320 | tf_op jit(solution)/shard_map/ppermute | solution.py:106
  127.2 8.0 %collective-permute-done.22 = bf16[128,2048]{1,0:T(8,128)(2,1)S(1)} collective-permute-done((bf16[128,2048]{1,0:T(8,128)(2,1)S(1)}, bf16[128,2048]{1,0:T(8,128)(2,1)S(1)}, u32[]{:S(2)}, u32[]{:S(2)}) %collective-permute-start.22) | collective-permute-done | bytes 524320 | tf_op jit(solution)/shard_map/ppermute | solution.py:106
  135.5 4.8 %collective-permute-done.19 = bf16[128,2048]{1,0:T(8,128)(2,1)S(1)} collective-permute-done((bf16[128,2048]{1,0:T(8,128)(2,1)S(1)}, bf16[128,2048]{1,0:T(8,128)(2,1)S(1)}, u32[]{:S(2)}, u32[]{:S(2)}) %collective-permute-start.19) | collective-permute-done | bytes 524320 | tf_op jit(solution)/shard_map/ppermute | solution.py:109
  140.3 8.2 %collective-permute-done.23 = bf16[128,2048]{1,0:T(8,128)(2,1)S(1)} collective-permute-done((bf16[128,2048]{1,0:T(8,128)(2,1)S(1)}, bf16[128,2048]{1,0:T(8,128)(2,1)S(1)}, u32[]{:S(2)}, u32[]{:S(2)}) %collective-permute-start.23) | collective-permute-done | bytes 524320 | tf_op jit(solution)/shard_map/ppermute | solution.py:106
  (62 shorter events, 19.1 us)
Async XLA Ops:
  0.0 21.5 %collective-permute-start.4 = (bf16[2048,512]{1,0:T(8,128)(2,1)}, bf16[2048,512]{1,0:T(8,128)(2,1)S(1)}, u32[]{:S(2)}, u32[]{:S(2)}) collective-permute-start(bf16[2048,512]{1,0:T(8,128)(2,1)} %bitcast.5), channel_id=1, source_target_pairs={{0,1},{1,0},{2,3},{3,2},{4,5},{5,4},{6,7},{7,6},{8,9},{9,8},{10,11... | collective-permute-start | bytes 6291464 | tf_op jit(solution)/shard_map/ppermute | solution.py:109
  2.7 15.4 %collective-permute-start.2 = (bf16[128,2048]{1,0:T(8,128)(2,1)}, bf16[128,2048]{1,0:T(8,128)(2,1)S(1)}, u32[]{:S(2)}, u32[]{:S(2)}) collective-permute-start(bf16[128,2048]{1,0:T(8,128)(2,1)} %refs_0_), channel_id=1, source_target_pairs={{0,2},{1,3},{2,0},{3,1},{4,6},{5,7},{6,4},{7,5},{8,10},{9,11},{10,... | collective-permute-start | bytes 1572872 | tf_op jit(solution)/shard_map/ppermute | solution.py:109
  5.3 16.2 %collective-permute-start.3 = (bf16[128,2048]{1,0:T(8,128)(2,1)}, bf16[128,2048]{1,0:T(8,128)(2,1)S(1)}, u32[]{:S(2)}, u32[]{:S(2)}) collective-permute-start(bf16[128,2048]{1,0:T(8,128)(2,1)} %refs_0_), channel_id=1, source_target_pairs={{0,4},{1,5},{2,6},{3,7},{4,8},{5,9},{6,10},{7,11},{8,12},{9,13},{1... | collective-permute-start | bytes 1572872 | tf_op jit(solution)/shard_map/ppermute | solution.py:106
  21.5 17.3 %collective-permute-start.5 = (bf16[2048,512]{1,0:T(8,128)(2,1)}, bf16[2048,512]{1,0:T(8,128)(2,1)}, u32[]{:S(2)}, u32[]{:S(2)}) collective-permute-start(bf16[2048,512]{1,0:T(8,128)(2,1)} %bitcast.11), channel_id=1, source_target_pairs={{0,1},{1,0},{2,3},{3,2},{4,5},{5,4},{6,7},{7,6},{8,9},{9,8},{10,11... | collective-permute-start | bytes 6291464 | tf_op jit(solution)/shard_map/ppermute | solution.py:109
  21.5 17.2 %collective-permute-start.6 = (bf16[512,2048]{1,0:T(8,128)(2,1)}, bf16[512,2048]{1,0:T(8,128)(2,1)}, u32[]{:S(2)}, u32[]{:S(2)}) collective-permute-start(bf16[512,2048]{1,0:T(8,128)(2,1)} %bitcast.17), channel_id=1, source_target_pairs={{0,1},{1,0},{2,3},{3,2},{4,5},{5,4},{6,7},{7,6},{8,9},{9,8},{10,11... | collective-permute-start | bytes 6291464 | tf_op jit(solution)/shard_map/ppermute | solution.py:109
  22.3 14.3 %collective-permute-start = (bf16[128,2176]{1,0:T(8,128)(2,1)S(1)}, bf16[128,2176]{1,0:T(8,128)(2,1)S(1)}, u32[]{:S(2)}, u32[]{:S(2)}) collective-permute-start(bf16[128,2176]{1,0:T(8,128)(2,1)S(1)} %concatenate.3.refs_2_), channel_id=1, source_target_pairs={{0,2},{1,3},{2,0},{3,1},{4,6},{5,7},{6,4},{7,5},{8,10},{9,11},{10,... | collective-permute-start | bytes 1671176 | tf_op jit(solution)/shard_map/ppermute | solution.py:109
  22.8 15.9 %collective-permute-start.1 = (bf16[128,2176]{1,0:T(8,128)(2,1)S(1)}, bf16[128,2176]{1,0:T(8,128)(2,1)}, u32[]{:S(2)}, u32[]{:S(2)}) collective-permute-start(bf16[128,2176]{1,0:T(8,128)(2,1)S(1)} %concatenate.3.refs_2_), channel_id=1, source_target_pairs={{0,4},{1,5},{2,6},{3,7},{4,8},{5,9},{6,10},{7,11},{8,12},{9,13},{1... | collective-permute-start | bytes 1671176 | tf_op jit(solution)/shard_map/ppermute | solution.py:106
  38.7 21.7 %collective-permute-start.7 = (bf16[128,2176]{1,0:T(8,128)(2,1)}, bf16[128,2176]{1,0:T(8,128)(2,1)S(1)}, u32[]{:S(2)}, u32[]{:S(2)}) collective-permute-start(bf16[128,2176]{1,0:T(8,128)(2,1)} %collective-permute-done.1.refs_2_), channel_id=1, source_target_pairs={{0,2},{1,3},{2,0},{3,1},{4,6},{5,7},{6,4},{7,5},{8,10},{9,11},{10,... | collective-permute-start | bytes 1671176 | tf_op jit(solution)/shard_map/ppermute | solution.py:109
  40.3 22.2 %collective-permute-start.8 = (bf16[128,2176]{1,0:T(8,128)(2,1)}, bf16[128,2176]{1,0:T(8,128)(2,1)S(1)}, u32[]{:S(2)}, u32[]{:S(2)}) collective-permute-start(bf16[128,2176]{1,0:T(8,128)(2,1)} %collective-permute-done.1.refs_2_), channel_id=1, source_target_pairs={{0,4},{1,5},{2,6},{3,7},{4,8},{5,9},{6,10},{7,11},{8,12},{9,13},{1... | collective-permute-start | bytes 1671176 | tf_op jit(solution)/shard_map/ppermute | solution.py:106
  40.3 28.7 %collective-permute-start.10 = (bf16[128,2048]{1,0:T(8,128)(2,1)}, bf16[128,2048]{1,0:T(8,128)(2,1)S(1)}, u32[]{:S(2)}, u32[]{:S(2)}) collective-permute-start(bf16[128,2048]{1,0:T(8,128)(2,1)} %copy-done.6), channel_id=1, source_target_pairs={{0,4},{1,5},{2,6},{3,7},{4,8},{5,9},{6,10},{7,11},{8,12},{9,13},{1... | collective-permute-start | bytes 1572872 | tf_op jit(solution)/shard_map/ppermute | solution.py:106
  40.3 28.7 %collective-permute-start.9 = (bf16[128,2048]{1,0:T(8,128)(2,1)}, bf16[128,2048]{1,0:T(8,128)(2,1)S(1)}, u32[]{:S(2)}, u32[]{:S(2)}) collective-permute-start(bf16[128,2048]{1,0:T(8,128)(2,1)} %copy-done.6), channel_id=1, source_target_pairs={{0,2},{1,3},{2,0},{3,1},{4,6},{5,7},{6,4},{7,5},{8,10},{9,11},{10,... | collective-permute-start | bytes 1572872 | tf_op jit(solution)/shard_map/ppermute | solution.py:109
  40.9 36.9 %collective-permute-start.13 = (bf16[128,2048]{1,0:T(8,128)(2,1)}, bf16[128,2048]{1,0:T(8,128)(2,1)S(1)}, u32[]{:S(2)}, u32[]{:S(2)}) collective-permute-start(bf16[128,2048]{1,0:T(8,128)(2,1)} %copy-done.8), channel_id=1, source_target_pairs={{0,12},{1,13},{2,14},{3,15},{4,0},{5,1},{6,2},{7,3},{8,4},{9,5},{1... | collective-permute-start | bytes 1572872 | tf_op jit(solution)/shard_map/ppermute | solution.py:106
  60.5 28.8 %collective-permute-start.14 = (bf16[128,2176]{1,0:T(8,128)(2,1)S(1)}, bf16[128,2176]{1,0:T(8,128)(2,1)S(1)}, u32[]{:S(2)}, u32[]{:S(2)}) collective-permute-start(bf16[128,2176]{1,0:T(8,128)(2,1)S(1)} %collective-permute-done.refs_3_), channel_id=1, source_target_pairs={{0,12},{1,13},{2,14},{3,15},{4,0},{5,1},{6,2},{7,3},{8,4},{9,5},{1... | collective-permute-start | bytes 1671176 | tf_op jit(solution)/shard_map/ppermute | solution.py:106
  62.5 30.2 %collective-permute-start.12 = (bf16[128,2176]{1,0:T(8,128)(2,1)S(1)}, bf16[128,2176]{1,0:T(8,128)(2,1)S(1)}, u32[]{:S(2)}, u32[]{:S(2)}) collective-permute-start(bf16[128,2176]{1,0:T(8,128)(2,1)S(1)} %collective-permute-done.8.refs_2_), channel_id=1, source_target_pairs={{0,2},{1,3},{2,0},{3,1},{4,6},{5,7},{6,4},{7,5},{8,10},{9,11},{10,... | collective-permute-start | bytes 1671176 | tf_op jit(solution)/shard_map/ppermute | solution.py:109
  69.1 23.6 %collective-permute-start.11 = (bf16[128,2048]{1,0:T(8,128)(2,1)S(1)}, bf16[128,2048]{1,0:T(8,128)(2,1)S(1)}, u32[]{:S(2)}, u32[]{:S(2)}) collective-permute-start(bf16[128,2048]{1,0:T(8,128)(2,1)S(1)} %collective-permute-done.10.refs_0_), channel_id=1, source_target_pairs={{0,2},{1,3},{2,0},{3,1},{4,6},{5,7},{6,4},{7,5},{8,10},{9,11},{10,... | collective-permute-start | bytes 1572872 | tf_op jit(solution)/shard_map/ppermute | solution.py:109
  77.8 25.7 %collective-permute-start.15 = (bf16[128,2048]{1,0:T(8,128)(2,1)S(1)}, bf16[128,2048]{1,0:T(8,128)(2,1)S(1)}, u32[]{:S(2)}, u32[]{:S(2)}) collective-permute-start(bf16[128,2048]{1,0:T(8,128)(2,1)S(1)} %collective-permute-done.10.refs_0_), channel_id=1, source_target_pairs={{0,4},{1,5},{2,6},{3,7},{4,8},{5,9},{6,10},{7,11},{8,12},{9,13},{1... | collective-permute-start | bytes 1572872 | tf_op jit(solution)/shard_map/ppermute | solution.py:106
  87.0 16.4 %collective-permute-start.16 = (bf16[128,2048]{1,0:T(8,128)(2,1)S(1)}, bf16[128,2048]{1,0:T(8,128)(2,1)S(1)}, u32[]{:S(2)}, u32[]{:S(2)}) collective-permute-start(bf16[128,2048]{1,0:T(8,128)(2,1)S(1)} %get-tuple-element.76), channel_id=1, source_target_pairs={{0,2},{1,3},{2,0},{3,1},{4,6},{5,7},{6,4},{7,5},{8,10},{9,11},{10,... | collective-permute-start | bytes 1572872 | tf_op jit(solution)/shard_map/ppermute | solution.py:109
  89.3 26.2 %collective-permute-start.17 = (bf16[128,2176]{1,0:T(8,128)(2,1)S(1)}, bf16[128,2176]{1,0:T(8,128)(2,1)S(1)}, u32[]{:S(2)}, u32[]{:S(2)}) collective-permute-start(bf16[128,2176]{1,0:T(8,128)(2,1)S(1)} %collective-permute-done.8.refs_2_), channel_id=1, source_target_pairs={{0,4},{1,5},{2,6},{3,7},{4,8},{5,9},{6,10},{7,11},{8,12},{9,13},{1... | collective-permute-start | bytes 1671176 | tf_op jit(solution)/shard_map/ppermute | solution.py:106
  103.5 11.9 %collective-permute-start.18 = (bf16[128,2048]{1,0:T(8,128)(2,1)S(1)}, bf16[128,2048]{1,0:T(8,128)(2,1)S(1)}, u32[]{:S(2)}, u32[]{:S(2)}) collective-permute-start(bf16[128,2048]{1,0:T(8,128)(2,1)S(1)} %get-tuple-element.81), channel_id=1, source_target_pairs={{0,2},{1,3},{2,0},{3,1},{4,6},{5,7},{6,4},{7,5},{8,10},{9,11},{10,... | collective-permute-start | bytes 1572872 | tf_op jit(solution)/shard_map/ppermute | solution.py:109
  104.2 22.5 %collective-permute-start.20 = (bf16[128,2048]{1,0:T(8,128)(2,1)S(1)}, bf16[128,2048]{1,0:T(8,128)(2,1)S(1)}, u32[]{:S(2)}, u32[]{:S(2)}) collective-permute-start(bf16[128,2048]{1,0:T(8,128)(2,1)S(1)} %add_convert_fusion.1), channel_id=1, source_target_pairs={{0,12},{1,13},{2,14},{3,15},{4,0},{5,1},{6,2},{7,3},{8,4},{9,5},{1... | collective-permute-start | bytes 1572872 | tf_op jit(solution)/shard_map/ppermute | solution.py:106
  115.5 11.7 %collective-permute-start.21 = (bf16[128,2048]{1,0:T(8,128)(2,1)S(1)}, bf16[128,2048]{1,0:T(8,128)(2,1)S(1)}, u32[]{:S(2)}, u32[]{:S(2)}) collective-permute-start(bf16[128,2048]{1,0:T(8,128)(2,1)S(1)} %pair_rows.8), channel_id=1, source_target_pairs={{0,2},{1,3},{2,0},{3,1},{4,6},{5,7},{6,4},{7,5},{8,10},{9,11},{10,... | collective-permute-start | bytes 1572872 | tf_op jit(solution)/shard_map/ppermute | solution.py:109
  116.2 19.1 %collective-permute-start.22 = (bf16[128,2048]{1,0:T(8,128)(2,1)S(1)}, bf16[128,2048]{1,0:T(8,128)(2,1)S(1)}, u32[]{:S(2)}, u32[]{:S(2)}) collective-permute-start(bf16[128,2048]{1,0:T(8,128)(2,1)S(1)} %add_convert_fusion.2), channel_id=1, source_target_pairs={{0,4},{1,5},{2,6},{3,7},{4,8},{5,9},{6,10},{7,11},{8,12},{9,13},{1... | collective-permute-start | bytes 1572872 | tf_op jit(solution)/shard_map/ppermute | solution.py:106
  126.6 13.7 %collective-permute-start.19 = (bf16[128,2048]{1,0:T(8,128)(2,1)S(1)}, bf16[128,2048]{1,0:T(8,128)(2,1)S(1)}, u32[]{:S(2)}, u32[]{:S(2)}) collective-permute-start(bf16[128,2048]{1,0:T(8,128)(2,1)S(1)} %get-tuple-element.84), channel_id=1, source_target_pairs={{0,2},{1,3},{2,0},{3,1},{4,6},{5,7},{6,4},{7,5},{8,10},{9,11},{10,... | collective-permute-start | bytes 1572872 | tf_op jit(solution)/shard_map/ppermute | solution.py:109
  135.4 13.1 %collective-permute-start.23 = (bf16[128,2048]{1,0:T(8,128)(2,1)S(1)}, bf16[128,2048]{1,0:T(8,128)(2,1)S(1)}, u32[]{:S(2)}, u32[]{:S(2)}) collective-permute-start(bf16[128,2048]{1,0:T(8,128)(2,1)S(1)} %add_convert_fusion), channel_id=1, source_target_pairs={{0,4},{1,5},{2,6},{3,7},{4,8},{5,9},{6,10},{7,11},{8,12},{9,13},{1... | collective-permute-start | bytes 1572872 | tf_op jit(solution)/shard_map/ppermute | solution.py:106
  (10 other events, 92.3 us)

commit v5 on v4

--- a/solution.py
+++ b/solution.py
@@ -10,6 +10,33 @@
 F32 = jnp.float32
 BF16 = jnp.bfloat16
 LAST = (((1,), (1,)), ((), ()))
+
+
+def gated_kernel(owners, ids, gates, grad, out):
+    width = grad.shape[1]
+    out[:, :width] = grad[...]
+    lane = lax.broadcasted_iota(jnp.int32, (out.shape[1] - width, grad.shape[0]), 0)
+    expert = lax.rem(lane, owners)
+    high = jnp.zeros(lane.shape, F32)
+    for k in range(ids.shape[0]):
+        high = jnp.where(ids[k : k + 1, :] == expert, gates[k : k + 1, :], high)
+    low = high - high.astype(BF16).astype(F32)
+    lowest = low - low.astype(BF16).astype(F32)
+    parts = jnp.where(lane < owners, high, jnp.where(lane < 2 * owners, low, lowest))
+    parts = jnp.where(lane < 3 * owners, parts, 0.0)
+    out[:, width:] = parts.T.astype(BF16)
+
+
+def gated_rows(grad, ids, gates, owners):
+    rows, width = grad.shape
+    near = pl.BlockSpec(memory_space=pltpu.VMEM)
+    return pl.pallas_call(
+        partial(gated_kernel, owners),
+        in_specs=[near] * 3,
+        out_specs=near,
+        out_shape=jax.ShapeDtypeStruct((rows, width + -(-3 * owners // 128) * 128), BF16),
+        name="gated_rows",
+    )(ids.T, gates.T, grad)
 
 
 def pair_kernel(blocks, owners, wide, experts, *refs):
@@ -98,7 +125,6 @@
 def gathered(layer_input, out_grad, expert_ids, gates, w_gate, w_up, w_down):
     owners = lax.axis_size("expert")
     ring = owners // 4
-    rows = layer_input.shape[0]
     me = lax.axis_index("expert")
     experts = jnp.stack([me, me ^ 1]).astype(jnp.int32)
 
@@ -110,19 +136,9 @@
 
     tie = lax.optimization_barrier
 
-    named = expert_ids[:, :, None] == jnp.arange(owners, dtype=jnp.int32)[None, None, :]
-    rest = jnp.sum(jnp.where(named, gates[:, :, None], 0.0), axis=1)
-    parts = []
-    for _ in range(3):
-        part = lax.reduce_precision(rest, 8, 7)
-        rest = rest - part
-        parts.append(part.astype(BF16))
-    spare = jnp.zeros((rows, -3 * owners % 128), BF16)
-
     own = (w_gate[0], w_up[0], w_down[0])
 
-    x, g = tie((layer_input, jnp.concatenate([out_grad, *parts, spare], axis=1)))
-    xs, gs = [x], [g]
+    xs, gs = [layer_input], [gated_rows(out_grad, expert_ids, gates, owners)]
     far_xs, far_gs, nears, fars = [], [], [], []
 
     def compute(s):
@@ -133,10 +149,9 @@
     for s in range(ring - 2):
         far_x, x, far_g, g = swap(xs[s], 2), turn(xs[s], 1), swap(gs[s], 2), turn(gs[s], 1)
         if s == 0:
-            theirs = [swap(own[0], 1)]
-            sent, far_x, x, theirs = tie((own[1:], far_x, x, theirs))
-            far_g, g, theirs = tie((far_g, g, theirs + [swap(w, 1) for w in sent]))
-            weights = (*own, *theirs)
+            theirs, sent = [swap(own[0], 1)], own[1:]
+            far_x, x, far_g, g, theirs, sent = tie((far_x, x, far_g, g, theirs, sent))
+            weights = (*own, *theirs, *(swap(w, 1) for w in sent))
         else:
             near, far = compute(s - 1)
             far_x, x = tie((far_x, x))

time: 150 us -> 147 us (0.980)
  waiting for transfers between devices: 73 us -> 69.9 us
  Pallas kernels: 42.6 us -> 45.1 us
  local copies, waits for them, and re-layouts: 8.66 us -> 6.88 us
    ppermute x13, waiting for transfers between devices: 32.2 us -> 29.4 us  [swap(): return lax.ppermute(value, 'expert', [(i, i ^ bit) for i in range(owners)])]
    ppermute x13, starting transfers between devices: 10.7 us -> 13 us  [swap(): return lax.ppermute(value, 'expert', [(i, i ^ bit) for i in range(owners)])]
    ppermute x11, starting transfers between devices: 12.2 us -> 10.1 us  [turn(): lax.ppermute(value, 'expert', [(i, (i + 4 * by) % owners) for i in range(...]
    pallas_call x0 -> x1, Pallas kernels: none -> 1.99 us  [gated_rows(): pl.pallas_call(partial(gated_kernel, owners), in_specs=[near] * 3, out_sp...]
    unnamed x20 -> x16, local copies, waits for them, and re-layouts: 7.15 us -> 6.88 us
  transfers between devices with their start and end apart: 24 -> 24, of which waited for: 13 -> 13; matrix products, arithmetic and copies ran while one was open for 2% -> 0% of each run, Pallas kernels for 28% -> 31%
where the time goes in v5:
time: 147 us
  waiting for transfers between devices  69.9 us (48%)
  Pallas kernels  45.1 us (31%)
  starting transfers between devices  23 us (16%)
  local copies, waits for them, and re-layouts  6.88 us (5%)
  other arithmetic  1.76 us (1%)
    pallas_call x5, Pallas kernels, pair_rows(): pl.pallas_call(partial(pair_kernel, blocks, owners, 512 if width % 512 ==...  43.1 us
    ppermute x11, waiting for transfers between devices, turn(): lax.ppermute(value, 'expert', [(i, (i + 4 * by) % owners) for i in range(...  40.5 us
    ppermute x13, waiting for transfers between devices, swap(): return lax.ppermute(value, 'expert', [(i, i ^ bit) for i in range(owners)])  29.4 us
    ppermute x13, starting transfers between devices, swap(): return lax.ppermute(value, 'expert', [(i, i ^ bit) for i in range(owners)])  13 us
    ppermute x11, starting transfers between devices, turn(): lax.ppermute(value, 'expert', [(i, (i + 4 * by) % owners) for i in range(...  10.1 us
    unnamed x16, local copies, waits for them, and re-layouts  6.88 us
  transfers between devices with their start and end apart: 24, of which 13 were waited for; matrix products, arithmetic and copies ran while one was open for 0% of the time, Pallas kernels for 31%

profile of v5, /device:TPU:0, one launch (start us, length us, event | category | flops | bytes accessed | tf_op | source)
XLA Modules:
  0.0 146.8 jit_solution(10778610026370544037)
XLA Ops:
  0.5 2.0 %gated_rows.1.refs_2_ = bf16[128,2176]{1,0:T(8,128)(2,1)} custom-call(s32[8,128]{1,0:T(8,128)} %bitcast.25, f32[8,128]{1,0:T(8,128)} %bitcast.26, bf16[128,2048]{1,0:T(8,128)(2,1)} %grad.1), custom_call_target="tpu_custom_call" | custom-call | tf_op jit(solution)/shard_map/gated_rows/pallas_call | solution.py:33
  2.4 2.5 %collective-permute-start.2 = (bf16[128,2176]{1,0:T(8,128)(2,1)}, bf16[128,2176]{1,0:T(8,128)(2,1)}, u32[]{:S(2)}, u32[]{:S(2)}) collective-permute-start(bf16[128,2176]{1,0:T(8,128)(2,1)} %gated_rows.1.refs_2_), channel_id=1, source_target_pairs={{0,2},{1,3},{2,0},{3,1},{4,6},{5,7},{6,4},{7,5},{8,10},{9,11},{10,... | collective-permute-start | bytes 1671176 | tf_op jit(solution)/shard_map/ppermute | solution.py:135
  8.6 21.2 %collective-permute-done.refs_1_ = bf16[128,2048]{1,0:T(8,128)(2,1)} collective-permute-done((bf16[128,2048]{1,0:T(8,128)(2,1)}, bf16[128,2048]{1,0:T(8,128)(2,1)}, u32[]{:S(2)}, u32[]{:S(2)}) %collective-permute-start) | collective-permute-done | bytes 524320 | tf_op jit(solution)/shard_map/ppermute | solution.py:135
  29.8 3.4 %collective-permute-done.1.refs_0_ = bf16[128,2048]{1,0:T(8,128)(2,1)} collective-permute-done((bf16[128,2048]{1,0:T(8,128)(2,1)}, bf16[128,2048]{1,0:T(8,128)(2,1)}, u32[]{:S(2)}, u32[]{:S(2)}) %collective-permute-start.1) | collective-permute-done | bytes 524320 | tf_op jit(solution)/shard_map/ppermute | solution.py:132
  35.6 2.1 %collective-permute-done.7.refs_8_.refs_6_ = bf16[2048,512]{1,0:T(8,128)(2,1)} collective-permute-done((bf16[2048,512]{1,0:T(8,128)(2,1)}, bf16[2048,512]{1,0:T(8,128)(2,1)}, u32[]{:S(2)}, u32[]{:S(2)}) %collective-permute-start.7) | collective-permute-done | bytes 2097184 | tf_op jit(solution)/shard_map/ppermute | solution.py:135
  38.3 2.5 %collective-permute-done.8.refs_9_.refs_7_ = bf16[512,2048]{1,0:T(8,128)(2,1)} collective-permute-done((bf16[512,2048]{1,0:T(8,128)(2,1)}, bf16[512,2048]{1,0:T(8,128)(2,1)}, u32[]{:S(2)}, u32[]{:S(2)}) %collective-permute-start.8) | collective-permute-done | bytes 2097184 | tf_op jit(solution)/shard_map/ppermute | solution.py:135
  40.7 1.7 %collective-permute-start.13 = (bf16[128,2048]{1,0:T(8,128)(2,1)}, bf16[128,2048]{1,0:T(8,128)(2,1)S(1)}, u32[]{:S(2)}, u32[]{:S(2)}) collective-permute-start(bf16[128,2048]{1,0:T(8,128)(2,1)} %collective-permute-done.refs_1_), channel_id=1, source_target_pairs={{0,12},{1,13},{2,14},{3,15},{4,0},{5,1},{6,2},{7,3},{8,4},{9,5},{1... | collective-permute-start | bytes 1572872 | tf_op jit(solution)/shard_map/ppermute | solution.py:132
  42.5 1.6 %copy-done = bf16[1,2048,512]{2,1,0:T(8,128)(2,1)S(1)} copy-done((bf16[1,2048,512]{2,1,0:T(8,128)(2,1)S(1)}, bf16[1,2048,512]{2,1,0:T(8,128)(2,1)}, u32[]{:S(2)}) %copy-start) | copy-done | bytes 2097176
  44.1 1.6 %copy-done.2 = bf16[1,2048,512]{2,1,0:T(8,128)(2,1)S(1)} copy-done((bf16[1,2048,512]{2,1,0:T(8,128)(2,1)S(1)}, bf16[1,2048,512]{2,1,0:T(8,128)(2,1)}, u32[]{:S(2)}) %copy-start.2) | copy-done | bytes 2097176
  45.6 1.6 %copy-done.4 = bf16[1,512,2048]{2,1,0:T(8,128)(2,1)S(1)} copy-done((bf16[1,512,2048]{2,1,0:T(8,128)(2,1)S(1)}, bf16[1,512,2048]{2,1,0:T(8,128)(2,1)}, u32[]{:S(2)}) %copy-start.4) | copy-done | bytes 2097176
  49.3 8.9 %pair_rows.5 = (f32[128,2048]{1,0:T(8,128)S(1)}, bf16[128,2048]{1,0:T(8,128)(2,1)S(1)}) custom-call(s32[2]{0:T(128)S(1)} %pad_add_fusion.experts, bf16[128,2048]{1,0:T(8,128)(2,1)S(1)} %copy-done.7, bf16[128,2048]{1,0:T(8,128)(2,1)} %collective-permute-done.refs_1_, bf16[128,2176]{1,0:T(8,128)(2,1)S(1)} %copy-done.6, ...), custom_call_target="tpu_custom_call" | custom-call | flops 5368709120 | bytes 16252928 | tf_op jit(solution)/shard_map/pair_rows/pallas_call | solution.py:102
  59.2 3.9 %collective-permute-done.10.refs_0_ = bf16[128,2048]{1,0:T(8,128)(2,1)S(1)} collective-permute-done((bf16[128,2048]{1,0:T(8,128)(2,1)}, bf16[128,2048]{1,0:T(8,128)(2,1)S(1)}, u32[]{:S(2)}, u32[]{:S(2)}) %collective-permute-start.10) | collective-permute-done | bytes 524320 | tf_op jit(solution)/shard_map/ppermute | solution.py:132
  64.6 8.6 %collective-permute-done.13.refs_0_ = bf16[128,2048]{1,0:T(8,128)(2,1)S(1)} collective-permute-done((bf16[128,2048]{1,0:T(8,128)(2,1)}, bf16[128,2048]{1,0:T(8,128)(2,1)S(1)}, u32[]{:S(2)}, u32[]{:S(2)}) %collective-permute-start.13) | collective-permute-done | bytes 524320 | tf_op jit(solution)/shard_map/ppermute | solution.py:132
  73.7 8.9 %pair_rows.6 = (f32[128,2048]{1,0:T(8,128)S(1)}, bf16[128,2048]{1,0:T(8,128)(2,1)S(1)}) custom-call(s32[2]{0:T(128)S(1)} %pad_add_fusion.experts, bf16[128,2048]{1,0:T(8,128)(2,1)} %collective-permute-done.1.refs_0_, bf16[128,2048]{1,0:T(8,128)(2,1)S(1)} %collective-permute-done.9.refs_1_, bf16[128,2176]{1,0:T(8,128)(2,1)} %collective-permute-done.3.refs_2_, ...), custom_call_target="tpu_custom_call" | custom-call | flops 5368709120 | bytes 16252928 | tf_op jit(solution)/shard_map/pair_rows/pallas_call | solution.py:102
  82.6 1.6 %collective-permute-start.16 = (bf16[128,2048]{1,0:T(8,128)(2,1)S(1)}, bf16[128,2048]{1,0:T(8,128)(2,1)S(1)}, u32[]{:S(2)}, u32[]{:S(2)}) collective-permute-start(bf16[128,2048]{1,0:T(8,128)(2,1)S(1)} %get-tuple-element.66), channel_id=1, source_target_pairs={{0,2},{1,3},{2,0},{3,1},{4,6},{5,7},{6,4},{7,5},{8,10},{9,11},{10,... | collective-permute-start | bytes 1572872 | tf_op jit(solution)/shard_map/ppermute | solution.py:135
  84.2 2.1 %collective-permute-done.14.refs_1_ = bf16[128,2176]{1,0:T(8,128)(2,1)S(1)} collective-permute-done((bf16[128,2176]{1,0:T(8,128)(2,1)}, bf16[128,2176]{1,0:T(8,128)(2,1)S(1)}, u32[]{:S(2)}, u32[]{:S(2)}) %collective-permute-start.14) | collective-permute-done | bytes 557088 | tf_op jit(solution)/shard_map/ppermute | solution.py:132
  86.7 9.0 %pair_rows.7 = (f32[128,2048]{1,0:T(8,128)S(1)}, bf16[128,2048]{1,0:T(8,128)(2,1)S(1)}) custom-call(s32[2]{0:T(128)S(1)} %pad_add_fusion.experts, bf16[128,2048]{1,0:T(8,128)(2,1)S(1)} %collective-permute-done.10.refs_0_, bf16[128,2048]{1,0:T(8,128)(2,1)S(1)} %collective-permute-done.11.refs_1_, bf16[128,2176]{1,0:T(8,128)(2,1)S(1)} %collective-permute-done.6.refs_2_, ...), custom_call_target="tpu_custom_call" | custom-call | flops 5368709120 | bytes 16252928 | tf_op jit(solution)/shard_map/pair_rows/pallas_call | solution.py:102
  95.7 1.8 %collective-permute-done.15.refs_0_ = bf16[128,2048]{1,0:T(8,128)(2,1)S(1)} collective-permute-done((bf16[128,2048]{1,0:T(8,128)(2,1)S(1)}, bf16[128,2048]{1,0:T(8,128)(2,1)S(1)}, u32[]{:S(2)}, u32[]{:S(2)}) %collective-permute-start.15) | collective-permute-done | bytes 524320 | tf_op jit(solution)/shard_map/ppermute | solution.py:132
  99.2 2.2 %collective-permute-start.20 = (bf16[128,2048]{1,0:T(8,128)(2,1)S(1)}, bf16[128,2048]{1,0:T(8,128)(2,1)S(1)}, u32[]{:S(2)}, u32[]{:S(2)}) collective-permute-start(bf16[128,2048]{1,0:T(8,128)(2,1)S(1)} %add_convert_fusion.1), channel_id=1, source_target_pairs={{0,12},{1,13},{2,14},{3,15},{4,0},{5,1},{6,2},{7,3},{8,4},{9,5},{1... | collective-permute-start | bytes 1572872 | tf_op jit(solution)/shard_map/ppermute | solution.py:132
  101.4 8.2 %pair_rows.8 = bf16[128,2048]{1,0:T(8,128)(2,1)S(1)} custom-call(s32[2]{0:T(128)S(1)} %pad_add_fusion.experts, bf16[128,2048]{1,0:T(8,128)(2,1)S(1)} %collective-permute-done.13.refs_0_, bf16[128,2176]{1,0:T(8,128)(2,1)S(1)} %collective-permute-done.14.refs_1_, bf16[2048,512]{1,0:T(8,128)(2,1)S(1)} %bitcast.11, bf16[2048,512]{1,0:T(8,128)(2,1)S(1)} %bitcast.17, ...), custom_call_target="tpu_custom_call" | custom-call | flops 2684354560 | bytes 14417920 | tf_op jit(solution)/shard_map/pair_rows/pallas_call | solution.py:102
  111.3 8.2 %pair_rows.9 = f32[128,2048]{1,0:T(8,128)S(1)} custom-call(s32[2]{0:T(128)S(1)} %pad_add_fusion.experts, bf16[128,2048]{1,0:T(8,128)(2,1)S(1)} %collective-permute-done.15.refs_0_, bf16[128,2176]{1,0:T(8,128)(2,1)S(1)} %collective-permute-done.17.refs_1_, bf16[2048,512]{1,0:T(8,128)(2,1)S(1)} %bitcast.12, bf16[2048,512]{1,0:T(8,128)(2,1)S(1)} %bitcast.18, ...), custom_call_target="tpu_custom_call" | custom-call | flops 2684354560 | bytes 14417920 | tf_op jit(solution)/shard_map/pair_rows/pallas_call | solution.py:102
  122.4 8.3 %collective-permute-done.22 = bf16[128,2048]{1,0:T(8,128)(2,1)S(1)} collective-permute-done((bf16[128,2048]{1,0:T(8,128)(2,1)S(1)}, bf16[128,2048]{1,0:T(8,128)(2,1)S(1)}, u32[]{:S(2)}, u32[]{:S(2)}) %collective-permute-start.22) | collective-permute-done | bytes 524320 | tf_op jit(solution)/shard_map/ppermute | solution.py:132
  131.0 3.3 %collective-permute-done.19 = bf16[128,2048]{1,0:T(8,128)(2,1)S(1)} collective-permute-done((bf16[128,2048]{1,0:T(8,128)(2,1)S(1)}, bf16[128,2048]{1,0:T(8,128)(2,1)S(1)}, u32[]{:S(2)}, u32[]{:S(2)}) %collective-permute-start.19) | collective-permute-done | bytes 524320 | tf_op jit(solution)/shard_map/ppermute | solution.py:135
  134.4 11.2 %collective-permute-done.23 = bf16[128,2048]{1,0:T(8,128)(2,1)S(1)} collective-permute-done((bf16[128,2048]{1,0:T(8,128)(2,1)S(1)}, bf16[128,2048]{1,0:T(8,128)(2,1)S(1)}, u32[]{:S(2)}, u32[]{:S(2)}) %collective-permute-start.23) | collective-permute-done | bytes 524320 | tf_op jit(solution)/shard_map/ppermute | solution.py:132
  (51 shorter events, 20.3 us)
Async XLA Ops:
  0.0 33.2 %collective-permute-start.4 = (bf16[2048,512]{1,0:T(8,128)(2,1)}, bf16[2048,512]{1,0:T(8,128)(2,1)S(1)}, u32[]{:S(2)}, u32[]{:S(2)}) collective-permute-start(bf16[2048,512]{1,0:T(8,128)(2,1)} %bitcast.7), channel_id=1, source_target_pairs={{0,1},{1,0},{2,3},{3,2},{4,5},{5,4},{6,7},{7,6},{8,9},{9,8},{10,11... | collective-permute-start | bytes 6291464 | tf_op jit(solution)/shard_map/ppermute | solution.py:135
  2.4 30.7 %collective-permute-start.2 = (bf16[128,2176]{1,0:T(8,128)(2,1)}, bf16[128,2176]{1,0:T(8,128)(2,1)}, u32[]{:S(2)}, u32[]{:S(2)}) collective-permute-start(bf16[128,2176]{1,0:T(8,128)(2,1)} %gated_rows.1.refs_2_), channel_id=1, source_target_pairs={{0,2},{1,3},{2,0},{3,1},{4,6},{5,7},{6,4},{7,5},{8,10},{9,11},{10,... | collective-permute-start | bytes 1671176 | tf_op jit(solution)/shard_map/ppermute | solution.py:135
  5.0 28.2 %collective-permute-start.3 = (bf16[128,2176]{1,0:T(8,128)(2,1)}, bf16[128,2176]{1,0:T(8,128)(2,1)}, u32[]{:S(2)}, u32[]{:S(2)}) collective-permute-start(bf16[128,2176]{1,0:T(8,128)(2,1)} %gated_rows.1.refs_2_), channel_id=1, source_target_pairs={{0,4},{1,5},{2,6},{3,7},{4,8},{5,9},{6,10},{7,11},{8,12},{9,13},{1... | collective-permute-start | bytes 1671176 | tf_op jit(solution)/shard_map/ppermute | solution.py:132
  6.5 23.3 %collective-permute-start = (bf16[128,2048]{1,0:T(8,128)(2,1)}, bf16[128,2048]{1,0:T(8,128)(2,1)}, u32[]{:S(2)}, u32[]{:S(2)}) collective-permute-start(bf16[128,2048]{1,0:T(8,128)(2,1)} %refs_0_.1), channel_id=1, source_target_pairs={{0,2},{1,3},{2,0},{3,1},{4,6},{5,7},{6,4},{7,5},{8,10},{9,11},{10,... | collective-permute-start | bytes 1572872 | tf_op jit(solution)/shard_map/ppermute | solution.py:135
  7.0 26.1 %collective-permute-start.1 = (bf16[128,2048]{1,0:T(8,128)(2,1)}, bf16[128,2048]{1,0:T(8,128)(2,1)}, u32[]{:S(2)}, u32[]{:S(2)}) collective-permute-start(bf16[128,2048]{1,0:T(8,128)(2,1)} %refs_0_.1), channel_id=1, source_target_pairs={{0,4},{1,5},{2,6},{3,7},{4,8},{5,9},{6,10},{7,11},{8,12},{9,13},{1... | collective-permute-start | bytes 1572872 | tf_op jit(solution)/shard_map/ppermute | solution.py:132
  33.2 4.6 %collective-permute-start.7 = (bf16[2048,512]{1,0:T(8,128)(2,1)}, bf16[2048,512]{1,0:T(8,128)(2,1)}, u32[]{:S(2)}, u32[]{:S(2)}) collective-permute-start(bf16[2048,512]{1,0:T(8,128)(2,1)} %bitcast.13), channel_id=1, source_target_pairs={{0,1},{1,0},{2,3},{3,2},{4,5},{5,4},{6,7},{7,6},{8,9},{9,8},{10,11... | collective-permute-start | bytes 6291464 | tf_op jit(solution)/shard_map/ppermute | solution.py:135
  33.3 7.5 %collective-permute-start.8 = (bf16[512,2048]{1,0:T(8,128)(2,1)}, bf16[512,2048]{1,0:T(8,128)(2,1)}, u32[]{:S(2)}, u32[]{:S(2)}) collective-permute-start(bf16[512,2048]{1,0:T(8,128)(2,1)} %bitcast.19), channel_id=1, source_target_pairs={{0,1},{1,0},{2,3},{3,2},{4,5},{5,4},{6,7},{7,6},{8,9},{9,8},{10,11... | collective-permute-start | bytes 6291464 | tf_op jit(solution)/shard_map/ppermute | solution.py:135
  33.8 24.4 %collective-permute-start.5 = (bf16[128,2176]{1,0:T(8,128)(2,1)}, bf16[128,2176]{1,0:T(8,128)(2,1)S(1)}, u32[]{:S(2)}, u32[]{:S(2)}) collective-permute-start(bf16[128,2176]{1,0:T(8,128)(2,1)} %collective-permute-done.3.refs_2_), channel_id=1, source_target_pairs={{0,2},{1,3},{2,0},{3,1},{4,6},{5,7},{6,4},{7,5},{8,10},{9,11},{10,... | collective-permute-start | bytes 1671176 | tf_op jit(solution)/shard_map/ppermute | solution.py:135
  34.3 24.5 %collective-permute-start.6 = (bf16[128,2176]{1,0:T(8,128)(2,1)}, bf16[128,2176]{1,0:T(8,128)(2,1)S(1)}, u32[]{:S(2)}, u32[]{:S(2)}) collective-permute-start(bf16[128,2176]{1,0:T(8,128)(2,1)} %collective-permute-done.3.refs_2_), channel_id=1, source_target_pairs={{0,4},{1,5},{2,6},{3,7},{4,8},{5,9},{6,10},{7,11},{8,12},{9,13},{1... | collective-permute-start | bytes 1671176 | tf_op jit(solution)/shard_map/ppermute | solution.py:132
  34.3 28.8 %collective-permute-start.10 = (bf16[128,2048]{1,0:T(8,128)(2,1)}, bf16[128,2048]{1,0:T(8,128)(2,1)S(1)}, u32[]{:S(2)}, u32[]{:S(2)}) collective-permute-start(bf16[128,2048]{1,0:T(8,128)(2,1)} %collective-permute-done.1.refs_0_), channel_id=1, source_target_pairs={{0,4},{1,5},{2,6},{3,7},{4,8},{5,9},{6,10},{7,11},{8,12},{9,13},{1... | collective-permute-start | bytes 1572872 | tf_op jit(solution)/shard_map/ppermute | solution.py:132
  37.7 25.4 %collective-permute-start.9 = (bf16[128,2048]{1,0:T(8,128)(2,1)}, bf16[128,2048]{1,0:T(8,128)(2,1)S(1)}, u32[]{:S(2)}, u32[]{:S(2)}) collective-permute-start(bf16[128,2048]{1,0:T(8,128)(2,1)} %collective-permute-done.1.refs_0_), channel_id=1, source_target_pairs={{0,2},{1,3},{2,0},{3,1},{4,6},{5,7},{6,4},{7,5},{8,10},{9,11},{10,... | collective-permute-start | bytes 1572872 | tf_op jit(solution)/shard_map/ppermute | solution.py:135
  40.7 32.5 %collective-permute-start.13 = (bf16[128,2048]{1,0:T(8,128)(2,1)}, bf16[128,2048]{1,0:T(8,128)(2,1)S(1)}, u32[]{:S(2)}, u32[]{:S(2)}) collective-permute-start(bf16[128,2048]{1,0:T(8,128)(2,1)} %collective-permute-done.refs_1_), channel_id=1, source_target_pairs={{0,12},{1,13},{2,14},{3,15},{4,0},{5,1},{6,2},{7,3},{8,4},{9,5},{1... | collective-permute-start | bytes 1572872 | tf_op jit(solution)/shard_map/ppermute | solution.py:132
  58.2 28.1 %collective-permute-start.14 = (bf16[128,2176]{1,0:T(8,128)(2,1)}, bf16[128,2176]{1,0:T(8,128)(2,1)S(1)}, u32[]{:S(2)}, u32[]{:S(2)}) collective-permute-start(bf16[128,2176]{1,0:T(8,128)(2,1)} %collective-permute-done.2.refs_3_), channel_id=1, source_target_pairs={{0,12},{1,13},{2,14},{3,15},{4,0},{5,1},{6,2},{7,3},{8,4},{9,5},{1... | collective-permute-start | bytes 1671176 | tf_op jit(solution)/shard_map/ppermute | solution.py:132
  58.7 28.0 %collective-permute-start.12 = (bf16[128,2176]{1,0:T(8,128)(2,1)S(1)}, bf16[128,2176]{1,0:T(8,128)(2,1)S(1)}, u32[]{:S(2)}, u32[]{:S(2)}) collective-permute-start(bf16[128,2176]{1,0:T(8,128)(2,1)S(1)} %collective-permute-done.6.refs_2_), channel_id=1, source_target_pairs={{0,2},{1,3},{2,0},{3,1},{4,6},{5,7},{6,4},{7,5},{8,10},{9,11},{10,... | collective-permute-start | bytes 1671176 | tf_op jit(solution)/shard_map/ppermute | solution.py:135
  63.1 23.6 %collective-permute-start.11 = (bf16[128,2048]{1,0:T(8,128)(2,1)S(1)}, bf16[128,2048]{1,0:T(8,128)(2,1)S(1)}, u32[]{:S(2)}, u32[]{:S(2)}) collective-permute-start(bf16[128,2048]{1,0:T(8,128)(2,1)S(1)} %collective-permute-done.10.refs_0_), channel_id=1, source_target_pairs={{0,2},{1,3},{2,0},{3,1},{4,6},{5,7},{6,4},{7,5},{8,10},{9,11},{10,... | collective-permute-start | bytes 1572872 | tf_op jit(solution)/shard_map/ppermute | solution.py:135
  73.3 24.3 %collective-permute-start.15 = (bf16[128,2048]{1,0:T(8,128)(2,1)S(1)}, bf16[128,2048]{1,0:T(8,128)(2,1)S(1)}, u32[]{:S(2)}, u32[]{:S(2)}) collective-permute-start(bf16[128,2048]{1,0:T(8,128)(2,1)S(1)} %collective-permute-done.10.refs_0_), channel_id=1, source_target_pairs={{0,4},{1,5},{2,6},{3,7},{4,8},{5,9},{6,10},{7,11},{8,12},{9,13},{1... | collective-permute-start | bytes 1572872 | tf_op jit(solution)/shard_map/ppermute | solution.py:132
  82.6 14.9 %collective-permute-start.16 = (bf16[128,2048]{1,0:T(8,128)(2,1)S(1)}, bf16[128,2048]{1,0:T(8,128)(2,1)S(1)}, u32[]{:S(2)}, u32[]{:S(2)}) collective-permute-start(bf16[128,2048]{1,0:T(8,128)(2,1)S(1)} %get-tuple-element.66), channel_id=1, source_target_pairs={{0,2},{1,3},{2,0},{3,1},{4,6},{5,7},{6,4},{7,5},{8,10},{9,11},{10,... | collective-permute-start | bytes 1572872 | tf_op jit(solution)/shard_map/ppermute | solution.py:135
  86.3 23.5 %collective-permute-start.17 = (bf16[128,2176]{1,0:T(8,128)(2,1)S(1)}, bf16[128,2176]{1,0:T(8,128)(2,1)S(1)}, u32[]{:S(2)}, u32[]{:S(2)}) collective-permute-start(bf16[128,2176]{1,0:T(8,128)(2,1)S(1)} %collective-permute-done.6.refs_2_), channel_id=1, source_target_pairs={{0,4},{1,5},{2,6},{3,7},{4,8},{5,9},{6,10},{7,11},{8,12},{9,13},{1... | collective-permute-start | bytes 1671176 | tf_op jit(solution)/shard_map/ppermute | solution.py:132
  97.5 12.1 %collective-permute-start.18 = (bf16[128,2048]{1,0:T(8,128)(2,1)S(1)}, bf16[128,2048]{1,0:T(8,128)(2,1)S(1)}, u32[]{:S(2)}, u32[]{:S(2)}) collective-permute-start(bf16[128,2048]{1,0:T(8,128)(2,1)S(1)} %get-tuple-element.71), channel_id=1, source_target_pairs={{0,2},{1,3},{2,0},{3,1},{4,6},{5,7},{6,4},{7,5},{8,10},{9,11},{10,... | collective-permute-start | bytes 1572872 | tf_op jit(solution)/shard_map/ppermute | solution.py:135
  99.2 21.5 %collective-permute-start.20 = (bf16[128,2048]{1,0:T(8,128)(2,1)S(1)}, bf16[128,2048]{1,0:T(8,128)(2,1)S(1)}, u32[]{:S(2)}, u32[]{:S(2)}) collective-permute-start(bf16[128,2048]{1,0:T(8,128)(2,1)S(1)} %add_convert_fusion.1), channel_id=1, source_target_pairs={{0,12},{1,13},{2,14},{3,15},{4,0},{5,1},{6,2},{7,3},{8,4},{9,5},{1... | collective-permute-start | bytes 1572872 | tf_op jit(solution)/shard_map/ppermute | solution.py:132
  109.8 12.7 %collective-permute-start.21 = (bf16[128,2048]{1,0:T(8,128)(2,1)S(1)}, bf16[128,2048]{1,0:T(8,128)(2,1)S(1)}, u32[]{:S(2)}, u32[]{:S(2)}) collective-permute-start(bf16[128,2048]{1,0:T(8,128)(2,1)S(1)} %pair_rows.8), channel_id=1, source_target_pairs={{0,2},{1,3},{2,0},{3,1},{4,6},{5,7},{6,4},{7,5},{8,10},{9,11},{10,... | collective-permute-start | bytes 1572872 | tf_op jit(solution)/shard_map/ppermute | solution.py:135
  111.0 19.8 %collective-permute-start.22 = (bf16[128,2048]{1,0:T(8,128)(2,1)S(1)}, bf16[128,2048]{1,0:T(8,128)(2,1)S(1)}, u32[]{:S(2)}, u32[]{:S(2)}) collective-permute-start(bf16[128,2048]{1,0:T(8,128)(2,1)S(1)} %add_convert_fusion.2), channel_id=1, source_target_pairs={{0,4},{1,5},{2,6},{3,7},{4,8},{5,9},{6,10},{7,11},{8,12},{9,13},{1... | collective-permute-start | bytes 1572872 | tf_op jit(solution)/shard_map/ppermute | solution.py:132
  120.7 13.7 %collective-permute-start.19 = (bf16[128,2048]{1,0:T(8,128)(2,1)S(1)}, bf16[128,2048]{1,0:T(8,128)(2,1)S(1)}, u32[]{:S(2)}, u32[]{:S(2)}) collective-permute-start(bf16[128,2048]{1,0:T(8,128)(2,1)S(1)} %get-tuple-element.74), channel_id=1, source_target_pairs={{0,2},{1,3},{2,0},{3,1},{4,6},{5,7},{6,4},{7,5},{8,10},{9,11},{10,... | collective-permute-start | bytes 1572872 | tf_op jit(solution)/shard_map/ppermute | solution.py:135
  131.0 14.6 %collective-permute-start.23 = (bf16[128,2048]{1,0:T(8,128)(2,1)S(1)}, bf16[128,2048]{1,0:T(8,128)(2,1)S(1)}, u32[]{:S(2)}, u32[]{:S(2)}) collective-permute-start(bf16[128,2048]{1,0:T(8,128)(2,1)S(1)} %add_convert_fusion), channel_id=1, source_target_pairs={{0,4},{1,5},{2,6},{3,7},{4,8},{5,9},{6,10},{7,11},{8,12},{9,13},{1... | collective-permute-start | bytes 1572872 | tf_op jit(solution)/shard_map/ppermute | solution.py:132
  (8 other events, 87.2 us)

commit v6 on v5

--- a/solution.py
+++ b/solution.py
@@ -39,12 +39,12 @@
     )(ids.T, gates.T, grad)
 
 
-def pair_kernel(blocks, owners, wide, experts, *refs):
-    xs, gs = refs[:blocks], refs[blocks : 2 * blocks]
-    weights = refs[2 * blocks : 2 * blocks + 6]
-    outs = refs[2 * blocks + 6 : 3 * blocks + 6]
-    x_buf, g_buf, w_in, w_out, d_buf, sems = refs[3 * blocks + 6 :]
-    rows = xs[0].shape[0]
+def pair_kernel(pieces, blocks, owners, wide, experts, *refs):
+    xs, gs = refs[:pieces], refs[pieces : pieces + blocks]
+    refs = refs[pieces + blocks :]
+    weights, outs = refs[:6], refs[6 : 6 + blocks]
+    x_buf, g_buf, w_in, w_out, d_buf, sems = refs[6 + blocks :]
+    rows = gs[0].shape[0]
     width, hidden = weights[0].shape
     copies = {}
 
@@ -52,8 +52,10 @@
         copies[key] = pltpu.make_async_copy(source, target, sems.at[len(copies)])
         copies[key].start()
 
-    for i in range(blocks):
-        start(("x", i), xs[i], x_buf.at[pl.ds(i * rows, rows)])
+    at = 0
+    for i in range(pieces):
+        start(("x", i), xs[i], x_buf.at[pl.ds(at, xs[i].shape[0])])
+        at = at + xs[i].shape[0]
     start(("w", 0), weights[0], w_in.at[:, pl.ds(0, hidden)])
     start(("w", 1), weights[1], w_in.at[:, pl.ds(hidden, hidden)])
     for i in range(blocks):
@@ -62,7 +64,7 @@
     start(("w", 3), weights[3], w_in.at[:, pl.ds(2 * hidden, hidden)])
     start(("w", 4), weights[4], w_in.at[:, pl.ds(3 * hidden, hidden)])
     start(("w", 5), weights[5], w_out.at[pl.ds(hidden, hidden)])
-    for i in range(blocks):
+    for i in range(pieces):
         copies["x", i].wait()
     for k in range(2):
         at = 2 * k * hidden
@@ -73,10 +75,10 @@
         if k == 0:
             for i in range(blocks):
                 copies["g", i].wait()
-            pieces = g_buf[:, width:].astype(F32)
-            lane = lax.broadcasted_iota(jnp.int32, pieces.shape, 1)
+            parts = g_buf[:, width:].astype(F32)
+            lane = lax.broadcasted_iota(jnp.int32, parts.shape, 1)
         chosen = (lane == experts[k]) | (lane == experts[k] + owners) | (lane == experts[k] + 2 * owners)
-        gate = jnp.sum(jnp.where(chosen, pieces, 0.0), axis=1, keepdims=True)
+        gate = jnp.sum(jnp.where(chosen, parts, 0.0), axis=1, keepdims=True)
         scaled = (gate * g_buf[:, :width].astype(F32)).astype(BF16)
         copies["w", 3 * k + 2].wait()
         back = lax.dot_general(
@@ -93,15 +95,15 @@
 
 
 def pair_rows(xs, gs, owners, experts, weights, kinds):
-    blocks = len(xs)
-    rows, width = xs[0].shape
+    pieces, blocks = len(xs), len(gs)
+    rows, width = gs[0].shape[0], xs[0].shape[1]
     hidden = weights[0].shape[1]
     there = pl.BlockSpec(memory_space=pltpu.HBM)
     near = pl.BlockSpec(memory_space=pltpu.VMEM)
     count = blocks * rows
     return pl.pallas_call(
-        partial(pair_kernel, blocks, owners, 512 if width % 512 == 0 else width),
-        in_specs=[pl.BlockSpec(memory_space=pltpu.SMEM)] + [there] * (2 * blocks) + [pl.BlockSpec(memory_space=pl.ANY)] * 6,
+        partial(pair_kernel, pieces, blocks, owners, 512 if width % 512 == 0 else width),
+        in_specs=[pl.BlockSpec(memory_space=pltpu.SMEM)] + [there] * (pieces + blocks) + [pl.BlockSpec(memory_space=pl.ANY)] * 6,
         out_specs=[near] * blocks,
         out_shape=[jax.ShapeDtypeStruct((rows, width), kind) for kind in kinds],
         scratch_shapes=[
@@ -110,7 +112,7 @@
             pltpu.VMEM((width, 4 * hidden), BF16),
             pltpu.VMEM((2 * hidden, width), BF16),
             pltpu.VMEM((count, 4 * hidden), BF16),
-            pltpu.SemaphoreType.DMA((2 * blocks + 6,)),
+            pltpu.SemaphoreType.DMA((pieces + blocks + 6,)),
         ],
         compiler_params=pltpu.CompilerParams(vmem_limit_bytes=36 * 2**20),
         cost_estimate=pl.CostEstimate(
@@ -160,21 +162,22 @@
             fars.append(far)
         xs, gs, far_xs, far_gs = xs + [x], gs + [g], far_xs + [far_x], far_gs + [far_g]
 
-    beyond_x, beyond_g = turn(far_xs[0], -1), turn(far_gs[0], -1)
-    x, beyond_x = tie((xs[-1], beyond_x))
-    x = turn(x, 1)
-    g, beyond_g = tie((gs[-1], beyond_g))
-    g = turn(g, 1)
+    half = xs[0].shape[0] // 2
+    x_last, beyond_g = turn(xs[0], -1), turn(far_gs[0], -1)
+    far_x, x_last = tie((far_xs[0], x_last))
+    top, bottom = turn(far_x[:half], -1), swap(x_last[half:], 2)
+    g_last, beyond_g = tie((gs[0], beyond_g))
+    g_last = turn(g_last, -1)
     near, far = compute(ring - 3)
-    far_x, far_g, near, beyond_x, beyond_g = tie((swap(xs[-1], 2), swap(gs[-1], 2), near, beyond_x, beyond_g))
+    far_x, far_g, near, beyond_g = tie((swap(xs[-1], 2), swap(gs[-1], 2), near, beyond_g))
     far_xs, far_gs, nears, fars = far_xs + [far_x], far_gs + [far_g], nears + [near], fars + [far]
     backs = [swap(far, 2) for far in fars[1:]]
     near, far = compute(ring - 2)
-    near, far, beyond_x, x, backs = tie((near, far, beyond_x, x, backs))
-    (beyond,) = pair_rows((beyond_x,), (beyond_g,), owners, experts, weights, (BF16,))
+    near, far, top, bottom, backs = tie((near, far, top, bottom, backs))
+    (beyond,) = pair_rows((top, bottom), (beyond_g,), owners, experts, weights, (BF16,))
     sums = [None, *(near + back.astype(F32) for near, back in zip(nears[1:] + [near], backs + [swap(far, 2)]))]
     one, carried = turn(sums[1].astype(BF16), -1), sums[2].astype(BF16)
-    x, g, first, carried, beyond = tie((x, g, fars[0], carried, beyond))
+    x, g, first, carried, beyond = tie((x_last, g_last, fars[0], carried, beyond))
     (last,) = pair_rows((x,), (g,), owners, experts, weights, (F32,))
     last, one = tie((last, one))
 

time: 147 us -> 146 us (level)
  starting transfers between devices: 23 us -> 21 us
    ppermute x13 -> x14, waiting for transfers between devices: 29.4 us -> 40.7 us  [swap(): return lax.ppermute(value, 'expert', [(i, i ^ bit) for i in range(owners)])]
    ppermute x11, waiting for transfers between devices: 40.5 us -> 29.3 us  [turn(): lax.ppermute(value, 'expert', [(i, (i + 4 * by) % owners) for i in range(...]
    ppermute x13 -> x14, starting transfers between devices: 13 us -> 11.8 us  [swap(): return lax.ppermute(value, 'expert', [(i, i ^ bit) for i in range(owners)])]
    unnamed x16 -> x28, local copies, waits for them, and re-layouts: 6.88 us -> 7.9 us
  transfers between devices with their start and end apart: 24 -> 25, of which waited for: 13 -> 12; matrix products, arithmetic and copies ran while one was open for 0% -> 0% of each run, Pallas kernels for 31% -> 31%
where the time goes in v6:
time: 146 us
  waiting for transfers between devices  70 us (48%)
  Pallas kernels  44.7 us (31%)
  starting transfers between devices  21 us (14%)
  local copies, waits for them, and re-layouts  7.93 us (5%)
  other arithmetic  1.71 us (1%)
    pallas_call x5, Pallas kernels, pair_rows(): pl.pallas_call(partial(pair_kernel, pieces, blocks, owners, 512 if width...  42.7 us
    ppermute x14, waiting for transfers between devices, swap(): return lax.ppermute(value, 'expert', [(i, i ^ bit) for i in range(owners)])  40.7 us
    ppermute x11, waiting for transfers between devices, turn(): lax.ppermute(value, 'expert', [(i, (i + 4 * by) % owners) for i in range(...  29.3 us
    ppermute x14, starting transfers between devices, swap(): return lax.ppermute(value, 'expert', [(i, i ^ bit) for i in range(owners)])  11.8 us
    ppermute x11, starting transfers between devices, turn(): lax.ppermute(value, 'expert', [(i, (i + 4 * by) % owners) for i in range(...  9.21 us
    unnamed x28, local copies, waits for them, and re-layouts  7.9 us
  transfers between devices with their start and end apart: 25, of which 12 were waited for; matrix products, arithmetic and copies ran while one was open for 0% of the time, Pallas kernels for 31%

profile of v6, /device:TPU:0, one launch (start us, length us, event | category | flops | bytes accessed | tf_op | source)
XLA Modules:
  0.0 145.5 jit_solution(16341799248079782625)
XLA Ops:
  0.5 2.0 %gated_rows.1.refs_2_ = bf16[128,2176]{1,0:T(8,128)(2,1)} custom-call(s32[8,128]{1,0:T(8,128)} %bitcast.25, f32[8,128]{1,0:T(8,128)} %bitcast.26, bf16[128,2048]{1,0:T(8,128)(2,1)} %grad.1), custom_call_target="tpu_custom_call" | custom-call | tf_op jit(solution)/shard_map/gated_rows/pallas_call | solution.py:33
  2.4 2.5 %collective-permute-start.2 = (bf16[128,2176]{1,0:T(8,128)(2,1)}, bf16[128,2176]{1,0:T(8,128)(2,1)S(1)}, u32[]{:S(2)}, u32[]{:S(2)}) collective-permute-start(bf16[128,2176]{1,0:T(8,128)(2,1)} %gated_rows.1.refs_2_), channel_id=1, source_target_pairs={{0,2},{1,3},{2,0},{3,1},{4,6},{5,7},{6,4},{7,5},{8,10},{9,11},{10,... | collective-permute-start | bytes 1671176 | tf_op jit(solution)/shard_map/ppermute | solution.py:137
  8.6 21.1 %collective-permute-done.refs_1_ = bf16[128,2048]{1,0:T(8,128)(2,1)S(1)} collective-permute-done((bf16[128,2048]{1,0:T(8,128)(2,1)}, bf16[128,2048]{1,0:T(8,128)(2,1)S(1)}, u32[]{:S(2)}, u32[]{:S(2)}) %collective-permute-start) | collective-permute-done | bytes 524320 | tf_op jit(solution)/shard_map/ppermute | solution.py:137
  29.7 3.4 %collective-permute-done.1.refs_0_ = bf16[128,2048]{1,0:T(8,128)(2,1)S(1)} collective-permute-done((bf16[128,2048]{1,0:T(8,128)(2,1)}, bf16[128,2048]{1,0:T(8,128)(2,1)S(1)}, u32[]{:S(2)}, u32[]{:S(2)}) %collective-permute-start.1) | collective-permute-done | bytes 524320 | tf_op jit(solution)/shard_map/ppermute | solution.py:134
  36.7 1.9 %collective-permute-done.7.refs_8_.refs_7_.refs_6_ = bf16[2048,512]{1,0:T(8,128)(2,1)} collective-permute-done((bf16[2048,512]{1,0:T(8,128)(2,1)}, bf16[2048,512]{1,0:T(8,128)(2,1)}, u32[]{:S(2)}, u32[]{:S(2)}) %collective-permute-start.7) | collective-permute-done | bytes 2097184 | tf_op jit(solution)/shard_map/ppermute | solution.py:137
  38.6 3.0 %collective-permute-done.8.refs_9_.refs_8_.refs_7_ = bf16[512,2048]{1,0:T(8,128)(2,1)} collective-permute-done((bf16[512,2048]{1,0:T(8,128)(2,1)}, bf16[512,2048]{1,0:T(8,128)(2,1)}, u32[]{:S(2)}, u32[]{:S(2)}) %collective-permute-start.8) | collective-permute-done | bytes 2097184 | tf_op jit(solution)/shard_map/ppermute | solution.py:137
  41.6 1.7 %collective-permute-start.10 = (bf16[128,2176]{1,0:T(8,128)(2,1)S(1)}, bf16[128,2176]{1,0:T(8,128)(2,1)S(1)}, u32[]{:S(2)}, u32[]{:S(2)}) collective-permute-start(bf16[128,2176]{1,0:T(8,128)(2,1)S(1)} %collective-permute-done.2.refs_3_), channel_id=1, source_target_pairs={{0,12},{1,13},{2,14},{3,15},{4,0},{5,1},{6,2},{7,3},{8,4},{9,5},{1... | collective-permute-start | bytes 1671176 | tf_op jit(solution)/shard_map/ppermute | solution.py:134
  43.3 1.6 %copy-done = bf16[1,2048,512]{2,1,0:T(8,128)(2,1)S(1)} copy-done((bf16[1,2048,512]{2,1,0:T(8,128)(2,1)S(1)}, bf16[1,2048,512]{2,1,0:T(8,128)(2,1)}, u32[]{:S(2)}) %copy-start) | copy-done | bytes 2097176
  44.9 1.6 %copy-done.2 = bf16[1,2048,512]{2,1,0:T(8,128)(2,1)S(1)} copy-done((bf16[1,2048,512]{2,1,0:T(8,128)(2,1)S(1)}, bf16[1,2048,512]{2,1,0:T(8,128)(2,1)}, u32[]{:S(2)}) %copy-start.2) | copy-done | bytes 2097176
  46.5 1.6 %copy-done.4 = bf16[1,512,2048]{2,1,0:T(8,128)(2,1)S(1)} copy-done((bf16[1,512,2048]{2,1,0:T(8,128)(2,1)S(1)}, bf16[1,512,2048]{2,1,0:T(8,128)(2,1)}, u32[]{:S(2)}) %copy-start.4) | copy-done | bytes 2097176
  50.2 8.9 %pair_rows.5 = (f32[128,2048]{1,0:T(8,128)S(1)}, bf16[128,2048]{1,0:T(8,128)(2,1)S(1)}) custom-call(s32[2]{0:T(128)S(1)} %pad_add_fusion.experts, bf16[128,2048]{1,0:T(8,128)(2,1)S(1)} %copy-done.10, bf16[128,2048]{1,0:T(8,128)(2,1)S(1)} %collective-permute-done.refs_1_, bf16[128,2176]{1,0:T(8,128)(2,1)S(1)} %copy-done.6, ...), custom_call_target="tpu_custom_call" | custom-call | flops 5368709120 | bytes 16252928 | tf_op jit(solution)/shard_map/pair_rows/pallas_call | solution.py:104
  60.6 3.4 %collective-permute-done.13.refs_0_ = bf16[128,2048]{1,0:T(8,128)(2,1)S(1)} collective-permute-done((bf16[128,2048]{1,0:T(8,128)(2,1)}, bf16[128,2048]{1,0:T(8,128)(2,1)S(1)}, u32[]{:S(2)}, u32[]{:S(2)}) %collective-permute-start.13) | collective-permute-done | bytes 524320 | tf_op jit(solution)/shard_map/ppermute | solution.py:134
  65.5 8.9 %pair_rows.6 = (f32[128,2048]{1,0:T(8,128)S(1)}, bf16[128,2048]{1,0:T(8,128)(2,1)S(1)}) custom-call(s32[2]{0:T(128)S(1)} %pad_add_fusion.experts, bf16[128,2048]{1,0:T(8,128)(2,1)S(1)} %copy-done.13, bf16[128,2048]{1,0:T(8,128)(2,1)S(1)} %collective-permute-done.12.refs_1_, bf16[128,2176]{1,0:T(8,128)(2,1)S(1)} %copy-done.9, ...), custom_call_target="tpu_custom_call" | custom-call | flops 5368709120 | bytes 16252928 | tf_op jit(solution)/shard_map/pair_rows/pallas_call | solution.py:104
  74.9 10.9 %collective-permute-done.9.refs_0_ = bf16[128,2048]{1,0:T(8,128)(2,1)S(1)} collective-permute-done((bf16[128,2048]{1,0:T(8,128)(2,1)S(1)}, bf16[128,2048]{1,0:T(8,128)(2,1)S(1)}, u32[]{:S(2)}, u32[]{:S(2)}) %collective-permute-start.9) | collective-permute-done | bytes 524320 | tf_op jit(solution)/shard_map/ppermute | solution.py:134
  85.9 1.6 %collective-permute-start.17 = (bf16[64,2048]{1,0:T(8,128)(2,1)S(1)}, bf16[64,2048]{1,0:T(8,128)(2,1)S(1)}, u32[]{:S(2)}, u32[]{:S(2)}) collective-permute-start(bf16[64,2048]{1,0:T(8,128)(2,1)S(1)} %slice.7), channel_id=1, source_target_pairs={{0,2},{1,3},{2,0},{3,1},{4,6},{5,7},{6,4},{7,5},{8,10},{9,11},{10,... | collective-permute-start | bytes 786440 | tf_op jit(solution)/shard_map/ppermute | solution.py:137
  87.8 1.8 %collective-permute-start.11 = (bf16[128,2176]{1,0:T(8,128)(2,1)S(1)}, bf16[128,2176]{1,0:T(8,128)(2,1)S(1)}, u32[]{:S(2)}, u32[]{:S(2)}) collective-permute-start(bf16[128,2176]{1,0:T(8,128)(2,1)S(1)} %copy-done.7), channel_id=1, source_target_pairs={{0,12},{1,13},{2,14},{3,15},{4,0},{5,1},{6,2},{7,3},{8,4},{9,5},{1... | collective-permute-start | bytes 1671176 | tf_op jit(solution)/shard_map/ppermute | solution.py:134
  89.6 8.9 %pair_rows.7 = (f32[128,2048]{1,0:T(8,128)S(1)}, bf16[128,2048]{1,0:T(8,128)(2,1)S(1)}) custom-call(s32[2]{0:T(128)S(1)} %pad_add_fusion.experts, bf16[128,2048]{1,0:T(8,128)(2,1)S(1)} %collective-permute-done.13.refs_0_, bf16[128,2048]{1,0:T(8,128)(2,1)S(1)} %collective-permute-done.14.refs_1_, bf16[128,2176]{1,0:T(8,128)(2,1)S(1)} %collective-permute-done.6.refs_2_, ...), custom_call_target="tpu_custom_call" | custom-call | flops 5368709120 | bytes 16252928 | tf_op jit(solution)/shard_map/pair_rows/pallas_call | solution.py:104
  98.5 3.2 %collective-permute-done.17.refs_1_ = bf16[64,2048]{1,0:T(8,128)(2,1)S(1)} collective-permute-done((bf16[64,2048]{1,0:T(8,128)(2,1)S(1)}, bf16[64,2048]{1,0:T(8,128)(2,1)S(1)}, u32[]{:S(2)}, u32[]{:S(2)}) %collective-permute-start.17) | collective-permute-done | bytes 262176 | tf_op jit(solution)/shard_map/ppermute | solution.py:137
  103.2 8.1 %pair_rows.8 = bf16[128,2048]{1,0:T(8,128)(2,1)S(1)} custom-call(s32[2]{0:T(128)S(1)} %pad_add_fusion.experts, bf16[64,2048]{1,0:T(8,128)(2,1)S(1)} %collective-permute-done.16.refs_0_, bf16[64,2048]{1,0:T(8,128)(2,1)S(1)} %collective-permute-done.17.refs_1_, bf16[128,2176]{1,0:T(8,128)(2,1)S(1)} %collective-permute-done.10.refs_2_, ...), custom_call_target="tpu_custom_call" | custom-call | flops 2684354560 | bytes 14417920 | tf_op jit(solution)/shard_map/pair_rows/pallas_call | solution.py:104
  111.3 3.2 %collective-permute-done.19 = bf16[128,2048]{1,0:T(8,128)(2,1)S(1)} collective-permute-done((bf16[128,2048]{1,0:T(8,128)(2,1)S(1)}, bf16[128,2048]{1,0:T(8,128)(2,1)S(1)}, u32[]{:S(2)}, u32[]{:S(2)}) %collective-permute-start.19) | collective-permute-done | bytes 524320 | tf_op jit(solution)/shard_map/ppermute | solution.py:137
  115.5 8.1 %pair_rows.9 = f32[128,2048]{1,0:T(8,128)S(1)} custom-call(s32[2]{0:T(128)S(1)} %pad_add_fusion.experts, bf16[128,2048]{1,0:T(8,128)(2,1)S(1)} %collective-permute-done.9.refs_0_, bf16[128,2176]{1,0:T(8,128)(2,1)S(1)} %collective-permute-done.11.refs_1_, bf16[2048,512]{1,0:T(8,128)(2,1)S(1)} %bitcast.12, bf16[2048,512]{1,0:T(8,128)(2,1)S(1)} %bitcast.18, ...), custom_call_target="tpu_custom_call" | custom-call | flops 2684354560 | bytes 14417920 | tf_op jit(solution)/shard_map/pair_rows/pallas_call | solution.py:104
  123.5 6.4 %collective-permute-done.21 = bf16[128,2048]{1,0:T(8,128)(2,1)S(1)} collective-permute-done((bf16[128,2048]{1,0:T(8,128)(2,1)S(1)}, bf16[128,2048]{1,0:T(8,128)(2,1)S(1)}, u32[]{:S(2)}, u32[]{:S(2)}) %collective-permute-start.21) | collective-permute-done | bytes 524320 | tf_op jit(solution)/shard_map/ppermute | solution.py:134
  131.2 7.9 %collective-permute-done.20 = bf16[128,2048]{1,0:T(8,128)(2,1)S(1)} collective-permute-done((bf16[128,2048]{1,0:T(8,128)(2,1)S(1)}, bf16[128,2048]{1,0:T(8,128)(2,1)S(1)}, u32[]{:S(2)}, u32[]{:S(2)}) %collective-permute-start.20) | collective-permute-done | bytes 524320 | tf_op jit(solution)/shard_map/ppermute | solution.py:137
  139.1 5.2 %collective-permute-done.24 = bf16[128,2048]{1,0:T(8,128)(2,1)S(1)} collective-permute-done((bf16[128,2048]{1,0:T(8,128)(2,1)S(1)}, bf16[128,2048]{1,0:T(8,128)(2,1)S(1)}, u32[]{:S(2)}, u32[]{:S(2)}) %collective-permute-start.24) | collective-permute-done | bytes 524320 | tf_op jit(solution)/shard_map/ppermute | solution.py:134
  (67 shorter events, 18.8 us)
Async XLA Ops:
  0.0 33.1 %collective-permute-start.4 = (bf16[2048,512]{1,0:T(8,128)(2,1)}, bf16[2048,512]{1,0:T(8,128)(2,1)S(1)}, u32[]{:S(2)}, u32[]{:S(2)}) collective-permute-start(bf16[2048,512]{1,0:T(8,128)(2,1)} %bitcast.7), channel_id=1, source_target_pairs={{0,1},{1,0},{2,3},{3,2},{4,5},{5,4},{6,7},{7,6},{8,9},{9,8},{10,11... | collective-permute-start | bytes 6291464 | tf_op jit(solution)/shard_map/ppermute | solution.py:137
  2.4 30.6 %collective-permute-start.2 = (bf16[128,2176]{1,0:T(8,128)(2,1)}, bf16[128,2176]{1,0:T(8,128)(2,1)S(1)}, u32[]{:S(2)}, u32[]{:S(2)}) collective-permute-start(bf16[128,2176]{1,0:T(8,128)(2,1)} %gated_rows.1.refs_2_), channel_id=1, source_target_pairs={{0,2},{1,3},{2,0},{3,1},{4,6},{5,7},{6,4},{7,5},{8,10},{9,11},{10,... | collective-permute-start | bytes 1671176 | tf_op jit(solution)/shard_map/ppermute | solution.py:137
  5.0 28.1 %collective-permute-start.3 = (bf16[128,2176]{1,0:T(8,128)(2,1)}, bf16[128,2176]{1,0:T(8,128)(2,1)S(1)}, u32[]{:S(2)}, u32[]{:S(2)}) collective-permute-start(bf16[128,2176]{1,0:T(8,128)(2,1)} %gated_rows.1.refs_2_), channel_id=1, source_target_pairs={{0,4},{1,5},{2,6},{3,7},{4,8},{5,9},{6,10},{7,11},{8,12},{9,13},{1... | collective-permute-start | bytes 1671176 | tf_op jit(solution)/shard_map/ppermute | solution.py:134
  6.5 23.2 %collective-permute-start = (bf16[128,2048]{1,0:T(8,128)(2,1)}, bf16[128,2048]{1,0:T(8,128)(2,1)S(1)}, u32[]{:S(2)}, u32[]{:S(2)}) collective-permute-start(bf16[128,2048]{1,0:T(8,128)(2,1)} %refs_0_.1), channel_id=1, source_target_pairs={{0,2},{1,3},{2,0},{3,1},{4,6},{5,7},{6,4},{7,5},{8,10},{9,11},{10,... | collective-permute-start | bytes 1572872 | tf_op jit(solution)/shard_map/ppermute | solution.py:137
  7.0 26.0 %collective-permute-start.1 = (bf16[128,2048]{1,0:T(8,128)(2,1)}, bf16[128,2048]{1,0:T(8,128)(2,1)S(1)}, u32[]{:S(2)}, u32[]{:S(2)}) collective-permute-start(bf16[128,2048]{1,0:T(8,128)(2,1)} %refs_0_.1), channel_id=1, source_target_pairs={{0,4},{1,5},{2,6},{3,7},{4,8},{5,9},{6,10},{7,11},{8,12},{9,13},{1... | collective-permute-start | bytes 1572872 | tf_op jit(solution)/shard_map/ppermute | solution.py:134
  34.1 7.5 %collective-permute-start.8 = (bf16[512,2048]{1,0:T(8,128)(2,1)}, bf16[512,2048]{1,0:T(8,128)(2,1)}, u32[]{:S(2)}, u32[]{:S(2)}) collective-permute-start(bf16[512,2048]{1,0:T(8,128)(2,1)} %bitcast.19), channel_id=1, source_target_pairs={{0,1},{1,0},{2,3},{3,2},{4,5},{5,4},{6,7},{7,6},{8,9},{9,8},{10,11... | collective-permute-start | bytes 6291464 | tf_op jit(solution)/shard_map/ppermute | solution.py:137
  34.6 24.5 %collective-permute-start.5 = (bf16[128,2176]{1,0:T(8,128)(2,1)}, bf16[128,2176]{1,0:T(8,128)(2,1)S(1)}, u32[]{:S(2)}, u32[]{:S(2)}) collective-permute-start(bf16[128,2176]{1,0:T(8,128)(2,1)} %copy-done.8), channel_id=1, source_target_pairs={{0,2},{1,3},{2,0},{3,1},{4,6},{5,7},{6,4},{7,5},{8,10},{9,11},{10,... | collective-permute-start | bytes 1671176 | tf_op jit(solution)/shard_map/ppermute | solution.py:137
  35.1 24.0 %collective-permute-start.6 = (bf16[128,2176]{1,0:T(8,128)(2,1)}, bf16[128,2176]{1,0:T(8,128)(2,1)S(1)}, u32[]{:S(2)}, u32[]{:S(2)}) collective-permute-start(bf16[128,2176]{1,0:T(8,128)(2,1)} %copy-done.8), channel_id=1, source_target_pairs={{0,4},{1,5},{2,6},{3,7},{4,8},{5,9},{6,10},{7,11},{8,12},{9,13},{1... | collective-permute-start | bytes 1671176 | tf_op jit(solution)/shard_map/ppermute | solution.py:134
  35.2 25.4 %collective-permute-start.12 = (bf16[128,2048]{1,0:T(8,128)(2,1)}, bf16[128,2048]{1,0:T(8,128)(2,1)S(1)}, u32[]{:S(2)}, u32[]{:S(2)}) collective-permute-start(bf16[128,2048]{1,0:T(8,128)(2,1)} %copy-done.12), channel_id=1, source_target_pairs={{0,2},{1,3},{2,0},{3,1},{4,6},{5,7},{6,4},{7,5},{8,10},{9,11},{10,... | collective-permute-start | bytes 1572872 | tf_op jit(solution)/shard_map/ppermute | solution.py:137
  38.6 25.4 %collective-permute-start.13 = (bf16[128,2048]{1,0:T(8,128)(2,1)}, bf16[128,2048]{1,0:T(8,128)(2,1)S(1)}, u32[]{:S(2)}, u32[]{:S(2)}) collective-permute-start(bf16[128,2048]{1,0:T(8,128)(2,1)} %copy-done.12), channel_id=1, source_target_pairs={{0,4},{1,5},{2,6},{3,7},{4,8},{5,9},{6,10},{7,11},{8,12},{9,13},{1... | collective-permute-start | bytes 1572872 | tf_op jit(solution)/shard_map/ppermute | solution.py:134
  41.6 45.9 %collective-permute-start.10 = (bf16[128,2176]{1,0:T(8,128)(2,1)S(1)}, bf16[128,2176]{1,0:T(8,128)(2,1)S(1)}, u32[]{:S(2)}, u32[]{:S(2)}) collective-permute-start(bf16[128,2176]{1,0:T(8,128)(2,1)S(1)} %collective-permute-done.2.refs_3_), channel_id=1, source_target_pairs={{0,12},{1,13},{2,14},{3,15},{4,0},{5,1},{6,2},{7,3},{8,4},{9,5},{1... | collective-permute-start | bytes 1671176 | tf_op jit(solution)/shard_map/ppermute | solution.py:134
  59.1 30.5 %collective-permute-start.15 = (bf16[128,2176]{1,0:T(8,128)(2,1)S(1)}, bf16[128,2176]{1,0:T(8,128)(2,1)S(1)}, u32[]{:S(2)}, u32[]{:S(2)}) collective-permute-start(bf16[128,2176]{1,0:T(8,128)(2,1)S(1)} %collective-permute-done.6.refs_2_), channel_id=1, source_target_pairs={{0,2},{1,3},{2,0},{3,1},{4,6},{5,7},{6,4},{7,5},{8,10},{9,11},{10,... | collective-permute-start | bytes 1671176 | tf_op jit(solution)/shard_map/ppermute | solution.py:137
  59.7 26.2 %collective-permute-start.9 = (bf16[128,2048]{1,0:T(8,128)(2,1)S(1)}, bf16[128,2048]{1,0:T(8,128)(2,1)S(1)}, u32[]{:S(2)}, u32[]{:S(2)}) collective-permute-start(bf16[128,2048]{1,0:T(8,128)(2,1)S(1)} %copy-done.11), channel_id=1, source_target_pairs={{0,12},{1,13},{2,14},{3,15},{4,0},{5,1},{6,2},{7,3},{8,4},{9,5},{1... | collective-permute-start | bytes 1572872 | tf_op jit(solution)/shard_map/ppermute | solution.py:134
  64.0 23.8 %collective-permute-start.14 = (bf16[128,2048]{1,0:T(8,128)(2,1)S(1)}, bf16[128,2048]{1,0:T(8,128)(2,1)S(1)}, u32[]{:S(2)}, u32[]{:S(2)}) collective-permute-start(bf16[128,2048]{1,0:T(8,128)(2,1)S(1)} %collective-permute-done.13.refs_0_), channel_id=1, source_target_pairs={{0,2},{1,3},{2,0},{3,1},{4,6},{5,7},{6,4},{7,5},{8,10},{9,11},{10,... | collective-permute-start | bytes 1572872 | tf_op jit(solution)/shard_map/ppermute | solution.py:137
  74.3 27.3 %collective-permute-start.18 = (bf16[128,2048]{1,0:T(8,128)(2,1)S(1)}, bf16[128,2048]{1,0:T(8,128)(2,1)S(1)}, u32[]{:S(2)}, u32[]{:S(2)}) collective-permute-start(bf16[128,2048]{1,0:T(8,128)(2,1)S(1)} %get-tuple-element.66), channel_id=1, source_target_pairs={{0,2},{1,3},{2,0},{3,1},{4,6},{5,7},{6,4},{7,5},{8,10},{9,11},{10,... | collective-permute-start | bytes 1572872 | tf_op jit(solution)/shard_map/ppermute | solution.py:137
  85.9 15.8 %collective-permute-start.17 = (bf16[64,2048]{1,0:T(8,128)(2,1)S(1)}, bf16[64,2048]{1,0:T(8,128)(2,1)S(1)}, u32[]{:S(2)}, u32[]{:S(2)}) collective-permute-start(bf16[64,2048]{1,0:T(8,128)(2,1)S(1)} %slice.7), channel_id=1, source_target_pairs={{0,2},{1,3},{2,0},{3,1},{4,6},{5,7},{6,4},{7,5},{8,10},{9,11},{10,... | collective-permute-start | bytes 786440 | tf_op jit(solution)/shard_map/ppermute | solution.py:137
  87.5 14.2 %collective-permute-start.16 = (bf16[64,2048]{1,0:T(8,128)(2,1)S(1)}, bf16[64,2048]{1,0:T(8,128)(2,1)S(1)}, u32[]{:S(2)}, u32[]{:S(2)}) collective-permute-start(bf16[64,2048]{1,0:T(8,128)(2,1)S(1)} %slice.6), channel_id=1, source_target_pairs={{0,12},{1,13},{2,14},{3,15},{4,0},{5,1},{6,2},{7,3},{8,4},{9,5},{1... | collective-permute-start | bytes 786440 | tf_op jit(solution)/shard_map/ppermute | solution.py:134
  87.8 26.8 %collective-permute-start.11 = (bf16[128,2176]{1,0:T(8,128)(2,1)S(1)}, bf16[128,2176]{1,0:T(8,128)(2,1)S(1)}, u32[]{:S(2)}, u32[]{:S(2)}) collective-permute-start(bf16[128,2176]{1,0:T(8,128)(2,1)S(1)} %copy-done.7), channel_id=1, source_target_pairs={{0,12},{1,13},{2,14},{3,15},{4,0},{5,1},{6,2},{7,3},{8,4},{9,5},{1... | collective-permute-start | bytes 1671176 | tf_op jit(solution)/shard_map/ppermute | solution.py:134
  101.7 12.8 %collective-permute-start.19 = (bf16[128,2048]{1,0:T(8,128)(2,1)S(1)}, bf16[128,2048]{1,0:T(8,128)(2,1)S(1)}, u32[]{:S(2)}, u32[]{:S(2)}) collective-permute-start(bf16[128,2048]{1,0:T(8,128)(2,1)S(1)} %get-tuple-element.68), channel_id=1, source_target_pairs={{0,2},{1,3},{2,0},{3,1},{4,6},{5,7},{6,4},{7,5},{8,10},{9,11},{10,... | collective-permute-start | bytes 1572872 | tf_op jit(solution)/shard_map/ppermute | solution.py:137
  102.3 27.6 %collective-permute-start.21 = (bf16[128,2048]{1,0:T(8,128)(2,1)S(1)}, bf16[128,2048]{1,0:T(8,128)(2,1)S(1)}, u32[]{:S(2)}, u32[]{:S(2)}) collective-permute-start(bf16[128,2048]{1,0:T(8,128)(2,1)S(1)} %add_convert_fusion.1), channel_id=1, source_target_pairs={{0,12},{1,13},{2,14},{3,15},{4,0},{5,1},{6,2},{7,3},{8,4},{9,5},{1... | collective-permute-start | bytes 1572872 | tf_op jit(solution)/shard_map/ppermute | solution.py:134
  114.6 15.8 %collective-permute-start.22 = (bf16[128,2048]{1,0:T(8,128)(2,1)S(1)}, bf16[128,2048]{1,0:T(8,128)(2,1)S(1)}, u32[]{:S(2)}, u32[]{:S(2)}) collective-permute-start(bf16[128,2048]{1,0:T(8,128)(2,1)S(1)} %pair_rows.8), channel_id=1, source_target_pairs={{0,2},{1,3},{2,0},{3,1},{4,6},{5,7},{6,4},{7,5},{8,10},{9,11},{10,... | collective-permute-start | bytes 1572872 | tf_op jit(solution)/shard_map/ppermute | solution.py:137
  115.1 15.3 %collective-permute-start.23 = (bf16[128,2048]{1,0:T(8,128)(2,1)S(1)}, bf16[128,2048]{1,0:T(8,128)(2,1)S(1)}, u32[]{:S(2)}, u32[]{:S(2)}) collective-permute-start(bf16[128,2048]{1,0:T(8,128)(2,1)S(1)} %add_convert_fusion.2), channel_id=1, source_target_pairs={{0,4},{1,5},{2,6},{3,7},{4,8},{5,9},{6,10},{7,11},{8,12},{9,13},{1... | collective-permute-start | bytes 1572872 | tf_op jit(solution)/shard_map/ppermute | solution.py:134
  129.9 9.2 %collective-permute-start.20 = (bf16[128,2048]{1,0:T(8,128)(2,1)S(1)}, bf16[128,2048]{1,0:T(8,128)(2,1)S(1)}, u32[]{:S(2)}, u32[]{:S(2)}) collective-permute-start(bf16[128,2048]{1,0:T(8,128)(2,1)S(1)} %get-tuple-element.72), channel_id=1, source_target_pairs={{0,2},{1,3},{2,0},{3,1},{4,6},{5,7},{6,4},{7,5},{8,10},{9,11},{10,... | collective-permute-start | bytes 1572872 | tf_op jit(solution)/shard_map/ppermute | solution.py:137
  130.6 13.7 %collective-permute-start.24 = (bf16[128,2048]{1,0:T(8,128)(2,1)S(1)}, bf16[128,2048]{1,0:T(8,128)(2,1)S(1)}, u32[]{:S(2)}, u32[]{:S(2)}) collective-permute-start(bf16[128,2048]{1,0:T(8,128)(2,1)S(1)} %add_convert_fusion), channel_id=1, source_target_pairs={{0,4},{1,5},{2,6},{3,7},{4,8},{5,9},{6,10},{7,11},{8,12},{9,13},{1... | collective-permute-start | bytes 1572872 | tf_op jit(solution)/shard_map/ppermute | solution.py:134
  (15 other events, 158.4 us)

commit v7 on v6

--- a/solution.py
+++ b/solution.py
@@ -173,7 +173,7 @@
     far_xs, far_gs, nears, fars = far_xs + [far_x], far_gs + [far_g], nears + [near], fars + [far]
     backs = [swap(far, 2) for far in fars[1:]]
     near, far = compute(ring - 2)
-    near, far, top, bottom, backs = tie((near, far, top, bottom, backs))
+    near, far, top, bottom, backs, g_last = tie((near, far, top, bottom, backs, g_last))
     (beyond,) = pair_rows((top, bottom), (beyond_g,), owners, experts, weights, (BF16,))
     sums = [None, *(near + back.astype(F32) for near, back in zip(nears[1:] + [near], backs + [swap(far, 2)]))]
     one, carried = turn(sums[1].astype(BF16), -1), sums[2].astype(BF16)

time: 146 us -> 144 us (0.986)
  waiting for transfers between devices: 70 us -> 59.2 us
  starting transfers between devices: 21 us -> 30.6 us
    ppermute x11, waiting for transfers between devices: 29.3 us -> 18.5 us  [turn(): lax.ppermute(value, 'expert', [(i, (i + 4 * by) % owners) for i in range(...]
    ppermute x11, starting transfers between devices: 9.21 us -> 16.3 us  [turn(): lax.ppermute(value, 'expert', [(i, (i + 4 * by) % owners) for i in range(...]
    ppermute x14, starting transfers between devices: 11.8 us -> 14.3 us  [swap(): return lax.ppermute(value, 'expert', [(i, i ^ bit) for i in range(owners)])]
    unnamed x28 -> x20, local copies, waits for them, and re-layouts: 7.9 us -> 6.84 us
  transfers between devices with their start and end apart: 25 -> 25, of which waited for: 12 -> 10; matrix products, arithmetic and copies ran while one was open for 0% -> 0% of each run, Pallas kernels for 31% -> 31%
where the time goes in v7:
time: 144 us; the launch traced here: 143 us
  waiting for transfers between devices  59.2 us (41%)
  Pallas kernels  44.8 us (31%)
  starting transfers between devices  30.6 us (21%)
  local copies, waits for them, and re-layouts  6.88 us (5%)
  other arithmetic  1.72 us (1%)
    pallas_call x5, Pallas kernels, pair_rows(): pl.pallas_call(partial(pair_kernel, pieces, blocks, owners, 512 if width...  42.8 us
    ppermute x14, waiting for transfers between devices, swap(): return lax.ppermute(value, 'expert', [(i, i ^ bit) for i in range(owners)])  40.7 us
    ppermute x11, waiting for transfers between devices, turn(): lax.ppermute(value, 'expert', [(i, (i + 4 * by) % owners) for i in range(...  18.5 us
    ppermute x11, starting transfers between devices, turn(): lax.ppermute(value, 'expert', [(i, (i + 4 * by) % owners) for i in range(...  16.3 us
    ppermute x14, starting transfers between devices, swap(): return lax.ppermute(value, 'expert', [(i, i ^ bit) for i in range(owners)])  14.3 us
    unnamed x20, local copies, waits for them, and re-layouts  6.84 us
  transfers between devices with their start and end apart: 25, of which 10 were waited for; matrix products, arithmetic and copies ran while one was open for 0% of the time, Pallas kernels for 31%

profile of v7, /device:TPU:0, one launch (start us, length us, event | category | flops | bytes accessed | tf_op | source)
XLA Modules:
  0.0 143.4 jit_solution(15422737213083845592)
XLA Ops:
  0.5 2.0 %gated_rows.1.refs_2_ = bf16[128,2176]{1,0:T(8,128)(2,1)} custom-call(s32[8,128]{1,0:T(8,128)} %bitcast.25, f32[8,128]{1,0:T(8,128)} %bitcast.26, bf16[128,2048]{1,0:T(8,128)(2,1)} %grad.1), custom_call_target="tpu_custom_call" | custom-call | tf_op jit(solution)/shard_map/gated_rows/pallas_call | solution.py:33
  2.4 2.5 %collective-permute-start.2 = (bf16[128,2176]{1,0:T(8,128)(2,1)}, bf16[128,2176]{1,0:T(8,128)(2,1)S(1)}, u32[]{:S(2)}, u32[]{:S(2)}) collective-permute-start(bf16[128,2176]{1,0:T(8,128)(2,1)} %gated_rows.1.refs_2_), channel_id=1, source_target_pairs={{0,2},{1,3},{2,0},{3,1},{4,6},{5,7},{6,4},{7,5},{8,10},{9,11},{10,... | collective-permute-start | bytes 1671176 | tf_op jit(solution)/shard_map/ppermute | solution.py:137
  5.0 1.6 %collective-permute-start.3 = (bf16[128,2176]{1,0:T(8,128)(2,1)}, bf16[128,2176]{1,0:T(8,128)(2,1)S(1)}, u32[]{:S(2)}, u32[]{:S(2)}) collective-permute-start(bf16[128,2176]{1,0:T(8,128)(2,1)} %gated_rows.1.refs_2_), channel_id=1, source_target_pairs={{0,4},{1,5},{2,6},{3,7},{4,8},{5,9},{6,10},{7,11},{8,12},{9,13},{1... | collective-permute-start | bytes 1671176 | tf_op jit(solution)/shard_map/ppermute | solution.py:134
  8.6 21.1 %collective-permute-done.refs_1_ = bf16[128,2048]{1,0:T(8,128)(2,1)S(1)} collective-permute-done((bf16[128,2048]{1,0:T(8,128)(2,1)}, bf16[128,2048]{1,0:T(8,128)(2,1)S(1)}, u32[]{:S(2)}, u32[]{:S(2)}) %collective-permute-start) | collective-permute-done | bytes 524320 | tf_op jit(solution)/shard_map/ppermute | solution.py:137
  29.7 3.4 %collective-permute-done.1.refs_0_ = bf16[128,2048]{1,0:T(8,128)(2,1)S(1)} collective-permute-done((bf16[128,2048]{1,0:T(8,128)(2,1)}, bf16[128,2048]{1,0:T(8,128)(2,1)S(1)}, u32[]{:S(2)}, u32[]{:S(2)}) %collective-permute-start.1) | collective-permute-done | bytes 524320 | tf_op jit(solution)/shard_map/ppermute | solution.py:134
  35.1 3.8 %collective-permute-start.14 = (bf16[128,2176]{1,0:T(8,128)(2,1)}, bf16[128,2176]{1,0:T(8,128)(2,1)S(1)}, u32[]{:S(2)}, u32[]{:S(2)}) collective-permute-start(bf16[128,2176]{1,0:T(8,128)(2,1)} %copy-done.6), channel_id=1, source_target_pairs={{0,12},{1,13},{2,14},{3,15},{4,0},{5,1},{6,2},{7,3},{8,4},{9,5},{1... | collective-permute-start | bytes 1671176 | tf_op jit(solution)/shard_map/ppermute | solution.py:134
  41.6 1.6 %copy-done = bf16[1,2048,512]{2,1,0:T(8,128)(2,1)S(1)} copy-done((bf16[1,2048,512]{2,1,0:T(8,128)(2,1)S(1)}, bf16[1,2048,512]{2,1,0:T(8,128)(2,1)}, u32[]{:S(2)}) %copy-start) | copy-done | bytes 2097176
  43.2 1.6 %copy-done.2 = bf16[1,2048,512]{2,1,0:T(8,128)(2,1)S(1)} copy-done((bf16[1,2048,512]{2,1,0:T(8,128)(2,1)S(1)}, bf16[1,2048,512]{2,1,0:T(8,128)(2,1)}, u32[]{:S(2)}) %copy-start.2) | copy-done | bytes 2097176
  44.8 1.6 %copy-done.4 = bf16[1,512,2048]{2,1,0:T(8,128)(2,1)S(1)} copy-done((bf16[1,512,2048]{2,1,0:T(8,128)(2,1)S(1)}, bf16[1,512,2048]{2,1,0:T(8,128)(2,1)}, u32[]{:S(2)}) %copy-start.4) | copy-done | bytes 2097176
  47.4 8.9 %pair_rows.5 = (f32[128,2048]{1,0:T(8,128)S(1)}, bf16[128,2048]{1,0:T(8,128)(2,1)S(1)}) custom-call(s32[2]{0:T(128)S(1)} %pad_add_fusion.experts, bf16[128,2048]{1,0:T(8,128)(2,1)} %refs_0_.1, bf16[128,2048]{1,0:T(8,128)(2,1)S(1)} %collective-permute-done.refs_1_, bf16[128,2176]{1,0:T(8,128)(2,1)} %gated_rows.1.refs_2_, bf16[128,2176]{1,0:T(8,128)(2,1)S(1)} %copy-done.7, ...), custom_call_target="tpu_custom_call" | custom-call | flops 5368709120 | bytes 16252928 | tf_op jit(solution)/shard_map/pair_rows/pallas_call | solution.py:104
  57.0 8.7 %collective-permute-start.9 = (bf16[128,2048]{1,0:T(8,128)(2,1)}, bf16[128,2048]{1,0:T(8,128)(2,1)S(1)}, u32[]{:S(2)}, u32[]{:S(2)}) collective-permute-start(bf16[128,2048]{1,0:T(8,128)(2,1)} %refs_0_.1), channel_id=1, source_target_pairs={{0,12},{1,13},{2,14},{3,15},{4,0},{5,1},{6,2},{7,3},{8,4},{9,5},{1... | collective-permute-start | bytes 1572872 | tf_op jit(solution)/shard_map/ppermute | solution.py:134
  65.7 9.9 %collective-permute-done.11.refs_0_ = bf16[128,2048]{1,0:T(8,128)(2,1)S(1)} collective-permute-done((bf16[128,2048]{1,0:T(8,128)(2,1)}, bf16[128,2048]{1,0:T(8,128)(2,1)S(1)}, u32[]{:S(2)}, u32[]{:S(2)}) %collective-permute-start.11) | collective-permute-done | bytes 524320 | tf_op jit(solution)/shard_map/ppermute | solution.py:134
  77.2 8.9 %pair_rows.6 = (f32[128,2048]{1,0:T(8,128)S(1)}, bf16[128,2048]{1,0:T(8,128)(2,1)S(1)}) custom-call(s32[2]{0:T(128)S(1)} %pad_add_fusion.experts, bf16[128,2048]{1,0:T(8,128)(2,1)S(1)} %copy-done.9, bf16[128,2048]{1,0:T(8,128)(2,1)S(1)} %collective-permute-done.10.refs_1_, bf16[128,2176]{1,0:T(8,128)(2,1)S(1)} %collective-permute-done.3.refs_2_, ...), custom_call_target="tpu_custom_call" | custom-call | flops 5368709120 | bytes 16252928 | tf_op jit(solution)/shard_map/pair_rows/pallas_call | solution.py:104
  86.7 1.6 %collective-permute-start.16 = (bf16[64,2048]{1,0:T(8,128)(2,1)S(1)}, bf16[64,2048]{1,0:T(8,128)(2,1)S(1)}, u32[]{:S(2)}, u32[]{:S(2)}) collective-permute-start(bf16[64,2048]{1,0:T(8,128)(2,1)S(1)} %slice.7), channel_id=1, source_target_pairs={{0,2},{1,3},{2,0},{3,1},{4,6},{5,7},{6,4},{7,5},{8,10},{9,11},{10,... | collective-permute-start | bytes 786440 | tf_op jit(solution)/shard_map/ppermute | solution.py:137
  88.6 8.8 %pair_rows.7 = (f32[128,2048]{1,0:T(8,128)S(1)}, bf16[128,2048]{1,0:T(8,128)(2,1)S(1)}) custom-call(s32[2]{0:T(128)S(1)} %pad_add_fusion.experts, bf16[128,2048]{1,0:T(8,128)(2,1)S(1)} %collective-permute-done.11.refs_0_, bf16[128,2048]{1,0:T(8,128)(2,1)S(1)} %collective-permute-done.12.refs_1_, bf16[128,2176]{1,0:T(8,128)(2,1)S(1)} %collective-permute-done.6.refs_2_, ...), custom_call_target="tpu_custom_call" | custom-call | flops 5368709120 | bytes 16252928 | tf_op jit(solution)/shard_map/pair_rows/pallas_call | solution.py:104
  97.4 6.6 %collective-permute-done.16.refs_1_ = bf16[64,2048]{1,0:T(8,128)(2,1)S(1)} collective-permute-done((bf16[64,2048]{1,0:T(8,128)(2,1)S(1)}, bf16[64,2048]{1,0:T(8,128)(2,1)S(1)}, u32[]{:S(2)}, u32[]{:S(2)}) %collective-permute-start.16) | collective-permute-done | bytes 262176 | tf_op jit(solution)/shard_map/ppermute | solution.py:137
  104.0 1.6 %collective-permute-start.19 = (bf16[128,2048]{1,0:T(8,128)(2,1)S(1)}, bf16[128,2048]{1,0:T(8,128)(2,1)S(1)}, u32[]{:S(2)}, u32[]{:S(2)}) collective-permute-start(bf16[128,2048]{1,0:T(8,128)(2,1)S(1)} %get-tuple-element.70), channel_id=1, source_target_pairs={{0,2},{1,3},{2,0},{3,1},{4,6},{5,7},{6,4},{7,5},{8,10},{9,11},{10,... | collective-permute-start | bytes 1572872 | tf_op jit(solution)/shard_map/ppermute | solution.py:137
  106.0 8.1 %pair_rows.8 = bf16[128,2048]{1,0:T(8,128)(2,1)S(1)} custom-call(s32[2]{0:T(128)S(1)} %pad_add_fusion.experts, bf16[64,2048]{1,0:T(8,128)(2,1)S(1)} %collective-permute-done.15.refs_0_, bf16[64,2048]{1,0:T(8,128)(2,1)S(1)} %collective-permute-done.16.refs_1_, bf16[128,2176]{1,0:T(8,128)(2,1)S(1)} %collective-permute-done.14.refs_2_, ...), custom_call_target="tpu_custom_call" | custom-call | flops 2684354560 | bytes 14417920 | tf_op jit(solution)/shard_map/pair_rows/pallas_call | solution.py:104
  114.1 1.7 %collective-permute-done.19 = bf16[128,2048]{1,0:T(8,128)(2,1)S(1)} collective-permute-done((bf16[128,2048]{1,0:T(8,128)(2,1)S(1)}, bf16[128,2048]{1,0:T(8,128)(2,1)S(1)}, u32[]{:S(2)}, u32[]{:S(2)}) %collective-permute-start.19) | collective-permute-done | bytes 524320 | tf_op jit(solution)/shard_map/ppermute | solution.py:137
  115.9 1.8 %collective-permute-start.22 = (bf16[128,2048]{1,0:T(8,128)(2,1)S(1)}, bf16[128,2048]{1,0:T(8,128)(2,1)S(1)}, u32[]{:S(2)}, u32[]{:S(2)}) collective-permute-start(bf16[128,2048]{1,0:T(8,128)(2,1)S(1)} %pair_rows.8), channel_id=1, source_target_pairs={{0,2},{1,3},{2,0},{3,1},{4,6},{5,7},{6,4},{7,5},{8,10},{9,11},{10,... | collective-permute-start | bytes 1572872 | tf_op jit(solution)/shard_map/ppermute | solution.py:137
  117.7 8.1 %pair_rows.9 = f32[128,2048]{1,0:T(8,128)S(1)} custom-call(s32[2]{0:T(128)S(1)} %pad_add_fusion.experts, bf16[128,2048]{1,0:T(8,128)(2,1)S(1)} %collective-permute-done.9.refs_0_, bf16[128,2176]{1,0:T(8,128)(2,1)S(1)} %collective-permute-done.18.refs_1_, bf16[2048,512]{1,0:T(8,128)(2,1)S(1)} %bitcast.12, bf16[2048,512]{1,0:T(8,128)(2,1)S(1)} %bitcast.18, ...), custom_call_target="tpu_custom_call" | custom-call | flops 2684354560 | bytes 14417920 | tf_op jit(solution)/shard_map/pair_rows/pallas_call | solution.py:104
  126.4 2.5 %collective-permute-done.22 = bf16[128,2048]{1,0:T(8,128)(2,1)S(1)} collective-permute-done((bf16[128,2048]{1,0:T(8,128)(2,1)S(1)}, bf16[128,2048]{1,0:T(8,128)(2,1)S(1)}, u32[]{:S(2)}, u32[]{:S(2)}) %collective-permute-start.22) | collective-permute-done | bytes 524320 | tf_op jit(solution)/shard_map/ppermute | solution.py:137
  130.5 7.7 %collective-permute-done.20 = bf16[128,2048]{1,0:T(8,128)(2,1)S(1)} collective-permute-done((bf16[128,2048]{1,0:T(8,128)(2,1)S(1)}, bf16[128,2048]{1,0:T(8,128)(2,1)S(1)}, u32[]{:S(2)}, u32[]{:S(2)}) %collective-permute-start.20) | collective-permute-done | bytes 524320 | tf_op jit(solution)/shard_map/ppermute | solution.py:137
  138.3 3.9 %collective-permute-done.24 = bf16[128,2048]{1,0:T(8,128)(2,1)S(1)} collective-permute-done((bf16[128,2048]{1,0:T(8,128)(2,1)S(1)}, bf16[128,2048]{1,0:T(8,128)(2,1)S(1)}, u32[]{:S(2)}, u32[]{:S(2)}) %collective-permute-start.24) | collective-permute-done | bytes 524320 | tf_op jit(solution)/shard_map/ppermute | solution.py:134
  (59 shorter events, 15.2 us)
Async XLA Ops:
  0.0 33.1 %collective-permute-start.4 = (bf16[2048,512]{1,0:T(8,128)(2,1)}, bf16[2048,512]{1,0:T(8,128)(2,1)S(1)}, u32[]{:S(2)}, u32[]{:S(2)}) collective-permute-start(bf16[2048,512]{1,0:T(8,128)(2,1)} %bitcast.7), channel_id=1, source_target_pairs={{0,1},{1,0},{2,3},{3,2},{4,5},{5,4},{6,7},{7,6},{8,9},{9,8},{10,11... | collective-permute-start | bytes 6291464 | tf_op jit(solution)/shard_map/ppermute | solution.py:137
  2.4 30.6 %collective-permute-start.2 = (bf16[128,2176]{1,0:T(8,128)(2,1)}, bf16[128,2176]{1,0:T(8,128)(2,1)S(1)}, u32[]{:S(2)}, u32[]{:S(2)}) collective-permute-start(bf16[128,2176]{1,0:T(8,128)(2,1)} %gated_rows.1.refs_2_), channel_id=1, source_target_pairs={{0,2},{1,3},{2,0},{3,1},{4,6},{5,7},{6,4},{7,5},{8,10},{9,11},{10,... | collective-permute-start | bytes 1671176 | tf_op jit(solution)/shard_map/ppermute | solution.py:137
  5.0 28.1 %collective-permute-start.3 = (bf16[128,2176]{1,0:T(8,128)(2,1)}, bf16[128,2176]{1,0:T(8,128)(2,1)S(1)}, u32[]{:S(2)}, u32[]{:S(2)}) collective-permute-start(bf16[128,2176]{1,0:T(8,128)(2,1)} %gated_rows.1.refs_2_), channel_id=1, source_target_pairs={{0,4},{1,5},{2,6},{3,7},{4,8},{5,9},{6,10},{7,11},{8,12},{9,13},{1... | collective-permute-start | bytes 1671176 | tf_op jit(solution)/shard_map/ppermute | solution.py:134
  6.5 23.2 %collective-permute-start = (bf16[128,2048]{1,0:T(8,128)(2,1)}, bf16[128,2048]{1,0:T(8,128)(2,1)S(1)}, u32[]{:S(2)}, u32[]{:S(2)}) collective-permute-start(bf16[128,2048]{1,0:T(8,128)(2,1)} %refs_0_.1), channel_id=1, source_target_pairs={{0,2},{1,3},{2,0},{3,1},{4,6},{5,7},{6,4},{7,5},{8,10},{9,11},{10,... | collective-permute-start | bytes 1572872 | tf_op jit(solution)/shard_map/ppermute | solution.py:137
  7.0 26.0 %collective-permute-start.1 = (bf16[128,2048]{1,0:T(8,128)(2,1)}, bf16[128,2048]{1,0:T(8,128)(2,1)S(1)}, u32[]{:S(2)}, u32[]{:S(2)}) collective-permute-start(bf16[128,2048]{1,0:T(8,128)(2,1)} %refs_0_.1), channel_id=1, source_target_pairs={{0,4},{1,5},{2,6},{3,7},{4,8},{5,9},{6,10},{7,11},{8,12},{9,13},{1... | collective-permute-start | bytes 1572872 | tf_op jit(solution)/shard_map/ppermute | solution.py:134
  34.1 7.5 %collective-permute-start.8 = (bf16[512,2048]{1,0:T(8,128)(2,1)}, bf16[512,2048]{1,0:T(8,128)(2,1)}, u32[]{:S(2)}, u32[]{:S(2)}) collective-permute-start(bf16[512,2048]{1,0:T(8,128)(2,1)} %bitcast.19), channel_id=1, source_target_pairs={{0,1},{1,0},{2,3},{3,2},{4,5},{5,4},{6,7},{7,6},{8,9},{9,8},{10,11... | collective-permute-start | bytes 6291464 | tf_op jit(solution)/shard_map/ppermute | solution.py:137
  34.6 21.7 %collective-permute-start.5 = (bf16[128,2176]{1,0:T(8,128)(2,1)S(1)}, bf16[128,2176]{1,0:T(8,128)(2,1)S(1)}, u32[]{:S(2)}, u32[]{:S(2)}) collective-permute-start(bf16[128,2176]{1,0:T(8,128)(2,1)S(1)} %collective-permute-done.3.refs_2_), channel_id=1, source_target_pairs={{0,2},{1,3},{2,0},{3,1},{4,6},{5,7},{6,4},{7,5},{8,10},{9,11},{10,... | collective-permute-start | bytes 1671176 | tf_op jit(solution)/shard_map/ppermute | solution.py:137
  35.1 21.3 %collective-permute-start.6 = (bf16[128,2176]{1,0:T(8,128)(2,1)S(1)}, bf16[128,2176]{1,0:T(8,128)(2,1)S(1)}, u32[]{:S(2)}, u32[]{:S(2)}) collective-permute-start(bf16[128,2176]{1,0:T(8,128)(2,1)S(1)} %collective-permute-done.3.refs_2_), channel_id=1, source_target_pairs={{0,4},{1,5},{2,6},{3,7},{4,8},{5,9},{6,10},{7,11},{8,12},{9,13},{1... | collective-permute-start | bytes 1671176 | tf_op jit(solution)/shard_map/ppermute | solution.py:134
  35.1 42.1 %collective-permute-start.14 = (bf16[128,2176]{1,0:T(8,128)(2,1)}, bf16[128,2176]{1,0:T(8,128)(2,1)S(1)}, u32[]{:S(2)}, u32[]{:S(2)}) collective-permute-start(bf16[128,2176]{1,0:T(8,128)(2,1)} %copy-done.6), channel_id=1, source_target_pairs={{0,12},{1,13},{2,14},{3,15},{4,0},{5,1},{6,2},{7,3},{8,4},{9,5},{1... | collective-permute-start | bytes 1671176 | tf_op jit(solution)/shard_map/ppermute | solution.py:134
  39.0 26.7 %collective-permute-start.10 = (bf16[128,2048]{1,0:T(8,128)(2,1)}, bf16[128,2048]{1,0:T(8,128)(2,1)S(1)}, u32[]{:S(2)}, u32[]{:S(2)}) collective-permute-start(bf16[128,2048]{1,0:T(8,128)(2,1)} %copy-done.8), channel_id=1, source_target_pairs={{0,2},{1,3},{2,0},{3,1},{4,6},{5,7},{6,4},{7,5},{8,10},{9,11},{10,... | collective-permute-start | bytes 1572872 | tf_op jit(solution)/shard_map/ppermute | solution.py:137
  41.6 34.1 %collective-permute-start.11 = (bf16[128,2048]{1,0:T(8,128)(2,1)}, bf16[128,2048]{1,0:T(8,128)(2,1)S(1)}, u32[]{:S(2)}, u32[]{:S(2)}) collective-permute-start(bf16[128,2048]{1,0:T(8,128)(2,1)} %copy-done.8), channel_id=1, source_target_pairs={{0,4},{1,5},{2,6},{3,7},{4,8},{5,9},{6,10},{7,11},{8,12},{9,13},{1... | collective-permute-start | bytes 1572872 | tf_op jit(solution)/shard_map/ppermute | solution.py:134
  56.4 32.2 %collective-permute-start.13 = (bf16[128,2176]{1,0:T(8,128)(2,1)S(1)}, bf16[128,2176]{1,0:T(8,128)(2,1)S(1)}, u32[]{:S(2)}, u32[]{:S(2)}) collective-permute-start(bf16[128,2176]{1,0:T(8,128)(2,1)S(1)} %collective-permute-done.6.refs_2_), channel_id=1, source_target_pairs={{0,2},{1,3},{2,0},{3,1},{4,6},{5,7},{6,4},{7,5},{8,10},{9,11},{10,... | collective-permute-start | bytes 1671176 | tf_op jit(solution)/shard_map/ppermute | solution.py:137
  57.0 29.7 %collective-permute-start.9 = (bf16[128,2048]{1,0:T(8,128)(2,1)}, bf16[128,2048]{1,0:T(8,128)(2,1)S(1)}, u32[]{:S(2)}, u32[]{:S(2)}) collective-permute-start(bf16[128,2048]{1,0:T(8,128)(2,1)} %refs_0_.1), channel_id=1, source_target_pairs={{0,12},{1,13},{2,14},{3,15},{4,0},{5,1},{6,2},{7,3},{8,4},{9,5},{1... | collective-permute-start | bytes 1572872 | tf_op jit(solution)/shard_map/ppermute | solution.py:134
  75.6 12.6 %collective-permute-start.12 = (bf16[128,2048]{1,0:T(8,128)(2,1)S(1)}, bf16[128,2048]{1,0:T(8,128)(2,1)S(1)}, u32[]{:S(2)}, u32[]{:S(2)}) collective-permute-start(bf16[128,2048]{1,0:T(8,128)(2,1)S(1)} %collective-permute-done.11.refs_0_), channel_id=1, source_target_pairs={{0,2},{1,3},{2,0},{3,1},{4,6},{5,7},{6,4},{7,5},{8,10},{9,11},{10,... | collective-permute-start | bytes 1572872 | tf_op jit(solution)/shard_map/ppermute | solution.py:137
  77.2 26.8 %collective-permute-start.18 = (bf16[128,2176]{1,0:T(8,128)(2,1)}, bf16[128,2176]{1,0:T(8,128)(2,1)S(1)}, u32[]{:S(2)}, u32[]{:S(2)}) collective-permute-start(bf16[128,2176]{1,0:T(8,128)(2,1)} %gated_rows.1.refs_2_), channel_id=1, source_target_pairs={{0,12},{1,13},{2,14},{3,15},{4,0},{5,1},{6,2},{7,3},{8,4},{9,5},{1... | collective-permute-start | bytes 1671176 | tf_op jit(solution)/shard_map/ppermute | solution.py:134
  86.1 17.9 %collective-permute-start.17 = (bf16[128,2048]{1,0:T(8,128)(2,1)S(1)}, bf16[128,2048]{1,0:T(8,128)(2,1)S(1)}, u32[]{:S(2)}, u32[]{:S(2)}) collective-permute-start(bf16[128,2048]{1,0:T(8,128)(2,1)S(1)} %get-tuple-element.65), channel_id=1, source_target_pairs={{0,2},{1,3},{2,0},{3,1},{4,6},{5,7},{6,4},{7,5},{8,10},{9,11},{10,... | collective-permute-start | bytes 1572872 | tf_op jit(solution)/shard_map/ppermute | solution.py:137
  86.7 17.3 %collective-permute-start.16 = (bf16[64,2048]{1,0:T(8,128)(2,1)S(1)}, bf16[64,2048]{1,0:T(8,128)(2,1)S(1)}, u32[]{:S(2)}, u32[]{:S(2)}) collective-permute-start(bf16[64,2048]{1,0:T(8,128)(2,1)S(1)} %slice.7), channel_id=1, source_target_pairs={{0,2},{1,3},{2,0},{3,1},{4,6},{5,7},{6,4},{7,5},{8,10},{9,11},{10,... | collective-permute-start | bytes 786440 | tf_op jit(solution)/shard_map/ppermute | solution.py:137
  88.3 15.7 %collective-permute-start.15 = (bf16[64,2048]{1,0:T(8,128)(2,1)S(1)}, bf16[64,2048]{1,0:T(8,128)(2,1)S(1)}, u32[]{:S(2)}, u32[]{:S(2)}) collective-permute-start(bf16[64,2048]{1,0:T(8,128)(2,1)S(1)} %slice.6), channel_id=1, source_target_pairs={{0,12},{1,13},{2,14},{3,15},{4,0},{5,1},{6,2},{7,3},{8,4},{9,5},{1... | collective-permute-start | bytes 786440 | tf_op jit(solution)/shard_map/ppermute | solution.py:134
  104.0 11.8 %collective-permute-start.19 = (bf16[128,2048]{1,0:T(8,128)(2,1)S(1)}, bf16[128,2048]{1,0:T(8,128)(2,1)S(1)}, u32[]{:S(2)}, u32[]{:S(2)}) collective-permute-start(bf16[128,2048]{1,0:T(8,128)(2,1)S(1)} %get-tuple-element.70), channel_id=1, source_target_pairs={{0,2},{1,3},{2,0},{3,1},{4,6},{5,7},{6,4},{7,5},{8,10},{9,11},{10,... | collective-permute-start | bytes 1572872 | tf_op jit(solution)/shard_map/ppermute | solution.py:137
  105.7 20.1 %collective-permute-start.21 = (bf16[128,2048]{1,0:T(8,128)(2,1)S(1)}, bf16[128,2048]{1,0:T(8,128)(2,1)S(1)}, u32[]{:S(2)}, u32[]{:S(2)}) collective-permute-start(bf16[128,2048]{1,0:T(8,128)(2,1)S(1)} %add_convert_fusion.1), channel_id=1, source_target_pairs={{0,12},{1,13},{2,14},{3,15},{4,0},{5,1},{6,2},{7,3},{8,4},{9,5},{1... | collective-permute-start | bytes 1572872 | tf_op jit(solution)/shard_map/ppermute | solution.py:134
  115.9 13.0 %collective-permute-start.22 = (bf16[128,2048]{1,0:T(8,128)(2,1)S(1)}, bf16[128,2048]{1,0:T(8,128)(2,1)S(1)}, u32[]{:S(2)}, u32[]{:S(2)}) collective-permute-start(bf16[128,2048]{1,0:T(8,128)(2,1)S(1)} %pair_rows.8), channel_id=1, source_target_pairs={{0,2},{1,3},{2,0},{3,1},{4,6},{5,7},{6,4},{7,5},{8,10},{9,11},{10,... | collective-permute-start | bytes 1572872 | tf_op jit(solution)/shard_map/ppermute | solution.py:137
  117.7 12.5 %collective-permute-start.23 = (bf16[128,2048]{1,0:T(8,128)(2,1)S(1)}, bf16[128,2048]{1,0:T(8,128)(2,1)S(1)}, u32[]{:S(2)}, u32[]{:S(2)}) collective-permute-start(bf16[128,2048]{1,0:T(8,128)(2,1)S(1)} %add_convert_fusion.2), channel_id=1, source_target_pairs={{0,4},{1,5},{2,6},{3,7},{4,8},{5,9},{6,10},{7,11},{8,12},{9,13},{1... | collective-permute-start | bytes 1572872 | tf_op jit(solution)/shard_map/ppermute | solution.py:134
  125.8 12.5 %collective-permute-start.20 = (bf16[128,2048]{1,0:T(8,128)(2,1)S(1)}, bf16[128,2048]{1,0:T(8,128)(2,1)S(1)}, u32[]{:S(2)}, u32[]{:S(2)}) collective-permute-start(bf16[128,2048]{1,0:T(8,128)(2,1)S(1)} %get-tuple-element.74), channel_id=1, source_target_pairs={{0,2},{1,3},{2,0},{3,1},{4,6},{5,7},{6,4},{7,5},{8,10},{9,11},{10,... | collective-permute-start | bytes 1572872 | tf_op jit(solution)/shard_map/ppermute | solution.py:137
  130.5 11.7 %collective-permute-start.24 = (bf16[128,2048]{1,0:T(8,128)(2,1)S(1)}, bf16[128,2048]{1,0:T(8,128)(2,1)S(1)}, u32[]{:S(2)}, u32[]{:S(2)}) collective-permute-start(bf16[128,2048]{1,0:T(8,128)(2,1)S(1)} %add_convert_fusion), channel_id=1, source_target_pairs={{0,4},{1,5},{2,6},{3,7},{4,8},{5,9},{6,10},{7,11},{8,12},{9,13},{1... | collective-permute-start | bytes 1572872 | tf_op jit(solution)/shard_map/ppermute | solution.py:134
  (11 other events, 136.5 us)

commit v8 on v7

--- a/solution.py
+++ b/solution.py
@@ -186,8 +186,9 @@
         if s < ring - 1:
             carried = (sums[s] + carried).astype(BF16)
     last = (last + swap(beyond, 2).astype(F32) + carried).astype(BF16)
-    total = nears[0] + swap(first, 2).astype(F32)
-    return total + turn(last, 1).astype(F32) + one.astype(F32)
+    total = nears[0] + swap(first, 2).astype(F32) + one.astype(F32)
+    total, last = tie((total, turn(last, 1)))
+    return total + last.astype(F32)
 
 
 def expert_rows(rows_in, rows_grad, gate_w, up_w, down_w):

time: 144 us -> 143 us (level)
  no operation moved by 1% of the time
where the time goes in v8:
time: 143 us
  waiting for transfers between devices  59.1 us (41%)
  Pallas kernels  44.5 us (31%)
  starting transfers between devices  30.7 us (21%)
  local copies, waits for them, and re-layouts  6.69 us (5%)
  other arithmetic  1.73 us (1%)
    pallas_call x5, Pallas kernels, pair_rows(): pl.pallas_call(partial(pair_kernel, pieces, blocks, owners, 512 if width...  42.6 us
    ppermute x14, waiting for transfers between devices, swap(): return lax.ppermute(value, 'expert', [(i, i ^ bit) for i in range(owners)])  41.8 us
    ppermute x11, waiting for transfers between devices, turn(): lax.ppermute(value, 'expert', [(i, (i + 4 * by) % owners) for i in range(...  17.3 us
    ppermute x11, starting transfers between devices, turn(): lax.ppermute(value, 'expert', [(i, (i + 4 * by) % owners) for i in range(...  16.6 us
    ppermute x14, starting transfers between devices, swap(): return lax.ppermute(value, 'expert', [(i, i ^ bit) for i in range(owners)])  14.1 us
    unnamed x20, local copies, waits for them, and re-layouts  6.66 us
  transfers between devices with their start and end apart: 25, of which 10 were waited for; matrix products, arithmetic and copies ran while one was open for 0% of the time, Pallas kernels for 31%

profile of v8, /device:TPU:0, one launch (start us, length us, event | category | flops | bytes accessed | tf_op | source)
XLA Modules:
  0.0 143.0 jit_solution(8565625221978485596)
XLA Ops:
  0.5 2.0 %gated_rows.1.refs_2_ = bf16[128,2176]{1,0:T(8,128)(2,1)} custom-call(s32[8,128]{1,0:T(8,128)} %bitcast.25, f32[8,128]{1,0:T(8,128)} %bitcast.26, bf16[128,2048]{1,0:T(8,128)(2,1)} %grad.1), custom_call_target="tpu_custom_call" | custom-call | tf_op jit(solution)/shard_map/gated_rows/pallas_call | solution.py:33
  2.4 2.5 %collective-permute-start.2 = (bf16[128,2176]{1,0:T(8,128)(2,1)}, bf16[128,2176]{1,0:T(8,128)(2,1)}, u32[]{:S(2)}, u32[]{:S(2)}) collective-permute-start(bf16[128,2176]{1,0:T(8,128)(2,1)} %gated_rows.1.refs_2_), channel_id=1, source_target_pairs={{0,2},{1,3},{2,0},{3,1},{4,6},{5,7},{6,4},{7,5},{8,10},{9,11},{10,... | collective-permute-start | bytes 1671176 | tf_op jit(solution)/shard_map/ppermute | solution.py:137
  5.0 1.6 %collective-permute-start.3 = (bf16[128,2176]{1,0:T(8,128)(2,1)}, bf16[128,2176]{1,0:T(8,128)(2,1)S(1)}, u32[]{:S(2)}, u32[]{:S(2)}) collective-permute-start(bf16[128,2176]{1,0:T(8,128)(2,1)} %gated_rows.1.refs_2_), channel_id=1, source_target_pairs={{0,4},{1,5},{2,6},{3,7},{4,8},{5,9},{6,10},{7,11},{8,12},{9,13},{1... | collective-permute-start | bytes 1671176 | tf_op jit(solution)/shard_map/ppermute | solution.py:134
  8.6 21.1 %collective-permute-done.refs_1_ = bf16[128,2048]{1,0:T(8,128)(2,1)S(1)} collective-permute-done((bf16[128,2048]{1,0:T(8,128)(2,1)}, bf16[128,2048]{1,0:T(8,128)(2,1)S(1)}, u32[]{:S(2)}, u32[]{:S(2)}) %collective-permute-start) | collective-permute-done | bytes 524320 | tf_op jit(solution)/shard_map/ppermute | solution.py:137
  29.7 3.5 %collective-permute-done.1.refs_0_ = bf16[128,2048]{1,0:T(8,128)(2,1)} collective-permute-done((bf16[128,2048]{1,0:T(8,128)(2,1)}, bf16[128,2048]{1,0:T(8,128)(2,1)}, u32[]{:S(2)}, u32[]{:S(2)}) %collective-permute-start.1) | collective-permute-done | bytes 524320 | tf_op jit(solution)/shard_map/ppermute | solution.py:134
  34.3 3.8 %collective-permute-start.14 = (bf16[128,2176]{1,0:T(8,128)(2,1)}, bf16[128,2176]{1,0:T(8,128)(2,1)S(1)}, u32[]{:S(2)}, u32[]{:S(2)}) collective-permute-start(bf16[128,2176]{1,0:T(8,128)(2,1)} %collective-permute-done.2.refs_3_), channel_id=1, source_target_pairs={{0,12},{1,13},{2,14},{3,15},{4,0},{5,1},{6,2},{7,3},{8,4},{9,5},{1... | collective-permute-start | bytes 1671176 | tf_op jit(solution)/shard_map/ppermute | solution.py:134
  40.8 1.6 %copy-done = bf16[1,2048,512]{2,1,0:T(8,128)(2,1)S(1)} copy-done((bf16[1,2048,512]{2,1,0:T(8,128)(2,1)S(1)}, bf16[1,2048,512]{2,1,0:T(8,128)(2,1)}, u32[]{:S(2)}) %copy-start) | copy-done | bytes 2097176
  42.3 1.6 %copy-done.2 = bf16[1,2048,512]{2,1,0:T(8,128)(2,1)S(1)} copy-done((bf16[1,2048,512]{2,1,0:T(8,128)(2,1)S(1)}, bf16[1,2048,512]{2,1,0:T(8,128)(2,1)}, u32[]{:S(2)}) %copy-start.2) | copy-done | bytes 2097176
  43.9 1.6 %copy-done.4 = bf16[1,512,2048]{2,1,0:T(8,128)(2,1)S(1)} copy-done((bf16[1,512,2048]{2,1,0:T(8,128)(2,1)S(1)}, bf16[1,512,2048]{2,1,0:T(8,128)(2,1)}, u32[]{:S(2)}) %copy-start.4) | copy-done | bytes 2097176
  45.5 8.8 %pair_rows.5 = (f32[128,2048]{1,0:T(8,128)S(1)}, bf16[128,2048]{1,0:T(8,128)(2,1)S(1)}) custom-call(s32[2]{0:T(128)S(1)} %pad_add_fusion.experts, bf16[128,2048]{1,0:T(8,128)(2,1)} %refs_0_.1, bf16[128,2048]{1,0:T(8,128)(2,1)S(1)} %collective-permute-done.refs_1_, bf16[128,2176]{1,0:T(8,128)(2,1)} %gated_rows.1.refs_2_, ...), custom_call_target="tpu_custom_call" | custom-call | flops 5368709120 | bytes 16252928 | tf_op jit(solution)/shard_map/pair_rows/pallas_call | solution.py:104
  55.7 9.1 %collective-permute-start.9 = (bf16[128,2048]{1,0:T(8,128)(2,1)}, bf16[128,2048]{1,0:T(8,128)(2,1)S(1)}, u32[]{:S(2)}, u32[]{:S(2)}) collective-permute-start(bf16[128,2048]{1,0:T(8,128)(2,1)} %refs_0_.1), channel_id=1, source_target_pairs={{0,12},{1,13},{2,14},{3,15},{4,0},{5,1},{6,2},{7,3},{8,4},{9,5},{1... | collective-permute-start | bytes 1572872 | tf_op jit(solution)/shard_map/ppermute | solution.py:134
  64.8 10.1 %collective-permute-done.11.refs_0_ = bf16[128,2048]{1,0:T(8,128)(2,1)} collective-permute-done((bf16[128,2048]{1,0:T(8,128)(2,1)}, bf16[128,2048]{1,0:T(8,128)(2,1)}, u32[]{:S(2)}, u32[]{:S(2)}) %collective-permute-start.11) | collective-permute-done | bytes 524320 | tf_op jit(solution)/shard_map/ppermute | solution.py:134
  76.4 8.8 %pair_rows.6 = (f32[128,2048]{1,0:T(8,128)S(1)}, bf16[128,2048]{1,0:T(8,128)(2,1)S(1)}) custom-call(s32[2]{0:T(128)S(1)} %pad_add_fusion.experts, bf16[128,2048]{1,0:T(8,128)(2,1)} %collective-permute-done.1.refs_0_, bf16[128,2048]{1,0:T(8,128)(2,1)S(1)} %collective-permute-done.10.refs_1_, bf16[128,2176]{1,0:T(8,128)(2,1)S(1)} %collective-permute-done.3.refs_2_, ...), custom_call_target="tpu_custom_call" | custom-call | flops 5368709120 | bytes 16252928 | tf_op jit(solution)/shard_map/pair_rows/pallas_call | solution.py:104
  85.9 1.6 %collective-permute-start.16 = (bf16[64,2048]{1,0:T(8,128)(2,1)S(1)}, bf16[64,2048]{1,0:T(8,128)(2,1)S(1)}, u32[]{:S(2)}, u32[]{:S(2)}) collective-permute-start(bf16[64,2048]{1,0:T(8,128)(2,1)S(1)} %slice.7), channel_id=1, source_target_pairs={{0,2},{1,3},{2,0},{3,1},{4,6},{5,7},{6,4},{7,5},{8,10},{9,11},{10,... | collective-permute-start | bytes 786440 | tf_op jit(solution)/shard_map/ppermute | solution.py:137
  89.2 8.8 %pair_rows.7 = (f32[128,2048]{1,0:T(8,128)S(1)}, bf16[128,2048]{1,0:T(8,128)(2,1)S(1)}) custom-call(s32[2]{0:T(128)S(1)} %pad_add_fusion.experts, bf16[128,2048]{1,0:T(8,128)(2,1)} %collective-permute-done.11.refs_0_, bf16[128,2048]{1,0:T(8,128)(2,1)S(1)} %collective-permute-done.12.refs_1_, bf16[128,2176]{1,0:T(8,128)(2,1)S(1)} %copy-done.7, ...), custom_call_target="tpu_custom_call" | custom-call | flops 5368709120 | bytes 16252928 | tf_op jit(solution)/shard_map/pair_rows/pallas_call | solution.py:104
  98.0 5.6 %collective-permute-done.16.refs_1_ = bf16[64,2048]{1,0:T(8,128)(2,1)S(1)} collective-permute-done((bf16[64,2048]{1,0:T(8,128)(2,1)S(1)}, bf16[64,2048]{1,0:T(8,128)(2,1)S(1)}, u32[]{:S(2)}, u32[]{:S(2)}) %collective-permute-start.16) | collective-permute-done | bytes 262176 | tf_op jit(solution)/shard_map/ppermute | solution.py:137
  103.6 1.6 %collective-permute-start.19 = (bf16[128,2048]{1,0:T(8,128)(2,1)S(1)}, bf16[128,2048]{1,0:T(8,128)(2,1)S(1)}, u32[]{:S(2)}, u32[]{:S(2)}) collective-permute-start(bf16[128,2048]{1,0:T(8,128)(2,1)S(1)} %get-tuple-element.72), channel_id=1, source_target_pairs={{0,2},{1,3},{2,0},{3,1},{4,6},{5,7},{6,4},{7,5},{8,10},{9,11},{10,... | collective-permute-start | bytes 1572872 | tf_op jit(solution)/shard_map/ppermute | solution.py:137
  105.6 8.1 %pair_rows.8 = bf16[128,2048]{1,0:T(8,128)(2,1)S(1)} custom-call(s32[2]{0:T(128)S(1)} %pad_add_fusion.experts, bf16[64,2048]{1,0:T(8,128)(2,1)S(1)} %collective-permute-done.15.refs_0_, bf16[64,2048]{1,0:T(8,128)(2,1)S(1)} %collective-permute-done.16.refs_1_, bf16[128,2176]{1,0:T(8,128)(2,1)S(1)} %collective-permute-done.14.refs_2_, ...), custom_call_target="tpu_custom_call" | custom-call | flops 2684354560 | bytes 14417920 | tf_op jit(solution)/shard_map/pair_rows/pallas_call | solution.py:104
  113.7 1.9 %collective-permute-done.19 = bf16[128,2048]{1,0:T(8,128)(2,1)S(1)} collective-permute-done((bf16[128,2048]{1,0:T(8,128)(2,1)S(1)}, bf16[128,2048]{1,0:T(8,128)(2,1)S(1)}, u32[]{:S(2)}, u32[]{:S(2)}) %collective-permute-start.19) | collective-permute-done | bytes 524320 | tf_op jit(solution)/shard_map/ppermute | solution.py:137
  115.7 1.6 %collective-permute-start.22 = (bf16[128,2048]{1,0:T(8,128)(2,1)S(1)}, bf16[128,2048]{1,0:T(8,128)(2,1)S(1)}, u32[]{:S(2)}, u32[]{:S(2)}) collective-permute-start(bf16[128,2048]{1,0:T(8,128)(2,1)S(1)} %pair_rows.8), channel_id=1, source_target_pairs={{0,2},{1,3},{2,0},{3,1},{4,6},{5,7},{6,4},{7,5},{8,10},{9,11},{10,... | collective-permute-start | bytes 1572872 | tf_op jit(solution)/shard_map/ppermute | solution.py:137
  118.0 8.1 %pair_rows.9 = f32[128,2048]{1,0:T(8,128)S(1)} custom-call(s32[2]{0:T(128)S(1)} %pad_add_fusion.experts, bf16[128,2048]{1,0:T(8,128)(2,1)S(1)} %collective-permute-done.9.refs_0_, bf16[128,2176]{1,0:T(8,128)(2,1)S(1)} %collective-permute-done.18.refs_1_, bf16[2048,512]{1,0:T(8,128)(2,1)S(1)} %bitcast.12, bf16[2048,512]{1,0:T(8,128)(2,1)S(1)} %bitcast.18, ...), custom_call_target="tpu_custom_call" | custom-call | flops 2684354560 | bytes 14417920 | tf_op jit(solution)/shard_map/pair_rows/pallas_call | solution.py:104
  126.0 4.6 %collective-permute-done.22 = bf16[128,2048]{1,0:T(8,128)(2,1)S(1)} collective-permute-done((bf16[128,2048]{1,0:T(8,128)(2,1)S(1)}, bf16[128,2048]{1,0:T(8,128)(2,1)S(1)}, u32[]{:S(2)}, u32[]{:S(2)}) %collective-permute-start.22) | collective-permute-done | bytes 524320 | tf_op jit(solution)/shard_map/ppermute | solution.py:137
  131.0 6.9 %collective-permute-done.20 = bf16[128,2048]{1,0:T(8,128)(2,1)S(1)} collective-permute-done((bf16[128,2048]{1,0:T(8,128)(2,1)S(1)}, bf16[128,2048]{1,0:T(8,128)(2,1)S(1)}, u32[]{:S(2)}, u32[]{:S(2)}) %collective-permute-start.20) | collective-permute-done | bytes 524320 | tf_op jit(solution)/shard_map/ppermute | solution.py:137
  138.1 3.8 %collective-permute-done.24 = bf16[128,2048]{1,0:T(8,128)(2,1)S(1)} collective-permute-done((bf16[128,2048]{1,0:T(8,128)(2,1)S(1)}, bf16[128,2048]{1,0:T(8,128)(2,1)S(1)}, u32[]{:S(2)}, u32[]{:S(2)}) %collective-permute-start.24) | collective-permute-done | bytes 524320 | tf_op jit(solution)/shard_map/ppermute | solution.py:134
  (60 shorter events, 14.3 us)
Async XLA Ops:
  0.0 33.2 %collective-permute-start.4 = (bf16[2048,512]{1,0:T(8,128)(2,1)}, bf16[2048,512]{1,0:T(8,128)(2,1)S(1)}, u32[]{:S(2)}, u32[]{:S(2)}) collective-permute-start(bf16[2048,512]{1,0:T(8,128)(2,1)} %bitcast.7), channel_id=1, source_target_pairs={{0,1},{1,0},{2,3},{3,2},{4,5},{5,4},{6,7},{7,6},{8,9},{9,8},{10,11... | collective-permute-start | bytes 6291464 | tf_op jit(solution)/shard_map/ppermute | solution.py:137
  2.4 30.7 %collective-permute-start.2 = (bf16[128,2176]{1,0:T(8,128)(2,1)}, bf16[128,2176]{1,0:T(8,128)(2,1)}, u32[]{:S(2)}, u32[]{:S(2)}) collective-permute-start(bf16[128,2176]{1,0:T(8,128)(2,1)} %gated_rows.1.refs_2_), channel_id=1, source_target_pairs={{0,2},{1,3},{2,0},{3,1},{4,6},{5,7},{6,4},{7,5},{8,10},{9,11},{10,... | collective-permute-start | bytes 1671176 | tf_op jit(solution)/shard_map/ppermute | solution.py:137
  5.0 28.2 %collective-permute-start.3 = (bf16[128,2176]{1,0:T(8,128)(2,1)}, bf16[128,2176]{1,0:T(8,128)(2,1)S(1)}, u32[]{:S(2)}, u32[]{:S(2)}) collective-permute-start(bf16[128,2176]{1,0:T(8,128)(2,1)} %gated_rows.1.refs_2_), channel_id=1, source_target_pairs={{0,4},{1,5},{2,6},{3,7},{4,8},{5,9},{6,10},{7,11},{8,12},{9,13},{1... | collective-permute-start | bytes 1671176 | tf_op jit(solution)/shard_map/ppermute | solution.py:134
  6.5 23.2 %collective-permute-start = (bf16[128,2048]{1,0:T(8,128)(2,1)}, bf16[128,2048]{1,0:T(8,128)(2,1)S(1)}, u32[]{:S(2)}, u32[]{:S(2)}) collective-permute-start(bf16[128,2048]{1,0:T(8,128)(2,1)} %refs_0_.1), channel_id=1, source_target_pairs={{0,2},{1,3},{2,0},{3,1},{4,6},{5,7},{6,4},{7,5},{8,10},{9,11},{10,... | collective-permute-start | bytes 1572872 | tf_op jit(solution)/shard_map/ppermute | solution.py:137
  7.0 26.1 %collective-permute-start.1 = (bf16[128,2048]{1,0:T(8,128)(2,1)}, bf16[128,2048]{1,0:T(8,128)(2,1)}, u32[]{:S(2)}, u32[]{:S(2)}) collective-permute-start(bf16[128,2048]{1,0:T(8,128)(2,1)} %refs_0_.1), channel_id=1, source_target_pairs={{0,4},{1,5},{2,6},{3,7},{4,8},{5,9},{6,10},{7,11},{8,12},{9,13},{1... | collective-permute-start | bytes 1572872 | tf_op jit(solution)/shard_map/ppermute | solution.py:134
  33.3 7.5 %collective-permute-start.8 = (bf16[512,2048]{1,0:T(8,128)(2,1)}, bf16[512,2048]{1,0:T(8,128)(2,1)}, u32[]{:S(2)}, u32[]{:S(2)}) collective-permute-start(bf16[512,2048]{1,0:T(8,128)(2,1)} %bitcast.19), channel_id=1, source_target_pairs={{0,1},{1,0},{2,3},{3,2},{4,5},{5,4},{6,7},{7,6},{8,9},{9,8},{10,11... | collective-permute-start | bytes 6291464 | tf_op jit(solution)/shard_map/ppermute | solution.py:137
  33.8 21.4 %collective-permute-start.5 = (bf16[128,2176]{1,0:T(8,128)(2,1)S(1)}, bf16[128,2176]{1,0:T(8,128)(2,1)S(1)}, u32[]{:S(2)}, u32[]{:S(2)}) collective-permute-start(bf16[128,2176]{1,0:T(8,128)(2,1)S(1)} %collective-permute-done.3.refs_2_), channel_id=1, source_target_pairs={{0,2},{1,3},{2,0},{3,1},{4,6},{5,7},{6,4},{7,5},{8,10},{9,11},{10,... | collective-permute-start | bytes 1671176 | tf_op jit(solution)/shard_map/ppermute | solution.py:137
  34.3 20.9 %collective-permute-start.6 = (bf16[128,2176]{1,0:T(8,128)(2,1)S(1)}, bf16[128,2176]{1,0:T(8,128)(2,1)S(1)}, u32[]{:S(2)}, u32[]{:S(2)}) collective-permute-start(bf16[128,2176]{1,0:T(8,128)(2,1)S(1)} %collective-permute-done.3.refs_2_), channel_id=1, source_target_pairs={{0,4},{1,5},{2,6},{3,7},{4,8},{5,9},{6,10},{7,11},{8,12},{9,13},{1... | collective-permute-start | bytes 1671176 | tf_op jit(solution)/shard_map/ppermute | solution.py:134
  34.3 42.2 %collective-permute-start.14 = (bf16[128,2176]{1,0:T(8,128)(2,1)}, bf16[128,2176]{1,0:T(8,128)(2,1)S(1)}, u32[]{:S(2)}, u32[]{:S(2)}) collective-permute-start(bf16[128,2176]{1,0:T(8,128)(2,1)} %collective-permute-done.2.refs_3_), channel_id=1, source_target_pairs={{0,12},{1,13},{2,14},{3,15},{4,0},{5,1},{6,2},{7,3},{8,4},{9,5},{1... | collective-permute-start | bytes 1671176 | tf_op jit(solution)/shard_map/ppermute | solution.py:134
  38.2 26.7 %collective-permute-start.10 = (bf16[128,2048]{1,0:T(8,128)(2,1)}, bf16[128,2048]{1,0:T(8,128)(2,1)S(1)}, u32[]{:S(2)}, u32[]{:S(2)}) collective-permute-start(bf16[128,2048]{1,0:T(8,128)(2,1)} %collective-permute-done.1.refs_0_), channel_id=1, source_target_pairs={{0,2},{1,3},{2,0},{3,1},{4,6},{5,7},{6,4},{7,5},{8,10},{9,11},{10,... | collective-permute-start | bytes 1572872 | tf_op jit(solution)/shard_map/ppermute | solution.py:137
  40.7 34.2 %collective-permute-start.11 = (bf16[128,2048]{1,0:T(8,128)(2,1)}, bf16[128,2048]{1,0:T(8,128)(2,1)}, u32[]{:S(2)}, u32[]{:S(2)}) collective-permute-start(bf16[128,2048]{1,0:T(8,128)(2,1)} %collective-permute-done.1.refs_0_), channel_id=1, source_target_pairs={{0,4},{1,5},{2,6},{3,7},{4,8},{5,9},{6,10},{7,11},{8,12},{9,13},{1... | collective-permute-start | bytes 1572872 | tf_op jit(solution)/shard_map/ppermute | solution.py:134
  55.1 33.0 %collective-permute-start.13 = (bf16[128,2176]{1,0:T(8,128)(2,1)S(1)}, bf16[128,2176]{1,0:T(8,128)(2,1)S(1)}, u32[]{:S(2)}, u32[]{:S(2)}) collective-permute-start(bf16[128,2176]{1,0:T(8,128)(2,1)S(1)} %collective-permute-done.6.refs_2_), channel_id=1, source_target_pairs={{0,2},{1,3},{2,0},{3,1},{4,6},{5,7},{6,4},{7,5},{8,10},{9,11},{10,... | collective-permute-start | bytes 1671176 | tf_op jit(solution)/shard_map/ppermute | solution.py:137
  55.7 30.1 %collective-permute-start.9 = (bf16[128,2048]{1,0:T(8,128)(2,1)}, bf16[128,2048]{1,0:T(8,128)(2,1)S(1)}, u32[]{:S(2)}, u32[]{:S(2)}) collective-permute-start(bf16[128,2048]{1,0:T(8,128)(2,1)} %refs_0_.1), channel_id=1, source_target_pairs={{0,12},{1,13},{2,14},{3,15},{4,0},{5,1},{6,2},{7,3},{8,4},{9,5},{1... | collective-permute-start | bytes 1572872 | tf_op jit(solution)/shard_map/ppermute | solution.py:134
  74.9 13.2 %collective-permute-start.12 = (bf16[128,2048]{1,0:T(8,128)(2,1)}, bf16[128,2048]{1,0:T(8,128)(2,1)S(1)}, u32[]{:S(2)}, u32[]{:S(2)}) collective-permute-start(bf16[128,2048]{1,0:T(8,128)(2,1)} %collective-permute-done.11.refs_0_), channel_id=1, source_target_pairs={{0,2},{1,3},{2,0},{3,1},{4,6},{5,7},{6,4},{7,5},{8,10},{9,11},{10,... | collective-permute-start | bytes 1572872 | tf_op jit(solution)/shard_map/ppermute | solution.py:137
  76.4 27.2 %collective-permute-start.18 = (bf16[128,2176]{1,0:T(8,128)(2,1)}, bf16[128,2176]{1,0:T(8,128)(2,1)S(1)}, u32[]{:S(2)}, u32[]{:S(2)}) collective-permute-start(bf16[128,2176]{1,0:T(8,128)(2,1)} %gated_rows.1.refs_2_), channel_id=1, source_target_pairs={{0,12},{1,13},{2,14},{3,15},{4,0},{5,1},{6,2},{7,3},{8,4},{9,5},{1... | collective-permute-start | bytes 1671176 | tf_op jit(solution)/shard_map/ppermute | solution.py:134
  85.3 18.4 %collective-permute-start.17 = (bf16[128,2048]{1,0:T(8,128)(2,1)S(1)}, bf16[128,2048]{1,0:T(8,128)(2,1)S(1)}, u32[]{:S(2)}, u32[]{:S(2)}) collective-permute-start(bf16[128,2048]{1,0:T(8,128)(2,1)S(1)} %get-tuple-element.67), channel_id=1, source_target_pairs={{0,2},{1,3},{2,0},{3,1},{4,6},{5,7},{6,4},{7,5},{8,10},{9,11},{10,... | collective-permute-start | bytes 1572872 | tf_op jit(solution)/shard_map/ppermute | solution.py:137
  85.9 17.7 %collective-permute-start.16 = (bf16[64,2048]{1,0:T(8,128)(2,1)S(1)}, bf16[64,2048]{1,0:T(8,128)(2,1)S(1)}, u32[]{:S(2)}, u32[]{:S(2)}) collective-permute-start(bf16[64,2048]{1,0:T(8,128)(2,1)S(1)} %slice.7), channel_id=1, source_target_pairs={{0,2},{1,3},{2,0},{3,1},{4,6},{5,7},{6,4},{7,5},{8,10},{9,11},{10,... | collective-permute-start | bytes 786440 | tf_op jit(solution)/shard_map/ppermute | solution.py:137
  88.1 15.5 %collective-permute-start.15 = (bf16[64,2048]{1,0:T(8,128)(2,1)S(1)}, bf16[64,2048]{1,0:T(8,128)(2,1)S(1)}, u32[]{:S(2)}, u32[]{:S(2)}) collective-permute-start(bf16[64,2048]{1,0:T(8,128)(2,1)S(1)} %slice.6), channel_id=1, source_target_pairs={{0,12},{1,13},{2,14},{3,15},{4,0},{5,1},{6,2},{7,3},{8,4},{9,5},{1... | collective-permute-start | bytes 786440 | tf_op jit(solution)/shard_map/ppermute | solution.py:134
  103.6 12.0 %collective-permute-start.19 = (bf16[128,2048]{1,0:T(8,128)(2,1)S(1)}, bf16[128,2048]{1,0:T(8,128)(2,1)S(1)}, u32[]{:S(2)}, u32[]{:S(2)}) collective-permute-start(bf16[128,2048]{1,0:T(8,128)(2,1)S(1)} %get-tuple-element.72), channel_id=1, source_target_pairs={{0,2},{1,3},{2,0},{3,1},{4,6},{5,7},{6,4},{7,5},{8,10},{9,11},{10,... | collective-permute-start | bytes 1572872 | tf_op jit(solution)/shard_map/ppermute | solution.py:137
  105.3 20.7 %collective-permute-start.21 = (bf16[128,2048]{1,0:T(8,128)(2,1)S(1)}, bf16[128,2048]{1,0:T(8,128)(2,1)S(1)}, u32[]{:S(2)}, u32[]{:S(2)}) collective-permute-start(bf16[128,2048]{1,0:T(8,128)(2,1)S(1)} %add_convert_fusion.1), channel_id=1, source_target_pairs={{0,12},{1,13},{2,14},{3,15},{4,0},{5,1},{6,2},{7,3},{8,4},{9,5},{1... | collective-permute-start | bytes 1572872 | tf_op jit(solution)/shard_map/ppermute | solution.py:134
  115.7 14.9 %collective-permute-start.22 = (bf16[128,2048]{1,0:T(8,128)(2,1)S(1)}, bf16[128,2048]{1,0:T(8,128)(2,1)S(1)}, u32[]{:S(2)}, u32[]{:S(2)}) collective-permute-start(bf16[128,2048]{1,0:T(8,128)(2,1)S(1)} %pair_rows.8), channel_id=1, source_target_pairs={{0,2},{1,3},{2,0},{3,1},{4,6},{5,7},{6,4},{7,5},{8,10},{9,11},{10,... | collective-permute-start | bytes 1572872 | tf_op jit(solution)/shard_map/ppermute | solution.py:137
  117.3 13.3 %collective-permute-start.23 = (bf16[128,2048]{1,0:T(8,128)(2,1)S(1)}, bf16[128,2048]{1,0:T(8,128)(2,1)S(1)}, u32[]{:S(2)}, u32[]{:S(2)}) collective-permute-start(bf16[128,2048]{1,0:T(8,128)(2,1)S(1)} %add_convert_fusion.2), channel_id=1, source_target_pairs={{0,4},{1,5},{2,6},{3,7},{4,8},{5,9},{6,10},{7,11},{8,12},{9,13},{1... | collective-permute-start | bytes 1572872 | tf_op jit(solution)/shard_map/ppermute | solution.py:134
  117.3 20.6 %collective-permute-start.20 = (bf16[128,2048]{1,0:T(8,128)(2,1)S(1)}, bf16[128,2048]{1,0:T(8,128)(2,1)S(1)}, u32[]{:S(2)}, u32[]{:S(2)}) collective-permute-start(bf16[128,2048]{1,0:T(8,128)(2,1)S(1)} %copy-done.9), channel_id=1, source_target_pairs={{0,2},{1,3},{2,0},{3,1},{4,6},{5,7},{6,4},{7,5},{8,10},{9,11},{10,... | collective-permute-start | bytes 1572872 | tf_op jit(solution)/shard_map/ppermute | solution.py:137
  130.8 11.0 %collective-permute-start.24 = (bf16[128,2048]{1,0:T(8,128)(2,1)S(1)}, bf16[128,2048]{1,0:T(8,128)(2,1)S(1)}, u32[]{:S(2)}, u32[]{:S(2)}) collective-permute-start(bf16[128,2048]{1,0:T(8,128)(2,1)S(1)} %add_convert_fusion), channel_id=1, source_target_pairs={{0,4},{1,5},{2,6},{3,7},{4,8},{5,9},{6,10},{7,11},{8,12},{9,13},{1... | collective-permute-start | bytes 1572872 | tf_op jit(solution)/shard_map/ppermute | solution.py:134
  (11 other events, 142.3 us)
